TPU v7x, 128 devices: a whole 4x4x4 slice. The times are simulated.
128 devices in a mesh: row: 8 (over z, core), col: 16 (over x, y).
Axes of the slice: x: 4, y: 4, z: 4, core: 2. Of those that a mesh axis runs over, the one named last changes fastest.
Arguments:
- embed: bfloat16 [262144, 64], P(('row', 'col')), may hold values from -6 to 6
- tiles: bfloat16 [8192, 128, 128], P(('row', 'col'))
- tile_rows: int32 [8192], P(('row', 'col')), may hold values from 0 to 2047, as said below
- tile_cols: int32 [8192], P(('row', 'col')), may hold values from 0 to 2047, as said below
- chg_tiles: bfloat16 [24576, 128, 128], P(('row', 'col'))
- chg_rows: int32 [24576], P(('row', 'col')), may hold values from 0 to 2047, as said below
- chg_cols: int32 [24576], P(('row', 'col')), may hold values from 0 to 2047, as said below
Outputs:
- embedding: float32 [262144, 64], P(('row', 'col'))
Inputs may be any that keep to these rules, and one draw needn't show every extreme that they name: Tile n lies in the row group of the device that holds it: tile_rows[n] // 256 equals (n // 64) // 16. Tile n lies in the column group of the device that holds it: tile_cols[n] // 128 equals (n // 64) % 16. `chg_rows`: one device's list names each transpose owner at most 3 times; in every draw some owner is named exactly 3 times by every device's list. `chg_cols`: read with chg_rows to give the transpose owner.
All inputs are finite; a program needn't handle non-finite values.
Results may differ from a plain program's by a relative error of at most 0.025.
Values may be sent and summed in bfloat16 or wider, within the bound.
A program may use at most 192 MiB of HBM per device.

v0:
```python
import jax
import jax.numpy as jnp
from jax import lax
from jax.sharding import PartitionSpec as P

ITERS = 3
CAP = 3


def block_terms(own, own_rows, own_cols, taken, taken_rows, taken_cols, blocked, row_blocks):
    own_terms = jnp.einsum(
        "nab,nbk->nak", own, blocked[own_cols], preferred_element_type=jnp.float32
    )
    taken_terms = jnp.einsum(
        "nab,nak->nbk", taken, blocked[taken_cols], preferred_element_type=jnp.float32
    )
    return jax.ops.segment_sum(own_terms, own_rows, row_blocks) + jax.ops.segment_sum(
        taken_terms, taken_rows, row_blocks
    )


def local(embed, tiles, tile_rows, tile_cols, chg_tiles, chg_rows, chg_cols):
    rows_dev, feature_width = embed.shape
    tile_size = tiles.shape[1]
    row_count = lax.axis_size("row")
    col_count = lax.axis_size("col")
    devices = row_count * col_count
    row_blocks = rows_dev * col_count // tile_size
    col_blocks = rows_dev * row_count // tile_size
    sub_rows = rows_dev // devices
    owners = chg_cols // row_blocks * col_count + chg_rows // col_blocks
    position = jnp.arange(owners.shape[0], dtype=jnp.int32)
    earlier = position[None, :] < position[:, None]
    slot_rank = jnp.sum(jnp.logical_and(owners[:, None] == owners[None, :], earlier), axis=1)
    outgoing = (
        jnp.zeros((devices, CAP, tile_size, tile_size), jnp.bfloat16)
        .at[owners, slot_rank]
        .set(chg_tiles)
    )
    placing = jnp.stack([chg_cols % row_blocks, chg_rows % col_blocks], axis=1)
    output_slots = jnp.zeros((devices, CAP, 2), jnp.int32).at[owners, slot_rank].set(placing)
    taken, taken_places = (
        lax.all_to_all(outgoing, ("row", "col"), split_axis=0, concat_axis=0, tiled=True),
        lax.all_to_all(output_slots, ("row", "col"), split_axis=0, concat_axis=0, tiled=True),
    )
    taken = taken.reshape(devices * CAP, tile_size, tile_size)
    taken_places = taken_places.reshape(devices * CAP, 2)
    taken_rows = taken_places[:, 0]
    taken_cols = taken_places[:, 1]
    own_rows = tile_rows % row_blocks
    own_cols = tile_cols % col_blocks
    degree_terms = jax.ops.segment_sum(
        jnp.sum(jnp.abs(tiles), axis=2, dtype=jnp.float32), own_rows, row_blocks
    )
    degree_terms = degree_terms + jax.ops.segment_sum(
        jnp.sum(jnp.abs(taken), axis=1, dtype=jnp.float32), taken_rows, row_blocks
    )
    degree = 1.0 + lax.psum_scatter(
        degree_terms.astype(jnp.bfloat16), "col", scatter_dimension=0, tiled=True
    ).astype(jnp.float32).reshape(rows_dev, 1)
    nodes = rows_dev * devices
    current = embed
    final_output = embed.astype(jnp.float32)
    for iteration in range(ITERS):
        received_terms = lax.all_to_all(
            current.reshape(devices, sub_rows, feature_width),
            ("row", "col"),
            split_axis=0,
            concat_axis=0,
            tiled=True,
        )
        group = lax.all_gather(
            received_terms.reshape(rows_dev, feature_width), "row", axis=0, tiled=True
        )
        blocked = group.reshape(col_blocks, tile_size, feature_width)
        partial_value = block_terms(
            tiles, own_rows, own_cols, taken, taken_rows, taken_cols, blocked, row_blocks
        )
        summed = lax.psum_scatter(
            partial_value.reshape(row_blocks * tile_size, feature_width).astype(jnp.bfloat16),
            "col",
            scatter_dimension=0,
            tiled=True,
        ).astype(jnp.float32)
        scaled = summed / degree
        local_gram = jnp.dot(
            scaled.T, scaled, precision=lax.Precision.HIGHEST, preferred_element_type=jnp.float32
        )
        gram = lax.psum(local_gram, ("row", "col")) / nodes
        lower = jnp.linalg.cholesky(gram)
        final_output = lax.linalg.triangular_solve(
            lower, scaled, left_side=False, lower=True, transpose_a=True
        )
        current = final_output.astype(jnp.bfloat16)
    return final_output


def solution(mesh):
    placed = (
        P(("row", "col"), None),
        P(("row", "col"), None, None),
        P(("row", "col")),
        P(("row", "col")),
        P(("row", "col"), None, None),
        P(("row", "col")),
        P(("row", "col")),
    )
    return jax.shard_map(
        local, mesh=mesh, in_specs=placed, out_specs=P(("row", "col"), None), check_vma=False
    )
```

profile of v0, /device:TPU:1, one launch (start us, length us, event | category | flops | bytes accessed | tf_op | source)
XLA Modules:
  0.0 1203.7 jit_solution(14980614209809009102)
XLA Ops:
  8.4 10.1 scatter_fusion.1
  20.0 11.5 all-to-all-start.1
  33.8 7.8 all-to-all-done.1
  41.6 4.1 all-to-all-start
  45.7 7.7 broadcast_in_dim.14
  53.4 30.9 %scatter_fusion.2 = bf16[128,3,128,128]{3,2,1,0:T(8,128)(2,1)} fusion(bf16[128,3,128,128]{3,2,1,0:T(8,128)(2,1)} %broadcast_in_dim.14, s32[192]{0:T(256)S(1)} %bitcast.91, bf16[192,128,128]{2,1,0:T(8,128)(2,1)} %param.14), kind=kCustom, calls=%fused_computation.8 | custom fusion | bytes 18875904 | tf_op jit(solution)/shard_map/scatter | solution.py:38
  84.3 10.1 all-to-all-start.2
  97.5 142.3 %all-gather.4.cloned.1.call-done = bf16[16384,64]{1,0:T(8,128)(2,1)} async-done(((bf16[2048,64]{1,0:T(8,128)(2,1)}), bf16[16384,64]{1,0:T(8,128)(2,1)}) %all-gather.4.cloned.1.call-update) | async-done | bytes 2097168 | tf_op jit(solution)/shard_map/all_gather | solution.py:72
  239.8 3.9 copy.77
  243.7 13.2 %gather_fusion.1 = bf16[384,128,64]{1,2,0:T(8,128)(2,1)} fusion(bf16[128,128,64]{1,2,0:T(8,128)(2,1)S(1)} %copy.77, s32[1024]{0:T(1024)S(1)} %pad_clamp_fusion), kind=kCustom, calls=%fused_computation.1 | custom fusion | bytes 12584448 | tf_op jit(solution)/shard_map/gather | solution.py:15
  260.9 4.3 broadcast.110.clone.2
  265.1 9.0 scatter_fusion
  274.1 9.2 convert_reduce_fusion
  286.9 14.3 %fusion.38 = f32[384,128,64]{1,2,0:T(8,128)} fusion(bf16[384,128,64]{1,2,0:T(8,128)(2,1)} %gather_fusion.1, bf16[384,128,128]{2,1,0:T(8,128)(2,1)} %bitcast.9), kind=kOutput, calls=%fused_computation.120 | convolution fusion | flops 805306368 | bytes 31457280 | tf_op jit(solution)/shard_map/nab,nak->nbk/dot_general | solution.py:14
  301.2 4.3 broadcast.110.clone.3
  305.5 61.3 %scatter_fusion.3 = f32[256,128,64]{1,2,0:T(8,128)} fusion(f32[256,128,64]{1,2,0:T(8,128)} %broadcast.110.clone.3, s32[384]{0:T(512)S(1)} %get-tuple-element.8, f32[384,128,64]{1,2,0:T(8,128)} %fusion.38), kind=kCustom, calls=%fused_computation.9 | custom fusion | flops 3145728 | bytes 37750272 | tf_op jit(solution)/shard_map/scatter-add | solution.py:17
  366.8 8.6 copy_bitcast_fusion.2
  376.8 6.4 all-reduce.3.cloned.1.call-done
  383.9 83.6 %reduce-scatter.4.cloned.1.call-done = bf16[2048,64]{0,1:T(8,128)(2,1)} async-done(((bf16[32768,64]{0,1:T(8,128)(2,1)}), bf16[2048,64]{0,1:T(8,128)(2,1)}) %reduce-scatter.4.cloned.1.call-update) | async-done | bytes 262160 | tf_op jit(solution)/shard_map/reduce_scatter | solution.py:79
  469.1 66.1 %psum.21 = f32[64,64]{0,1:T(8,128)S(1)} all-reduce(f32[64,64]{0,1:T(8,128)S(1)} %fusion.5), channel_id=1, replica_groups=mesh['row'=8,'col'=16] {'row','col'}, use_global_device_ids=true, to_apply=%region_11.12 | all-reduce | flops 4096 | bytes 32768 | tf_op jit(solution)/shard_map/psum | solution.py:89
  535.4 5.8 cholesky.59
  542.6 4.9 custom-call.11
  549.6 15.7 %all_to_all.25 = bf16[128,2,512]{2,1,0:T(2,128)(2,1)S(1)} all-to-all(bf16[128,2,512]{2,1,0:T(2,128)(2,1)S(1)} %reshape.237), channel_id=1, replica_groups=mesh['row'=8,'col'=16] {'row','col'}, dimensions={0} | all-to-all | bytes 524288 | tf_op jit(solution)/shard_map/all_to_all | solution.py:65
  566.7 28.7 %all-gather.6.cloned.1.call-done = bf16[16384,64]{1,0:T(8,128)(2,1)} async-done(((bf16[2048,64]{1,0:T(8,128)(2,1)}), bf16[16384,64]{1,0:T(8,128)(2,1)}) %all-gather.6.cloned.1.call-update) | async-done | bytes 2097168 | tf_op jit(solution)/shard_map/all_gather | solution.py:72
  599.1 13.2 %gather_fusion.3 = bf16[384,128,64]{1,2,0:T(8,128)(2,1)} fusion(bf16[128,128,64]{1,2,0:T(8,128)(2,1)S(1)} %copy.87, s32[1024]{0:T(1024)S(1)} %pad_clamp_fusion), kind=kCustom, calls=%fused_computation.3 | custom fusion | bytes 12584448 | tf_op jit(solution)/shard_map/gather | solution.py:15
  613.1 14.4 %fusion.39 = f32[384,128,64]{1,2,0:T(8,128)} fusion(bf16[384,128,64]{1,2,0:T(8,128)(2,1)} %gather_fusion.3, bf16[384,128,128]{2,1,0:T(8,128)(2,1)} %bitcast.9), kind=kOutput, calls=%fused_computation.121 | convolution fusion | flops 805306368 | bytes 31457280 | tf_op jit(solution)/shard_map/nab,nak->nbk/dot_general | solution.py:14
  629.1 4.3 broadcast.110.clone.4
  633.3 61.3 %scatter_fusion.5 = f32[256,128,64]{1,2,0:T(8,128)} fusion(f32[256,128,64]{1,2,0:T(8,128)} %broadcast.110.clone.4, s32[384]{0:T(512)S(1)} %get-tuple-element.8, f32[384,128,64]{1,2,0:T(8,128)} %fusion.39), kind=kCustom, calls=%fused_computation.13 | custom fusion | flops 3145728 | bytes 37750272 | tf_op jit(solution)/shard_map/scatter-add | solution.py:17
  694.6 4.3 broadcast.110.clone.1
  698.9 9.2 scatter_fusion.4
  708.1 8.6 copy_bitcast_fusion.1
  716.7 74.2 %reduce-scatter.6.cloned.1.call-done = bf16[2048,64]{0,1:T(8,128)(2,1)} async-done(((bf16[32768,64]{0,1:T(8,128)(2,1)}), bf16[2048,64]{0,1:T(8,128)(2,1)}) %reduce-scatter.6.cloned.1.call-update) | async-done | bytes 262160 | tf_op jit(solution)/shard_map/reduce_scatter | solution.py:79
  792.6 66.2 %psum.22 = f32[64,64]{0,1:T(8,128)S(1)} all-reduce(f32[64,64]{0,1:T(8,128)S(1)} %fusion.6), channel_id=1, replica_groups=mesh['row'=8,'col'=16] {'row','col'}, use_global_device_ids=true, to_apply=%region_17.20 | all-reduce | flops 4096 | bytes 32768 | tf_op jit(solution)/shard_map/psum | solution.py:89
  858.9 5.8 cholesky.70
  866.1 4.9 custom-call.12
  873.2 15.7 %all_to_all.26 = bf16[128,2,512]{2,1,0:T(2,128)(2,1)S(1)} all-to-all(bf16[128,2,512]{2,1,0:T(2,128)(2,1)S(1)} %reshape.239), channel_id=1, replica_groups=mesh['row'=8,'col'=16] {'row','col'}, dimensions={0} | all-to-all | bytes 524288 | tf_op jit(solution)/shard_map/all_to_all | solution.py:65
  890.1 28.8 %all-gather.8.cloned.1.call-done = bf16[16384,64]{1,0:T(8,128)(2,1)} async-done(((bf16[2048,64]{1,0:T(8,128)(2,1)}), bf16[16384,64]{1,0:T(8,128)(2,1)}) %all-gather.8.cloned.1.call-update) | async-done | bytes 2097168 | tf_op jit(solution)/shard_map/all_gather | solution.py:72
  922.6 13.2 %gather_fusion.5 = bf16[384,128,64]{1,2,0:T(8,128)(2,1)} fusion(bf16[128,128,64]{1,2,0:T(8,128)(2,1)S(1)} %copy.94, s32[1024]{0:T(1024)S(1)} %pad_clamp_fusion), kind=kCustom, calls=%fused_computation.5 | custom fusion | bytes 12584448 | tf_op jit(solution)/shard_map/gather | solution.py:15
  936.6 14.4 %fusion.40 = f32[384,128,64]{1,2,0:T(8,128)} fusion(bf16[384,128,64]{1,2,0:T(8,128)(2,1)} %gather_fusion.5, bf16[384,128,128]{2,1,0:T(8,128)(2,1)} %bitcast.9), kind=kOutput, calls=%fused_computation.122 | convolution fusion | flops 805306368 | bytes 31457280 | tf_op jit(solution)/shard_map/nab,nak->nbk/dot_general | solution.py:14
  952.6 4.3 broadcast.110.clone.5
  956.9 59.0 %scatter_fusion.7 = f32[256,128,64]{1,2,0:T(8,128)} fusion(f32[256,128,64]{1,2,0:T(8,128)} %broadcast.110.clone.5, s32[384]{0:T(512)S(1)} %get-tuple-element.8, f32[384,128,64]{1,2,0:T(8,128)} %fusion.40), kind=kCustom, calls=%fused_computation.15 | custom fusion | flops 3145728 | bytes 37750272 | tf_op jit(solution)/shard_map/scatter-add | solution.py:17
  1015.9 4.3 broadcast.110.clone
  1020.2 9.3 scatter_fusion.6
  1029.4 8.5 copy_bitcast_fusion
  1038.0 75.4 %reduce-scatter.8.cloned.1.call-done = bf16[2048,64]{0,1:T(8,128)(2,1)} async-done(((bf16[32768,64]{0,1:T(8,128)(2,1)}), bf16[2048,64]{0,1:T(8,128)(2,1)}) %reduce-scatter.8.cloned.1.call-update) | async-done | bytes 262160 | tf_op jit(solution)/shard_map/reduce_scatter | solution.py:79
  1115.1 66.2 %psum.23 = f32[64,64]{0,1:T(8,128)S(1)} all-reduce(f32[64,64]{0,1:T(8,128)S(1)} %fusion.7), channel_id=1, replica_groups=mesh['row'=8,'col'=16] {'row','col'}, use_global_device_ids=true, to_apply=%region_21.24 | all-reduce | flops 4096 | bytes 32768 | tf_op jit(solution)/shard_map/psum | solution.py:89
  1181.4 5.8 cholesky.81
  1188.6 4.9 custom-call.13
  (90 shorter events, 47.1 us)
Async XLA Ops:
  20.0 21.5 %all-to-all-start.1 = ((s32[128,3,2]{1,2,0:T(2,128)}), s32[128,3,2]{1,2,0:T(2,128)S(1)}, u32[]{:S(2)}, u32[]{:S(2)}) async-start(s32[128,3,2]{1,2,0:T(2,128)} %copy.79), calls=%async_computation.1 | async-start | bytes 262144 | tf_op jit(solution)/shard_map/all_to_all | solution.py:44
  41.6 42.7 %all-to-all-start = ((bf16[128,2,512]{2,1,0:T(2,128)(2,1)}), bf16[128,2,512]{2,1,0:T(2,128)(2,1)S(1)}, u32[]{:S(2)}, u32[]{:S(2)}) async-start(bf16[128,2,512]{2,1,0:T(2,128)(2,1)} %reshape.235), calls=%async_computation | async-start | bytes 524288 | tf_op jit(solution)/shard_map/all_to_all | solution.py:65
  84.3 11.4 copy-start.3
  84.3 11.5 copy-start
  84.3 12.9 %copy-start.4 = (s32[64]{0:T(128)S(1)}, s32[64]{0:T(128)}, u32[]{:S(2)}) copy-start(s32[64]{0:T(128)} %param.13) | copy-start | bytes 772
  84.3 189.8 %all-to-all-start.2 = ((bf16[128,3,128,128]{3,2,1,0:T(8,128)(2,1)}), bf16[128,3,128,128]{3,2,1,0:T(8,128)(2,1)}, u32[]{:S(2)}, u32[]{:S(2)}) async-start(bf16[128,3,128,128]{3,2,1,0:T(8,128)(2,1)} %scatter_fusion.2), calls=%async_computation.2 | async-start | bytes 25165824 | tf_op jit(solution)/shard_map/all_to_all | solution.py:43
  94.4 145.4 %all-gather.4.cloned.1.call-start = ((), (), s32[]{:S(2)}) async-start(), calls=%async_computation.8 | async-start | bytes 4718592 | tf_op jit(solution)/shard_map/all_gather | solution.py:72
  95.7 287.5 %all-reduce.3.cloned.1.call-start = ((), (), s32[]{:S(2)}) async-start(), calls=%async_computation.14 | async-start | bytes 131072
  286.9 180.6 %reduce-scatter.4.cloned.1.call-start = ((), (), s32[]{:S(2)}) async-start(), calls=%async_computation.9 | async-start | bytes 4456448 | tf_op jit(solution)/shard_map/reduce_scatter | solution.py:79
  366.8 8.7 copy-start.5
  375.4 219.9 %all-gather.6.cloned.1.call-start = ((), (), s32[]{:S(2)}) async-start(), calls=%async_computation.10 | async-start | bytes 4718592 | tf_op jit(solution)/shard_map/all_gather | solution.py:72
  566.5 224.5 %reduce-scatter.6.cloned.1.call-start = ((), (), s32[]{:S(2)}) async-start(), calls=%async_computation.11 | async-start | bytes 4456448 | tf_op jit(solution)/shard_map/reduce_scatter | solution.py:79
  613.1 14.4 %copy-start.1 = (bf16[64,128,128]{2,1,0:T(8,128)(2,1)S(1)}, bf16[64,128,128]{2,1,0:T(8,128)(2,1)}, u32[]{:S(2)}) copy-start(bf16[64,128,128]{2,1,0:T(8,128)(2,1)} %param.11) | copy-start | bytes 6291460
  716.7 202.2 %all-gather.8.cloned.1.call-start = ((), (), s32[]{:S(2)}) async-start(), calls=%async_computation.12 | async-start | bytes 4718592 | tf_op jit(solution)/shard_map/all_gather | solution.py:72
  890.1 223.4 %reduce-scatter.8.cloned.1.call-start = ((), (), s32[]{:S(2)}) async-start(), calls=%async_computation.13 | async-start | bytes 4456448 | tf_op jit(solution)/shard_map/reduce_scatter | solution.py:79
  936.6 14.4 %copy-start.2 = (bf16[64,128,128]{2,1,0:T(8,128)(2,1)S(1)}, bf16[64,128,128]{2,1,0:T(8,128)(2,1)}, u32[]{:S(2)}) copy-start(bf16[64,128,128]{2,1,0:T(8,128)(2,1)} %param.11) | copy-start | bytes 6291460
Sparse Core Ops, SparseCore 0:
  97.1 142.6 all-gather.3
  566.6 28.7 all-gather.5
  890.2 28.7 all-gather.7
Sparse Core Ops, SparseCore 1:
  287.0 96.1 all-reduce.2
  386.7 80.7 reduce-scatter.3
  716.8 74.1 reduce-scatter.5
  1038.1 75.3 reduce-scatter.7
where the time goes:
time: 1210 us; the launch traced here: 1200 us
  waiting for transfers between devices  447 us (37%)
  other arithmetic  287 us (24%)
  blocking collectives  230 us (19%)
  local copies, waits for them, and re-layouts  137 us (11%)
  matrix products  59.9 us (5%)
  starting transfers between devices  26.2 us (2%)
  between operations  16.4 us (1%)
    reduce_scatter x3, waiting for transfers between devices, local(): lax.psum_scatter(partial_value.reshape(row_blocks * tile_size, feature_wi...  233 us
    all_gather x3, waiting for transfers between devices, local(): lax.all_gather(received_terms.reshape(rows_dev, feature_width), 'row', ax...  200 us
    psum x3, blocking collectives, local(): gram = lax.psum(local_gram, ('row', 'col')) / nodes  199 us
    scatter-add x3, other arithmetic, block_terms(): jax.ops.segment_sum(taken_terms, taken_rows, row_blocks)  182 us
    dot_general x3, matrix products, block_terms(): jnp.einsum('nab,nak->nbk', taken, blocked[taken_cols], preferred_element_...  43.1 us
    gather x3, local copies, waits for them, and re-layouts, block_terms(): blocked[taken_cols]  39.7 us
    all_to_all x2, blocking collectives, local(): lax.all_to_all(current.reshape(devices, sub_rows, feature_width), ('row',...  31.4 us
    scatter x1, local copies, waits for them, and re-layouts, local(): outgoing = jnp.zeros((devices, CAP, tile_size, tile_size), jnp.bfloat16)....  30.9 us
  transfers between devices with their start and end apart: 10, of which 8 were waited for; matrix products, arithmetic and copies ran while one was open for 14% of the time, Pallas kernels for 0%

commit v1 on v0

v1 whole, which is shorter than its diff:
```python
import functools

import jax
import jax.numpy as jnp
from jax import lax
from jax.experimental import pallas as pl
from jax.experimental.pallas import tpu as pltpu
from jax.sharding import PartitionSpec as P

ITERS = 3
CAP = 3
K = 64
TILE = 128
NR = 8
NC = 16
DEV = NR * NC
ROWS_BLK = 256
SLOT_ROWS = CAP * TILE + 16
OWN = 64
NODES = 262144
BF = jnp.bfloat16
F32 = jnp.float32
ANY = pl.BlockSpec(memory_space=pl.ANY)
VMEM = pl.BlockSpec(memory_space=pltpu.VMEM)
SMEM = pl.BlockSpec(memory_space=pltpu.SMEM)
MIB = 1024 * 1024
ROW_ORDER = ((1, 0), (3, 1), (2, 0), (1, 1), (3, 0), (2, 1), (0, 1))


def dot(a, b, dims, precision=None):
    return lax.dot_general(a, b, (dims, ((), ())), precision=precision, preferred_element_type=F32)


def pack_kernel(pick_ref, tiles_ref, meta_ref, out_ref, tile_sem, meta_sem):
    meta_copy = pltpu.make_async_copy(meta_ref, out_ref.at[:, pl.ds(CAP * TILE, 16)], meta_sem)
    meta_copy.start()

    def body(owner, carry):
        for slot in range(CAP):
            pltpu.make_async_copy(
                tiles_ref.at[pick_ref[owner * CAP + slot]],
                out_ref.at[owner, pl.ds(slot * TILE, TILE)],
                tile_sem,
            ).start()
        return carry

    lax.fori_loop(0, DEV, body, 0)
    filled = out_ref.at[:, pl.ds(0, CAP * TILE)]
    pltpu.make_async_copy(filled, filled, tile_sem).wait()
    meta_copy.wait()


def pack(pick, chg_tiles, meta):
    return pl.pallas_call(
        pack_kernel,
        out_shape=jax.ShapeDtypeStruct((DEV, SLOT_ROWS, TILE), BF),
        in_specs=[SMEM, ANY, ANY],
        out_specs=ANY,
        scratch_shapes=[pltpu.SemaphoreType.DMA, pltpu.SemaphoreType.DMA],
        name="pack",
    )(pick, chg_tiles, meta)


def greet(row, col):
    barrier = pltpu.get_barrier_semaphore()

    def cols(k, carry):
        pl.semaphore_signal(barrier, inc=1, device_id={"col": lax.rem(col + k, NC)}, device_id_type=pl.DeviceIdType.MESH)
        return carry

    def rows(k, carry):
        pl.semaphore_signal(barrier, inc=1, device_id={"row": lax.rem(row + k, NR)}, device_id_type=pl.DeviceIdType.MESH)
        return carry

    lax.fori_loop(1, NC, cols, 0)
    lax.fori_loop(1, NR, rows, 0)
    pl.semaphore_wait(barrier, NC + NR - 2)


def remote(src, dst, send_sem, recv_sem, **peer):
    return pltpu.make_async_remote_copy(
        src_ref=src, dst_ref=dst, send_sem=send_sem, recv_sem=recv_sem,
        device_id=peer, device_id_type=pl.DeviceIdType.MESH,
    )


def wait_bytes(ref, sem):
    pltpu.make_async_copy(ref, ref, sem).wait()


def x_first(row, col, xs, xc, sems):
    own = pltpu.make_async_copy(xs.at[col], xc.at[row, col], sems["x_own"])
    own.start()

    def send(k, carry):
        peer = lax.rem(col + k, NC)
        remote(xs.at[peer], xc.at[row, col], sems["xa_send"], sems["xa_recv"], col=peer).start()
        return carry

    lax.fori_loop(1, NC, send, 0)


def x_second(row, col, xs, xc, sems):
    pltpu.make_async_copy(xs.at[col], xc.at[row, col], sems["x_own"]).wait()
    wait_bytes(xc.at[row, pl.ds(0, NC - 1)], sems["xa_recv"])

    def send(k, carry):
        peer = lax.rem(row + k, NR)
        remote(xc.at[row], xc.at[row], sems["xb_send"], sems["xb_recv"], row=peer).start()
        return carry

    lax.fori_loop(1, NR, send, 0)


def x_finish(row, col, xs, xc, sems):
    wait_bytes(xs.at[pl.ds(0, NC - 1)], sems["xa_send"])
    wait_bytes(xc.at[pl.ds(0, NR - 1)], sems["xb_recv"])
    wait_bytes(xc.at[pl.ds(0, NR - 1)], sems["xb_send"])


def exchange_kernel(send_ref, xs_ref, recv_ref, mid_ref, xc_ref,
                    x_own, xa_send, xa_recv, xb_send, xb_recv,
                    a_own, a_send, a_recv, b_send, b_recv):
    row = lax.axis_index("row")
    col = lax.axis_index("col")
    sems = dict(x_own=x_own, xa_send=xa_send, xa_recv=xa_recv, xb_send=xb_send, xb_recv=xb_recv)
    greet(row, col)
    x_first(row, col, xs_ref, xc_ref, sems)
    plane, core = row // 2, lax.rem(row, 2)
    targets = [
        lax.rem(plane + dz, 4) * 2 + (lax.rem(core + flip, 2)) for dz, flip in ROW_ORDER
    ]

    def first(step, target, dst_ref):
        pltpu.make_async_copy(send_ref.at[target, col], dst_ref.at[target, col], a_own.at[step]).start()

        def send(k, carry):
            peer = lax.rem(col + k, NC)
            remote(send_ref.at[target, peer], dst_ref.at[target, col], a_send.at[step], a_recv.at[step], col=peer).start()
            return carry

        lax.fori_loop(1, NC, send, 0)

    first(0, targets[0], mid_ref)
    x_second(row, col, xs_ref, xc_ref, sems)
    for step in range(1, NR - 1):
        first(step, targets[step], mid_ref)
    first(NR - 1, row, recv_ref)
    for step in range(NR - 1):
        target = targets[step]
        wait_bytes(mid_ref.at[target, pl.ds(0, NC - 1)], a_recv.at[step])
        pltpu.make_async_copy(send_ref.at[target, col], mid_ref.at[target, col], a_own.at[step]).wait()
        remote(mid_ref.at[target], recv_ref.at[row], b_send.at[step], b_recv.at[row], row=target).start()
    wait_bytes(recv_ref.at[row, pl.ds(0, NC - 1)], a_recv.at[NR - 1])
    pltpu.make_async_copy(send_ref.at[row, col], recv_ref.at[row, col], a_own.at[NR - 1]).wait()
    x_finish(row, col, xs_ref, xc_ref, sems)
    for step in range(NR):
        wait_bytes(send_ref.at[0, pl.ds(0, NC - 1)], a_send.at[step])
    for step in range(NR - 1):
        source = targets[step]
        wait_bytes(mid_ref.at[source], b_send.at[step])
        wait_bytes(recv_ref.at[source], b_recv.at[source])


def exchange(send, xs):
    dma = pltpu.SemaphoreType.DMA
    slots = jax.ShapeDtypeStruct((NR, NC, SLOT_ROWS, TILE), BF)
    recv, _, xc = pl.pallas_call(
        exchange_kernel,
        out_shape=(slots, slots, jax.ShapeDtypeStruct((NR, NC, 4, 16, TILE), BF)),
        in_specs=[ANY, ANY],
        out_specs=(ANY, ANY, ANY),
        scratch_shapes=[dma, dma, dma, dma, dma, dma((NR,)), dma((NR,)), dma((NR,)), dma((NR,)), dma((NR,))],
        compiler_params=pltpu.CompilerParams(collective_id=0, has_side_effects=True),
        name="exchange",
    )(send.reshape(NR, NC, SLOT_ROWS, TILE), xs)
    return recv, xc


def product_kernel(with_degree, rows_ref, cols_ref, own_rows_ref, own_cols_ref, x_ref, own_ref, slots_ref, *rest):
    if with_degree:
        part_ref, degree_ref, xt_ref, acc_ref = rest
    else:
        part_ref, xt_ref, acc_ref = rest
        degree_ref = None
    step = pl.program_id(0)
    ones = jnp.ones((8, TILE), BF)

    def run(terms):
        products = []
        for load, _, x_index, dims, valid in terms:
            tile = load()
            value = dot(xt_ref[x_index], tile, dims)
            sums = None
            if with_degree:
                scale = ones if valid is None else jnp.where(valid, ones, jnp.zeros_like(ones))
                sums = dot(scale, jnp.abs(tile), dims)[0:1]
            products.append((value, sums))
        for (_, target, _, _, _), (value, sums) in zip(terms, products):
            acc_ref[target] += value
            if with_degree:
                degree_ref[target] += sums

    @pl.when(step == 0)
    def _():
        acc_ref[...] = jnp.zeros_like(acc_ref)
        if with_degree:
            degree_ref[...] = jnp.zeros_like(degree_ref)

        def turn(q, carry):
            pair, j = q // 16, lax.rem(q, 16)
            block = x_ref[pl.ds(j * 8, 8), pair].reshape(TILE, TILE)
            xt_ref[pl.ds(q * 2, 2)] = block.T.reshape(2, K, TILE)
            return carry

        lax.fori_loop(0, 64, turn, 0)
        xt_ref[pl.ds(128, 2)] = jnp.zeros((2, K, TILE), BF)

        def own(i, carry):
            run([
                (functools.partial(lambda n: own_ref[n], i * 4 + u), own_rows_ref[i * 4 + u],
                 own_cols_ref[i * 4 + u], ((1,), (1,)), None)
                for u in range(4)
            ])
            return carry

        lax.fori_loop(0, OWN // 4, own, 0)

    def taken(i, carry):
        terms = []
        for u in range(2):
            for slot in range(CAP):
                source = i * 2 + u
                n = (step * 8 + source) * CAP + slot
                x_index = cols_ref[n]
                terms.append((
                    functools.partial(lambda s, k: slots_ref[s, pl.ds(k * TILE, TILE)], source, slot),
                    rows_ref[n], x_index, ((1,), (0,)), x_index < 128,
                ))
        run(terms)
        return carry

    lax.fori_loop(0, 4, taken, 0)

    @pl.when(step == pl.num_programs(0) - 1)
    def _():
        def flush(i, carry):
            part_ref[pl.ds(i * 8, 8)] = acc_ref[pl.ds(i * 8, 8)].astype(BF)
            return carry

        lax.fori_loop(0, ROWS_BLK // 8, flush, 0)


def product(with_degree, rows, cols, own_rows, own_cols, xc, own, slots):
    whole = lambda shape: pl.BlockSpec(shape, lambda i: (0,) * len(shape))
    out_shape = [jax.ShapeDtypeStruct((ROWS_BLK, K, TILE), BF)]
    out_specs = [whole((ROWS_BLK, K, TILE))]
    if with_degree:
        out_shape.append(jax.ShapeDtypeStruct((ROWS_BLK, 1, TILE), F32))
        out_specs.append(whole((ROWS_BLK, 1, TILE)))
    terms = DEV * CAP + OWN
    return pl.pallas_call(
        functools.partial(product_kernel, with_degree),
        grid=(DEV // 8,),
        out_shape=out_shape,
        in_specs=[SMEM, SMEM, SMEM, SMEM, whole((DEV, 4, 16, TILE)), whole((OWN, TILE, TILE)),
                  pl.BlockSpec((8, SLOT_ROWS, TILE), lambda i: (i, 0, 0))],
        out_specs=out_specs,
        scratch_shapes=[pltpu.VMEM((130, K, TILE), BF), pltpu.VMEM((ROWS_BLK, K, TILE), F32)],
        compiler_params=pltpu.CompilerParams(vmem_limit_bytes=48 * MIB),
        cost_estimate=pl.CostEstimate(flops=terms * 2 * K * TILE * TILE, bytes_accessed=terms * TILE * TILE * 2, transcendentals=0),
        name="product",
    )(rows, cols, own_rows, own_cols, xc.reshape(DEV, 4, 16, TILE), own, slots.reshape(DEV, SLOT_ROWS, TILE))


def inverse_factor(gram):
    eye = (lax.broadcasted_iota(jnp.int32, (K, K), 0) == lax.broadcasted_iota(jnp.int32, (K, K), 1)).astype(F32)
    work = jnp.concatenate([gram, eye], axis=1)
    index = lax.broadcasted_iota(jnp.int32, (K, 1), 0)
    pivots = jnp.ones((K, 1), F32)
    for j in range(K):
        pivot = work[j:j + 1, j:j + 1]
        pivots = jnp.where(index == j, pivot, pivots)
        factor = jnp.where(index > j, work[:, j:j + 1] * (1.0 / pivot), 0.0)
        work = work - factor * work[j:j + 1, :]
    return lax.rsqrt(pivots) * work[:, K:]


def normalize_kernel(first, last, part_ref, degree_in_ref, *rest):
    rest = list(rest)
    if last:
        z_ref = rest.pop(0)
        xc_ref = None
    else:
        xc_ref = rest.pop(0)
    degree_ref = rest.pop(0) if first else degree_in_ref
    y_ref, rs_ref, g1_ref, g2_ref = [rest.pop(0) for _ in range(4)]
    rs_own, rs_send, rs_recv, g1_send, g1_recv, g2_send, g2_recv = [rest.pop(0) for _ in range(7)]
    if first:
        dg_ref, dg_own, dg_send, dg_recv = [rest.pop(0) for _ in range(4)]
    if not last:
        xs_ref = rest.pop(0)
        sems = dict(zip(("x_own", "xa_send", "xa_recv", "xb_send", "xb_recv"), rest))
    row = lax.axis_index("row")
    col = lax.axis_index("col")
    greet(row, col)

    if first:
        pltpu.make_async_copy(degree_in_ref.at[pl.ds(col * 16, 16)], dg_ref.at[col], dg_own).start()
    pltpu.make_async_copy(part_ref.at[pl.ds(col * 16, 16)], rs_ref.at[col], rs_own).start()

    def send(k, carry):
        peer = lax.rem(col + k, NC)
        if first:
            remote(degree_in_ref.at[pl.ds(peer * 16, 16)], dg_ref.at[col], dg_send, dg_recv, col=peer).start()
        remote(part_ref.at[pl.ds(peer * 16, 16)], rs_ref.at[col], rs_send, rs_recv.at[col], col=peer).start()
        return carry

    lax.fori_loop(1, NC, send, 0)
    if first:
        pltpu.make_async_copy(degree_in_ref.at[pl.ds(col * 16, 16)], dg_ref.at[col], dg_own).wait()
        wait_bytes(dg_ref.at[pl.ds(0, NC - 1)], dg_recv)
        degree = dg_ref[0]
        for k in range(1, NC):
            degree = degree + dg_ref[k]
        degree_ref[...] = 1.0 + degree
    pltpu.make_async_copy(part_ref.at[pl.ds(col * 16, 16)], rs_ref.at[col], rs_own).wait()
    y_ref[...] = rs_ref[col].astype(F32)

    def gather(k, carry):
        peer = lax.rem(col + NC - k, NC)
        wait_bytes(rs_ref.at[peer], rs_recv.at[peer])
        y_ref[...] += rs_ref[peer].astype(F32)
        return carry

    lax.fori_loop(1, NC, gather, 0)

    gram = jnp.zeros((K, K), F32)
    for b in range(16):
        block = y_ref[b] * (1.0 / degree_ref[b])
        y_ref[b] = block
        gram = gram + dot(block, block, ((1,), (1,)), lax.Precision.HIGHEST)
    half = K // 2
    g1_ref[col] = jnp.concatenate([gram[:half], gram[half:]], axis=1)

    def send_g1(k, carry):
        peer = lax.rem(col + k, NC)
        remote(g1_ref.at[col], g1_ref.at[col], g1_send, g1_recv, col=peer).start()
        return carry

    lax.fori_loop(1, NC, send_g1, 0)
    wait_bytes(g1_ref.at[pl.ds(0, NC - 1)], g1_recv)
    total = g1_ref[0]
    for k in range(1, NC):
        total = total + g1_ref[k]
    g2_ref[row] = total

    def send_g2(k, carry):
        peer = lax.rem(row + k, NR)
        remote(g2_ref.at[row], g2_ref.at[row], g2_send, g2_recv, row=peer).start()
        return carry

    lax.fori_loop(1, NR, send_g2, 0)
    wait_bytes(g2_ref.at[pl.ds(0, NR - 1)], g2_recv)
    total = g2_ref[0]
    for k in range(1, NR):
        total = total + g2_ref[k]
    total = total * (1.0 / NODES)
    inverse = inverse_factor(jnp.concatenate([total[:, :K], total[:, K:]], axis=0))

    def solve(b):
        return dot(inverse, y_ref[b], ((1,), (0,)), lax.Precision.HIGHEST)

    if last:
        for b in range(0, 16, 2):
            both = jnp.concatenate([solve(b), solve(b + 1)], axis=0).T
            z_ref[b * TILE:(b + 1) * TILE] = both[:, :K]
            z_ref[(b + 1) * TILE:(b + 2) * TILE] = both[:, K:]
    else:
        for pair in range(4):
            for part in range(2):
                both = jnp.concatenate([solve(pair * 4 + part), solve(pair * 4 + 2 + part)], axis=0).T
                xs_ref[part * 8:(part + 1) * 8, pair] = both.astype(BF).reshape(8, 16, TILE)
        x_first(row, col, xs_ref, xc_ref, sems)
        x_second(row, col, xs_ref, xc_ref, sems)
        x_finish(row, col, xs_ref, xc_ref, sems)
    if first:
        wait_bytes(dg_ref.at[pl.ds(0, NC - 1)], dg_send)
    wait_bytes(rs_ref.at[pl.ds(0, NC - 1)], rs_send)
    wait_bytes(g1_ref.at[pl.ds(0, NC - 1)], g1_send)
    wait_bytes(g2_ref.at[pl.ds(0, NR - 1)], g2_send)


def normalize(first, last, part, degree):
    dma = pltpu.SemaphoreType.DMA
    out_shape, out_specs = [], []
    if last:
        out_shape.append(jax.ShapeDtypeStruct((16 * TILE, K), F32))
        out_specs.append(VMEM)
    else:
        out_shape.append(jax.ShapeDtypeStruct((NR, NC, 4, 16, TILE), BF))
        out_specs.append(ANY)
    if first:
        out_shape.append(jax.ShapeDtypeStruct((16, 1, TILE), F32))
        out_specs.append(VMEM)
    scratch = [
        pltpu.VMEM((16, K, TILE), F32), pltpu.VMEM((NC, 16, K, TILE), BF),
        pltpu.VMEM((NC, K // 2, TILE), F32), pltpu.VMEM((NR, K // 2, TILE), F32),
        dma, dma, dma((NC,)), dma, dma, dma, dma,
    ]
    if first:
        scratch += [pltpu.VMEM((NC, 16, 1, TILE), F32), dma, dma, dma]
    if not last:
        scratch += [pltpu.VMEM((NC, 4, 16, TILE), BF), dma, dma, dma, dma, dma]
    return pl.pallas_call(
        functools.partial(normalize_kernel, first, last),
        out_shape=out_shape,
        in_specs=[ANY, ANY if first else VMEM],
        out_specs=out_specs,
        scratch_shapes=scratch,
        compiler_params=pltpu.CompilerParams(
            collective_id=1 if first else (3 if last else 2), has_side_effects=True, vmem_limit_bytes=40 * MIB
        ),
        name="normalize",
    )(part, degree)


def block_index(block):
    return block // 32 * 32 + block % 16 * 2 + block // 16 % 2


def local(embed, tiles, tile_rows, tile_cols, chg_tiles, chg_rows, chg_cols):
    owners = chg_cols // 256 * NC + chg_rows // 128
    count = owners.shape[0]
    position = jnp.arange(count, dtype=jnp.int32)
    earlier = position[None, :] < position[:, None]
    rank = jnp.sum(jnp.logical_and(owners[:, None] == owners[None, :], earlier).astype(jnp.int32), axis=1)
    key = owners * CAP + rank
    hit = jnp.arange(DEV * CAP, dtype=jnp.int32)[:, None] == key[None, :]
    pick = jnp.sum(jnp.where(hit, position[None, :], 0), axis=1)
    code = jnp.sum(jnp.where(hit, (1 + chg_cols % 256 * 128 + block_index(chg_rows % 128))[None, :], 0), axis=1)
    slot_rows = jnp.where(code > 0, (code - 1) // 128, 0).reshape(DEV, CAP)
    slot_cols = jnp.where(code > 0, (code - 1) % 128, 128).reshape(DEV, CAP)
    meta = jnp.pad(jnp.concatenate([slot_rows, slot_cols], axis=1).astype(BF), ((0, 0), (0, TILE - 2 * CAP)))
    meta = jnp.broadcast_to(meta[:, None, :], (DEV, 16, TILE))
    send = pack(pick, chg_tiles, meta)
    xs = embed.reshape(4, 2, NC, 16, K).transpose(2, 0, 3, 1, 4).reshape(NC, 4, 16, TILE)
    slots, xc = exchange(send, xs)
    places = slots.reshape(DEV, SLOT_ROWS, TILE)[:, CAP * TILE, :2 * CAP].astype(jnp.int32)
    rows = places[:, :CAP].reshape(DEV * CAP)
    cols = places[:, CAP:].reshape(DEV * CAP)
    own_rows = tile_rows % 256
    own_cols = block_index(tile_cols % 128)
    degree = None
    for iteration in range(ITERS):
        first, last = iteration == 0, iteration == ITERS - 1
        outs = product(first, rows, cols, own_rows, own_cols, xc, tiles, slots)
        if first:
            xc, degree = normalize(first, last, outs[0], outs[1])
        else:
            (xc,) = normalize(first, last, outs[0], degree)
    return xc


def solution(mesh):
    placed = (
        P(("row", "col"), None),
        P(("row", "col"), None, None),
        P(("row", "col")),
        P(("row", "col")),
        P(("row", "col"), None, None),
        P(("row", "col")),
        P(("row", "col")),
    )
    return jax.shard_map(
        local, mesh=mesh, in_specs=placed, out_specs=P(("row", "col"), None), check_vma=False
    )
```

time: 1210 us -> 1160 us (0.959)
  Pallas kernels: 0 us -> 1150 us
  waiting for transfers between devices: 447 us -> 0 us
  other arithmetic: 287 us -> 2.71 us
  blocking collectives: 230 us -> 0 us
  local copies, waits for them, and re-layouts: 137 us -> 13.1 us
  matrix products: 59.9 us -> 0 us
  starting transfers between devices: 26.2 us -> 0 us
  between operations: 16.4 us -> 0.16 us
    pallas_call x0 -> x8, Pallas kernels: none -> 1150 us  [the longest x3 476 us: normalize(): pl.pallas_call(functools.partial(normalize_kernel, first, last), out_shap...]
    reduce_scatter x3 -> x0, waiting for transfers between devices: 233 us -> none  [local(): lax.psum_scatter(partial_value.reshape(row_blocks * tile_size, feature_wi...]
    scatter-add x8 -> x0, other arithmetic: 213 us -> none  [the longest x3 182 us: block_terms(): jax.ops.segment_sum(taken_terms, taken_rows, row_blocks)]
    all_gather x3 -> x0, waiting for transfers between devices: 200 us -> none  [local(): lax.all_gather(received_terms.reshape(rows_dev, feature_width), 'row', ax...]
    psum x3 -> x0, blocking collectives: 199 us -> none  [local(): gram = lax.psum(local_gram, ('row', 'col')) / nodes]
    dot_general x9 -> x0, matrix products: 54.3 us -> none  [the longest x3 43.1 us: block_terms(): jnp.einsum('nab,nak->nbk', taken, blocked[taken_cols], preferred_element_...]
    scatter x3 -> x0, local copies, waits for them, and re-layouts: 42.5 us -> none  [the longest x1 30.9 us: local(): outgoing = jnp.zeros((devices, CAP, tile_size, tile_size), jnp.bfloat16)....]
    gather x6 -> x0, local copies, waits for them, and re-layouts: 42 us -> none  [the longest x3 39.7 us: block_terms(): blocked[taken_cols]]
  transfers between devices with their start and end apart: 10 -> 0, of which waited for: 8 -> 0; matrix products, arithmetic and copies ran while one was open for 14% -> 0% of each run, Pallas kernels for 0% -> 0%
where the time goes in v1:
time: 1160 us
  Pallas kernels  1150 us (99%)
  local copies, waits for them, and re-layouts  13.1 us (1%)
    pallas_call x3, Pallas kernels, normalize(): pl.pallas_call(functools.partial(normalize_kernel, first, last), out_shap...  476 us
    pallas_call x1, Pallas kernels, pack(): pl.pallas_call(pack_kernel, out_shape=jax.ShapeDtypeStruct((DEV, SLOT_ROW...  399 us
    pallas_call x1, Pallas kernels, exchange(): pl.pallas_call(exchange_kernel, out_shape=(slots, slots, jax.ShapeDtypeSt...  186 us
    pallas_call x3, Pallas kernels, product(): pl.pallas_call(functools.partial(product_kernel, with_degree), grid=(DEV...  84.7 us

profile of v1, /device:TPU:1, one launch (start us, length us, event | category | flops | bytes accessed | tf_op | source)
XLA Modules:
  0.0 1161.5 jit_solution(10854242701155198750)
XLA Ops:
  0.0 0.7 fusion.8
  0.7 0.2 convert_reduce_fusion
  0.9 0.7 select_reduce_fusion
  1.6 0.2 sub.45
  1.9 0.1 copy.25
  1.9 0.3 gt.10
  2.2 0.1 copy.29
  2.3 0.1 copy.35
  2.5 0.9 broadcast_in_dim.38.meta_ref
  3.3 0.0 copy-start.5
  3.3 399.0 %pack.1 = bf16[128,400,128]{2,1,0:T(8,128)(2,1)} custom-call(s32[384]{0:T(512)} %get-tuple-element.18.pick_ref, bf16[192,128,128]{2,1,0:T(8,128)(2,1)} %tiles_ref.1, bf16[128,16,128]{2,1,0:T(8,128)(2,1)} %broadcast_in_dim.38.meta_ref), custom_call_target="tpu_custom_call" | custom-call | tf_op jit(solution)/shard_map/pack/pallas_call | solution.py:54
  402.3 0.0 copy-done.5
  402.3 0.3 copy.32
  402.6 0.5 copy.33
  403.2 1.0 reshape.47.xs_ref
  404.1 0.0 copy-start.6
  404.1 0.0 copy-start.7
  404.1 0.0 copy-start
  404.1 186.2 %exchange.1 = (bf16[8,16,400,128]{3,2,1,0:T(8,128)(2,1)}, bf16[8,16,400,128]{3,2,1,0:T(8,128)(2,1)}, bf16[8,16,4,16,128]{4,3,2,1,0:T(8,128)(2,1)}) custom-call(bf16[8,16,400,128]{3,2,1,0:T(8,128)(2,1)} %bitcast.16, bf16[16,4,16,128]{3,2,1,0:T(8,128)(2,1)} %reshape.47.xs_ref), custom_call_target="tpu_custom_call" | custom-call | tf_op jit(solution)/shard_map/exchange/pallas_call | solution.py:168
  590.3 1.0 slice_convert_fusion
  591.3 0.1 fusion.19
  591.4 0.2 reshape.49.rows_ref
  591.6 0.2 reshape.50.cols_ref
  591.8 0.0 copy-done.6
  591.8 0.0 copy-done.7
  591.9 0.0 copy-done
  591.9 0.0 copy-start.4
  591.9 1.6 copy-done.4
  593.5 29.5 %product.3 = (bf16[256,64,128]{2,1,0:T(8,128)(2,1)}, f32[256,1,128]{2,1,0:T(1,128)S(1)}) custom-call(s32[384]{0:T(512)S(1)} %reshape.49.rows_ref, s32[384]{0:T(512)S(1)} %reshape.50.cols_ref, s32[64]{0:T(128)S(1)} %get-tuple-element.25.own_rows_ref, s32[64]{0:T(128)S(1)} %get-tuple-element.26.own_cols_ref, bf16[128,4,16,128]{3,2,1,0:T(8,128)(2,1)S(1)} %bitcast.10, ...), custom_call_target="tpu_custom_call" | custom-call | flops 939524096 | bytes 14680064 | tf_op jit(solution)/shard_map/product/pallas_call | solution.py:262
  623.0 0.0 copy-start.3
  623.0 2.2 copy-done.3
  625.2 210.0 %normalize.3 = (bf16[8,16,4,16,128]{4,3,2,1,0:T(8,128)(2,1)S(1)}, f32[16,1,128]{2,1,0:T(1,128)S(1)}) custom-call(bf16[256,64,128]{2,1,0:T(8,128)(2,1)S(1)} %copy-done.3, f32[256,1,128]{2,1,0:T(1,128)S(1)} %get-tuple-element.14.degree_in_ref), custom_call_target="tpu_custom_call" | custom-call | tf_op jit(solution)/shard_map/normalize/pallas_call | solution.py:415
  835.2 27.6 %product.4.part_ref = bf16[256,64,128]{2,1,0:T(8,128)(2,1)} custom-call(s32[384]{0:T(512)S(1)} %reshape.49.rows_ref, s32[384]{0:T(512)S(1)} %reshape.50.cols_ref, s32[64]{0:T(128)S(1)} %get-tuple-element.25.own_rows_ref, s32[64]{0:T(128)S(1)} %get-tuple-element.26.own_cols_ref, bf16[128,4,16,128]{3,2,1,0:T(8,128)(2,1)S(1)} %bitcast.11, ...), custom_call_target="tpu_custom_call" | custom-call | flops 939524096 | bytes 14680064 | tf_op jit(solution)/shard_map/product/pallas_call | solution.py:262
  862.8 0.0 copy-start.2
  862.8 2.2 copy-done.2
  865.0 151.1 %normalize.4 = bf16[8,16,4,16,128]{4,3,2,1,0:T(8,128)(2,1)S(1)} custom-call(bf16[256,64,128]{2,1,0:T(8,128)(2,1)S(1)} %copy-done.2, f32[16,1,128]{2,1,0:T(1,128)S(1)} %get-tuple-element.16.degree_in_ref), custom_call_target="tpu_custom_call" | custom-call | tf_op jit(solution)/shard_map/normalize/pallas_call | solution.py:415
  1016.1 27.6 %product.5.part_ref = bf16[256,64,128]{2,1,0:T(8,128)(2,1)} custom-call(s32[384]{0:T(512)S(1)} %reshape.49.rows_ref, s32[384]{0:T(512)S(1)} %reshape.50.cols_ref, s32[64]{0:T(128)S(1)} %get-tuple-element.25.own_rows_ref, s32[64]{0:T(128)S(1)} %get-tuple-element.26.own_cols_ref, bf16[128,4,16,128]{3,2,1,0:T(8,128)(2,1)S(1)} %bitcast.9, ...), custom_call_target="tpu_custom_call" | custom-call | flops 939524096 | bytes 14680064 | tf_op jit(solution)/shard_map/product/pallas_call | solution.py:262
  1043.7 0.0 copy-start.1
  1043.7 2.2 copy-done.1
  1045.9 114.5 %normalize.5 = f32[2048,64]{1,0:T(8,128)S(1)} custom-call(bf16[256,64,128]{2,1,0:T(8,128)(2,1)S(1)} %copy-done.1, f32[16,1,128]{2,1,0:T(1,128)S(1)} %get-tuple-element.16.degree_in_ref), custom_call_target="tpu_custom_call" | custom-call | tf_op jit(solution)/shard_map/normalize/pallas_call | solution.py:415
  1160.4 1.1 copy.34
  (7 shorter events, 0.1 us)
Async XLA Ops:
  3.3 399.0 %copy-start.5 = (bf16[2048,64]{0,1:T(8,128)(2,1)S(1)}, bf16[2048,64]{0,1:T(8,128)(2,1)}, u32[]{:S(2)}) copy-start(bf16[2048,64]{0,1:T(8,128)(2,1)} %param.7) | copy-start | bytes 786436
  404.1 187.7 %copy-start.6 = (s32[64]{0:T(128)S(1)}, s32[64]{0:T(128)}, u32[]{:S(2)}) copy-start(s32[64]{0:T(128)} %param.9) | copy-start | bytes 772
  404.1 187.7 %copy-start.7 = (s32[64]{0:T(128)S(1)}, s32[64]{0:T(128)}, u32[]{:S(2)}) copy-start(s32[64]{0:T(128)} %param.10) | copy-start | bytes 772
  404.1 187.7 %copy-start = (bf16[64,128,128]{2,1,0:T(8,128)(2,1)S(1)}, bf16[64,128,128]{2,1,0:T(8,128)(2,1)}, u32[]{:S(2)}) copy-start(bf16[64,128,128]{2,1,0:T(8,128)(2,1)} %own_ref.5) | copy-start | bytes 6291460
  591.9 1.6 copy-start.4
  623.0 2.2 copy-start.3
  862.8 2.2 copy-start.2
  1043.7 2.2 copy-start.1

commit v2 on v1

--- a/solution.py
+++ b/solution.py
@@ -31,32 +31,28 @@
     return lax.dot_general(a, b, (dims, ((), ())), precision=precision, preferred_element_type=F32)
 
 
-def pack_kernel(pick_ref, tiles_ref, meta_ref, out_ref, tile_sem, meta_sem):
-    meta_copy = pltpu.make_async_copy(meta_ref, out_ref.at[:, pl.ds(CAP * TILE, 16)], meta_sem)
-    meta_copy.start()
-
-    def body(owner, carry):
+def pack_kernel(pick_ref, tiles_ref, meta_ref, out_ref):
+    step = pl.program_id(0)
+
+    def body(i, carry):
         for slot in range(CAP):
-            pltpu.make_async_copy(
-                tiles_ref.at[pick_ref[owner * CAP + slot]],
-                out_ref.at[owner, pl.ds(slot * TILE, TILE)],
-                tile_sem,
-            ).start()
-        return carry
-
-    lax.fori_loop(0, DEV, body, 0)
-    filled = out_ref.at[:, pl.ds(0, CAP * TILE)]
-    pltpu.make_async_copy(filled, filled, tile_sem).wait()
-    meta_copy.wait()
+            tile = tiles_ref[pick_ref[(step * 8 + i) * CAP + slot]]
+            out_ref[i, slot * TILE:(slot + 1) * TILE] = tile
+        out_ref[i, CAP * TILE:] = meta_ref[i]
+        return carry
+
+    lax.fori_loop(0, 8, body, 0)
 
 
 def pack(pick, chg_tiles, meta):
     return pl.pallas_call(
         pack_kernel,
+        grid=(DEV // 8,),
         out_shape=jax.ShapeDtypeStruct((DEV, SLOT_ROWS, TILE), BF),
-        in_specs=[SMEM, ANY, ANY],
-        out_specs=ANY,
-        scratch_shapes=[pltpu.SemaphoreType.DMA, pltpu.SemaphoreType.DMA],
+        in_specs=[SMEM, pl.BlockSpec(chg_tiles.shape, lambda i: (0, 0, 0)),
+                  pl.BlockSpec((8, 16, TILE), lambda i: (i, 0, 0))],
+        out_specs=pl.BlockSpec((8, SLOT_ROWS, TILE), lambda i: (i, 0, 0)),
+        compiler_params=pltpu.CompilerParams(vmem_limit_bytes=32 * MIB),
         name="pack",
     )(pick, chg_tiles, meta)
 
@@ -179,7 +175,7 @@
 
 def product_kernel(with_degree, rows_ref, cols_ref, own_rows_ref, own_cols_ref, x_ref, own_ref, slots_ref, *rest):
     if with_degree:
-        part_ref, degree_ref, xt_ref, acc_ref = rest
+        part_ref, degree_out_ref, xt_ref, acc_ref, degree_ref = rest
     else:
         part_ref, xt_ref, acc_ref = rest
         degree_ref = None
@@ -249,6 +245,8 @@
             return carry
 
         lax.fori_loop(0, ROWS_BLK // 8, flush, 0)
+        if with_degree:
+            degree_out_ref[...] = degree_ref[...].reshape(ROWS_BLK, TILE)
 
 
 def product(with_degree, rows, cols, own_rows, own_cols, xc, own, slots):
@@ -256,8 +254,11 @@
     out_shape = [jax.ShapeDtypeStruct((ROWS_BLK, K, TILE), BF)]
     out_specs = [whole((ROWS_BLK, K, TILE))]
     if with_degree:
-        out_shape.append(jax.ShapeDtypeStruct((ROWS_BLK, 1, TILE), F32))
-        out_specs.append(whole((ROWS_BLK, 1, TILE)))
+        out_shape.append(jax.ShapeDtypeStruct((ROWS_BLK, TILE), F32))
+        out_specs.append(whole((ROWS_BLK, TILE)))
+    scratch = [pltpu.VMEM((130, K, TILE), BF), pltpu.VMEM((ROWS_BLK, K, TILE), F32)]
+    if with_degree:
+        scratch.append(pltpu.VMEM((ROWS_BLK, 1, TILE), F32))
     terms = DEV * CAP + OWN
     return pl.pallas_call(
         functools.partial(product_kernel, with_degree),
@@ -266,7 +267,7 @@
         in_specs=[SMEM, SMEM, SMEM, SMEM, whole((DEV, 4, 16, TILE)), whole((OWN, TILE, TILE)),
                   pl.BlockSpec((8, SLOT_ROWS, TILE), lambda i: (i, 0, 0))],
         out_specs=out_specs,
-        scratch_shapes=[pltpu.VMEM((130, K, TILE), BF), pltpu.VMEM((ROWS_BLK, K, TILE), F32)],
+        scratch_shapes=scratch,
         compiler_params=pltpu.CompilerParams(vmem_limit_bytes=48 * MIB),
         cost_estimate=pl.CostEstimate(flops=terms * 2 * K * TILE * TILE, bytes_accessed=terms * TILE * TILE * 2, transcendentals=0),
         name="product",
@@ -337,7 +338,7 @@
 
     gram = jnp.zeros((K, K), F32)
     for b in range(16):
-        block = y_ref[b] * (1.0 / degree_ref[b])
+        block = y_ref[b] * (1.0 / degree_ref[b:b + 1])
         y_ref[b] = block
         gram = gram + dot(block, block, ((1,), (1,)), lax.Precision.HIGHEST)
     half = K // 2
@@ -401,7 +402,7 @@
         out_shape.append(jax.ShapeDtypeStruct((NR, NC, 4, 16, TILE), BF))
         out_specs.append(ANY)
     if first:
-        out_shape.append(jax.ShapeDtypeStruct((16, 1, TILE), F32))
+        out_shape.append(jax.ShapeDtypeStruct((16, TILE), F32))
         out_specs.append(VMEM)
     scratch = [
         pltpu.VMEM((16, K, TILE), F32), pltpu.VMEM((NC, 16, K, TILE), BF),
@@ -409,7 +410,7 @@
         dma, dma, dma((NC,)), dma, dma, dma, dma,
     ]
     if first:
-        scratch += [pltpu.VMEM((NC, 16, 1, TILE), F32), dma, dma, dma]
+        scratch += [pltpu.VMEM((NC, 16, TILE), F32), dma, dma, dma]
     if not last:
         scratch += [pltpu.VMEM((NC, 4, 16, TILE), BF), dma, dma, dma, dma, dma]
     return pl.pallas_call(

time: 1160 us -> 773 us (0.67)
  Pallas kernels: 1150 us -> 750 us
    pallas_call x1, Pallas kernels: 399 us -> 2.53 us  [pack(): pl.pallas_call(pack_kernel, grid=(DEV // 8,), out_shape=jax.ShapeDtypeStr...]
where the time goes in v2:
time: 773 us; the launch traced here: 772 us
  Pallas kernels  750 us (97%)
  local copies, waits for them, and re-layouts  19.8 us (3%)
    pallas_call x3, Pallas kernels, normalize(): pl.pallas_call(functools.partial(normalize_kernel, first, last), out_shap...  476 us
    pallas_call x1, Pallas kernels, exchange(): pl.pallas_call(exchange_kernel, out_shape=(slots, slots, jax.ShapeDtypeSt...  186 us
    pallas_call x3, Pallas kernels, product(): pl.pallas_call(functools.partial(product_kernel, with_degree), grid=(DEV...  84.8 us
    unnamed x22, local copies, waits for them, and re-layouts  16.1 us

profile of v2, /device:TPU:1, one launch (start us, length us, event | category | flops | bytes accessed | tf_op | source)
XLA Modules:
  0.0 771.9 jit_solution(4868706558259732643)
XLA Ops:
  0.0 0.7 fusion.8
  0.7 0.2 convert_reduce_fusion
  0.9 0.1 select_reduce_fusion
  1.1 0.2 sub.45
  1.3 0.1 copy.25
  1.3 0.3 gt.10
  1.6 0.1 copy.29
  1.7 0.1 copy.35
  1.9 0.1 broadcast_in_dim.38.meta_ref
  2.0 0.0 copy-start.4
  2.0 2.8 copy-done.4
  4.8 0.0 copy-start.7
  4.8 2.5 pack.1
  7.3 0.0 copy-start
  7.3 4.7 copy-done
  12.0 0.0 copy-done.7
  12.0 0.3 copy.32
  12.3 0.5 copy.33
  12.9 1.0 reshape.47.xs_ref
  13.8 0.0 copy-start.8
  13.8 0.0 copy-start.9
  13.8 0.0 copy-start.1
  13.8 186.2 %exchange.1 = (bf16[8,16,400,128]{3,2,1,0:T(8,128)(2,1)}, bf16[8,16,400,128]{3,2,1,0:T(8,128)(2,1)}, bf16[8,16,4,16,128]{4,3,2,1,0:T(8,128)(2,1)}) custom-call(bf16[8,16,400,128]{3,2,1,0:T(8,128)(2,1)} %bitcast.9, bf16[16,4,16,128]{3,2,1,0:T(8,128)(2,1)} %reshape.47.xs_ref), custom_call_target="tpu_custom_call" | custom-call | tf_op jit(solution)/shard_map/exchange/pallas_call | solution.py:164
  200.0 1.0 slice_convert_fusion
  201.0 0.1 fusion.19
  201.1 0.2 reshape.49.rows_ref
  201.3 0.2 reshape.50.cols_ref
  201.5 0.0 copy-done.8
  201.5 0.0 copy-done.9
  201.5 0.0 copy-done.1
  201.6 0.0 copy-start.6
  201.6 1.6 copy-done.6
  203.1 29.6 %product.3 = (bf16[256,64,128]{2,1,0:T(8,128)(2,1)}, f32[256,128]{1,0:T(8,128)S(1)}) custom-call(s32[384]{0:T(512)S(1)} %reshape.49.rows_ref, s32[384]{0:T(512)S(1)} %reshape.50.cols_ref, s32[64]{0:T(128)S(1)} %get-tuple-element.25.own_rows_ref, s32[64]{0:T(128)S(1)} %get-tuple-element.26.own_cols_ref, bf16[128,4,16,128]{3,2,1,0:T(8,128)(2,1)S(1)} %bitcast.11, ...), custom_call_target="tpu_custom_call" | custom-call | flops 939524096 | bytes 14680064 | tf_op jit(solution)/shard_map/product/pallas_call | solution.py:263
  232.7 0.0 copy-start.5
  232.7 2.2 copy-done.5
  234.9 210.0 %normalize.3 = (bf16[8,16,4,16,128]{4,3,2,1,0:T(8,128)(2,1)S(1)}, f32[16,128]{1,0:T(8,128)S(1)}) custom-call(bf16[256,64,128]{2,1,0:T(8,128)(2,1)S(1)} %copy-done.5, f32[256,128]{1,0:T(8,128)S(1)} %get-tuple-element.14.degree_in_ref), custom_call_target="tpu_custom_call" | custom-call | tf_op jit(solution)/shard_map/normalize/pallas_call | solution.py:416
  444.9 27.6 %product.4.part_ref = bf16[256,64,128]{2,1,0:T(8,128)(2,1)} custom-call(s32[384]{0:T(512)S(1)} %reshape.49.rows_ref, s32[384]{0:T(512)S(1)} %reshape.50.cols_ref, s32[64]{0:T(128)S(1)} %get-tuple-element.25.own_rows_ref, s32[64]{0:T(128)S(1)} %get-tuple-element.26.own_cols_ref, bf16[128,4,16,128]{3,2,1,0:T(8,128)(2,1)S(1)} %bitcast.12, ...), custom_call_target="tpu_custom_call" | custom-call | flops 939524096 | bytes 14680064 | tf_op jit(solution)/shard_map/product/pallas_call | solution.py:263
  472.5 0.0 copy-start.3
  472.5 2.2 copy-done.3
  474.7 151.1 %normalize.4 = bf16[8,16,4,16,128]{4,3,2,1,0:T(8,128)(2,1)S(1)} custom-call(bf16[256,64,128]{2,1,0:T(8,128)(2,1)S(1)} %copy-done.3, f32[16,128]{1,0:T(8,128)S(1)} %get-tuple-element.16.degree_in_ref), custom_call_target="tpu_custom_call" | custom-call | tf_op jit(solution)/shard_map/normalize/pallas_call | solution.py:416
  625.9 27.6 %product.5.part_ref = bf16[256,64,128]{2,1,0:T(8,128)(2,1)} custom-call(s32[384]{0:T(512)S(1)} %reshape.49.rows_ref, s32[384]{0:T(512)S(1)} %reshape.50.cols_ref, s32[64]{0:T(128)S(1)} %get-tuple-element.25.own_rows_ref, s32[64]{0:T(128)S(1)} %get-tuple-element.26.own_cols_ref, bf16[128,4,16,128]{3,2,1,0:T(8,128)(2,1)S(1)} %bitcast.10, ...), custom_call_target="tpu_custom_call" | custom-call | flops 939524096 | bytes 14680064 | tf_op jit(solution)/shard_map/product/pallas_call | solution.py:263
  653.5 0.0 copy-start.2
  653.5 2.2 copy-done.2
  655.6 115.1 %normalize.5 = f32[2048,64]{1,0:T(8,128)S(1)} custom-call(bf16[256,64,128]{2,1,0:T(8,128)(2,1)S(1)} %copy-done.2, f32[16,128]{1,0:T(8,128)S(1)} %get-tuple-element.16.degree_in_ref), custom_call_target="tpu_custom_call" | custom-call | tf_op jit(solution)/shard_map/normalize/pallas_call | solution.py:416
  770.8 1.1 copy.34
  (7 shorter events, 0.1 us)
Async XLA Ops:
  2.0 2.8 copy-start.4
  4.8 7.3 copy-start.7
  7.3 4.7 copy-start
  13.8 187.7 %copy-start.8 = (s32[64]{0:T(128)S(1)}, s32[64]{0:T(128)}, u32[]{:S(2)}) copy-start(s32[64]{0:T(128)} %param.9) | copy-start | bytes 772
  13.8 187.7 %copy-start.9 = (s32[64]{0:T(128)S(1)}, s32[64]{0:T(128)}, u32[]{:S(2)}) copy-start(s32[64]{0:T(128)} %param.10) | copy-start | bytes 772
  13.8 187.7 %copy-start.1 = (bf16[64,128,128]{2,1,0:T(8,128)(2,1)S(1)}, bf16[64,128,128]{2,1,0:T(8,128)(2,1)}, u32[]{:S(2)}) copy-start(bf16[64,128,128]{2,1,0:T(8,128)(2,1)} %own_ref.5) | copy-start | bytes 6291460
  201.6 1.6 copy-start.6
  232.7 2.2 copy-start.5
  472.5 2.2 copy-start.3
  653.5 2.2 copy-start.2

commit v3 on v2

--- a/solution.py
+++ b/solution.py
@@ -84,12 +84,19 @@
     pltpu.make_async_copy(ref, ref, sem).wait()
 
 
+def col_peer(col, k):
+    return lax.rem(col // 4 + k // 4, 4) * 4 + lax.rem(lax.rem(col, 4) + lax.rem(k, 4), 4)
+
+
+def row_peer(row, dz, flip=0):
+    return lax.rem(row // 2 + dz, 4) * 2 + lax.rem(row + flip, 2)
+
+
 def x_first(row, col, xs, xc, sems):
-    own = pltpu.make_async_copy(xs.at[col], xc.at[row, col], sems["x_own"])
-    own.start()
+    pltpu.make_async_copy(xs.at[col], xc.at[row, col], sems["x_own"]).start()
 
     def send(k, carry):
-        peer = lax.rem(col + k, NC)
+        peer = col_peer(col, k)
         remote(xs.at[peer], xc.at[row, col], sems["xa_send"], sems["xa_recv"], col=peer).start()
         return carry
 
@@ -99,19 +106,32 @@
 def x_second(row, col, xs, xc, sems):
     pltpu.make_async_copy(xs.at[col], xc.at[row, col], sems["x_own"]).wait()
     wait_bytes(xc.at[row, pl.ds(0, NC - 1)], sems["xa_recv"])
-
-    def send(k, carry):
-        peer = lax.rem(row + k, NR)
-        remote(xc.at[row], xc.at[row], sems["xb_send"], sems["xb_recv"], row=peer).start()
-        return carry
-
-    lax.fori_loop(1, NR, send, 0)
+    for i, (dz, flip) in enumerate(((1, 0), (3, 0), (2, 0), (0, 1))):
+        remote(xc.at[row], xc.at[row], sems["xb_send"].at[i], sems["xb_recv"].at[row], row=row_peer(row, dz, flip)).start()
+
+
+def x_third(row, col, xs, xc, sems):
+    for i, dz in enumerate((1, 3, 2)):
+        source = row_peer(row, dz)
+        wait_bytes(xc.at[source], sems["xb_recv"].at[source])
+        remote(xc.at[source], xc.at[source], sems["xb_send"].at[4 + i], sems["xb_recv"].at[source], row=row_peer(row, 0, 1)).start()
 
 
 def x_finish(row, col, xs, xc, sems):
+    for dz in range(4):
+        source = row_peer(row, dz, 1)
+        wait_bytes(xc.at[source], sems["xb_recv"].at[source])
     wait_bytes(xs.at[pl.ds(0, NC - 1)], sems["xa_send"])
-    wait_bytes(xc.at[pl.ds(0, NR - 1)], sems["xb_recv"])
-    wait_bytes(xc.at[pl.ds(0, NR - 1)], sems["xb_send"])
+    for i in range(7):
+        wait_bytes(xc.at[row], sems["xb_send"].at[i])
+
+
+X_SEMS = ("x_own", "xa_send", "xa_recv", "xb_send", "xb_recv")
+
+
+def x_sems():
+    dma = pltpu.SemaphoreType.DMA
+    return [dma, dma, dma, dma((7,)), dma((NR,))]
 
 
 def exchange_kernel(send_ref, xs_ref, recv_ref, mid_ref, xc_ref,
@@ -131,7 +151,7 @@
         pltpu.make_async_copy(send_ref.at[target, col], dst_ref.at[target, col], a_own.at[step]).start()
 
         def send(k, carry):
-            peer = lax.rem(col + k, NC)
+            peer = col_peer(col, k)
             remote(send_ref.at[target, peer], dst_ref.at[target, col], a_send.at[step], a_recv.at[step], col=peer).start()
             return carry
 
@@ -142,6 +162,7 @@
     for step in range(1, NR - 1):
         first(step, targets[step], mid_ref)
     first(NR - 1, row, recv_ref)
+    x_third(row, col, xs_ref, xc_ref, sems)
     for step in range(NR - 1):
         target = targets[step]
         wait_bytes(mid_ref.at[target, pl.ds(0, NC - 1)], a_recv.at[step])
@@ -166,7 +187,7 @@
         out_shape=(slots, slots, jax.ShapeDtypeStruct((NR, NC, 4, 16, TILE), BF)),
         in_specs=[ANY, ANY],
         out_specs=(ANY, ANY, ANY),
-        scratch_shapes=[dma, dma, dma, dma, dma, dma((NR,)), dma((NR,)), dma((NR,)), dma((NR,)), dma((NR,))],
+        scratch_shapes=x_sems() + [dma((NR,)), dma((NR,)), dma((NR,)), dma((NR,)), dma((NR,))],
         compiler_params=pltpu.CompilerParams(collective_id=0, has_side_effects=True),
         name="exchange",
     )(send.reshape(NR, NC, SLOT_ROWS, TILE), xs)
@@ -287,37 +308,74 @@
     return lax.rsqrt(pivots) * work[:, K:]
 
 
+def gram_pack(gram):
+    return jnp.concatenate([gram[:K // 2], gram[K // 2:]], axis=1)
+
+
+def gram_unpack(packed):
+    return jnp.concatenate([packed[:, :K], packed[:, K:]], axis=0)
+
+
 def normalize_kernel(first, last, part_ref, degree_in_ref, *rest):
     rest = list(rest)
+    take = lambda count: [rest.pop(0) for _ in range(count)]
+    gram_in_ref = None if first else rest.pop(0)
     if last:
-        z_ref = rest.pop(0)
-        xc_ref = None
+        (z_ref,) = take(1)
     else:
-        xc_ref = rest.pop(0)
+        xc_ref, gram_ref = take(2)
     degree_ref = rest.pop(0) if first else degree_in_ref
-    y_ref, rs_ref, g1_ref, g2_ref = [rest.pop(0) for _ in range(4)]
-    rs_own, rs_send, rs_recv, g1_send, g1_recv, g2_send, g2_recv = [rest.pop(0) for _ in range(7)]
+    y_ref, a1_ref, r1_ref, a2_ref, g1_ref, g2_ref, g3_ref = take(7)
+    s1_send, s1_recv, s2_send, s2_recv, g_send, g_recv = take(6)
     if first:
-        dg_ref, dg_own, dg_send, dg_recv = [rest.pop(0) for _ in range(4)]
+        dg_ref, dg_own, dg_send, dg_recv = take(4)
     if not last:
         xs_ref = rest.pop(0)
-        sems = dict(zip(("x_own", "xa_send", "xa_recv", "xb_send", "xb_recv"), rest))
+        sems = dict(zip(X_SEMS, rest))
     row = lax.axis_index("row")
     col = lax.axis_index("col")
+    x, y = col // 4, lax.rem(col, 4)
+    x_peer = lambda k: lax.rem(x + k, 4) * 4 + y
+    y_peer = lambda k: x * 4 + lax.rem(y + k, 4)
     greet(row, col)
 
+    for k in (1, 3, 2):
+        remote(part_ref.at[lax.rem(x + k, 4), :, pl.ds(0, 8)], a1_ref.at[0, k - 1],
+               s1_send.at[0, k - 1], s1_recv.at[0, k - 1], col=x_peer(k)).start()
+        remote(part_ref.at[:, lax.rem(y + k, 4), pl.ds(8, 8)], a1_ref.at[1, k - 1],
+               s1_send.at[1, k - 1], s1_recv.at[1, k - 1], col=y_peer(k)).start()
     if first:
         pltpu.make_async_copy(degree_in_ref.at[pl.ds(col * 16, 16)], dg_ref.at[col], dg_own).start()
-    pltpu.make_async_copy(part_ref.at[pl.ds(col * 16, 16)], rs_ref.at[col], rs_own).start()
-
-    def send(k, carry):
-        peer = lax.rem(col + k, NC)
-        if first:
+
+        def send(k, carry):
+            peer = col_peer(col, k)
             remote(degree_in_ref.at[pl.ds(peer * 16, 16)], dg_ref.at[col], dg_send, dg_recv, col=peer).start()
-        remote(part_ref.at[pl.ds(peer * 16, 16)], rs_ref.at[col], rs_send, rs_recv.at[col], col=peer).start()
-        return carry
-
-    lax.fori_loop(1, NC, send, 0)
+            return carry
+
+        lax.fori_loop(1, NC, send, 0)
+    else:
+        inverse = inverse_factor(gram_unpack(gram_in_ref[...]))
+    for h in range(2):
+        for k in range(3):
+            wait_bytes(a1_ref.at[h, k], s1_recv.at[h, k])
+        for k in (1, 3, 2, 0):
+            target = lax.rem((x if h else y) + k, 4)
+
+            def add(b, carry):
+                mine = part_ref[target, y, 8 + b] if h else part_ref[x, target, b]
+                value = mine.astype(F32)
+                for source in range(3):
+                    value = value + a1_ref[h, source, target, b].astype(F32)
+                if k:
+                    r1_ref[h, k - 1, b] = value.astype(BF)
+                else:
+                    y_ref[h * 8 + b] = value
+                return carry
+
+            lax.fori_loop(0, 8, add, 0)
+            if k:
+                remote(r1_ref.at[h, k - 1], a2_ref.at[h, k - 1], s2_send.at[h, k - 1], s2_recv.at[h, k - 1],
+                       col=x_peer(k) if h else y_peer(k)).start()
     if first:
         pltpu.make_async_copy(degree_in_ref.at[pl.ds(col * 16, 16)], dg_ref.at[col], dg_own).wait()
         wait_bytes(dg_ref.at[pl.ds(0, NC - 1)], dg_recv)
@@ -325,105 +383,105 @@
         for k in range(1, NC):
             degree = degree + dg_ref[k]
         degree_ref[...] = 1.0 + degree
-    pltpu.make_async_copy(part_ref.at[pl.ds(col * 16, 16)], rs_ref.at[col], rs_own).wait()
-    y_ref[...] = rs_ref[col].astype(F32)
-
-    def gather(k, carry):
-        peer = lax.rem(col + NC - k, NC)
-        wait_bytes(rs_ref.at[peer], rs_recv.at[peer])
-        y_ref[...] += rs_ref[peer].astype(F32)
-        return carry
-
-    lax.fori_loop(1, NC, gather, 0)
+    for h in range(2):
+        for k in range(3):
+            wait_bytes(a2_ref.at[h, k], s2_recv.at[h, k])
+        for b in range(8):
+            value = y_ref[h * 8 + b]
+            for k in range(3):
+                value = value + a2_ref[h, k, b].astype(F32)
+            value = value * (1.0 / degree_ref[h * 8 + b:h * 8 + b + 1])
+            if not first:
+                value = dot(inverse, value, ((1,), (0,)), lax.Precision.HIGHEST)
+            y_ref[h * 8 + b] = value
+
+    if not last:
+        for pair in range(4):
+            for part in range(2):
+                both = jnp.concatenate([y_ref[pair * 4 + part], y_ref[pair * 4 + 2 + part]], axis=0).T
+                xs_ref[part * 8:(part + 1) * 8, pair] = both.astype(BF).reshape(8, 16, TILE)
+        x_first(row, col, xs_ref, xc_ref, sems)
 
     gram = jnp.zeros((K, K), F32)
     for b in range(16):
-        block = y_ref[b] * (1.0 / degree_ref[b:b + 1])
-        y_ref[b] = block
+        block = y_ref[b]
         gram = gram + dot(block, block, ((1,), (1,)), lax.Precision.HIGHEST)
-    half = K // 2
-    g1_ref[col] = jnp.concatenate([gram[:half], gram[half:]], axis=1)
-
-    def send_g1(k, carry):
-        peer = lax.rem(col + k, NC)
-        remote(g1_ref.at[col], g1_ref.at[col], g1_send, g1_recv, col=peer).start()
-        return carry
-
-    lax.fori_loop(1, NC, send_g1, 0)
-    wait_bytes(g1_ref.at[pl.ds(0, NC - 1)], g1_recv)
-    total = g1_ref[0]
-    for k in range(1, NC):
-        total = total + g1_ref[k]
-    g2_ref[row] = total
-
-    def send_g2(k, carry):
-        peer = lax.rem(row + k, NR)
-        remote(g2_ref.at[row], g2_ref.at[row], g2_send, g2_recv, row=peer).start()
-        return carry
-
-    lax.fori_loop(1, NR, send_g2, 0)
-    wait_bytes(g2_ref.at[pl.ds(0, NR - 1)], g2_recv)
-    total = g2_ref[0]
-    for k in range(1, NR):
-        total = total + g2_ref[k]
-    total = total * (1.0 / NODES)
-    inverse = inverse_factor(jnp.concatenate([total[:, :K], total[:, K:]], axis=0))
-
-    def solve(b):
-        return dot(inverse, y_ref[b], ((1,), (0,)), lax.Precision.HIGHEST)
-
+
+    def share(buffer, place, value, peers, base):
+        buffer[place] = value
+        for i, peer in enumerate(peers):
+            remote(buffer.at[place], buffer.at[place], g_send.at[base + i], g_recv.at[base], **peer).start()
+
+    def collect(buffer, count, base):
+        wait_bytes(buffer.at[pl.ds(0, count - 1)], g_recv.at[base])
+        total = buffer[0]
+        for k in range(1, count):
+            total = total + buffer[k]
+        return total
+
+    share(g1_ref, x, gram_pack(gram), [dict(col=x_peer(k)) for k in (1, 3, 2)], 0)
+    if not last:
+        x_second(row, col, xs_ref, xc_ref, sems)
+    share(g2_ref, y, collect(g1_ref, 4, 0), [dict(col=y_peer(k)) for k in (1, 3, 2)], 3)
+    share(g3_ref, row, collect(g2_ref, 4, 3), [dict(row=row_peer(row, dz, flip)) for dz, flip in ROW_ORDER], 6)
+    if not last:
+        x_third(row, col, xs_ref, xc_ref, sems)
+    total = collect(g3_ref, NR, 6) * (1.0 / NODES)
     if last:
+        final = inverse_factor(gram_unpack(total))
         for b in range(0, 16, 2):
-            both = jnp.concatenate([solve(b), solve(b + 1)], axis=0).T
+            both = [dot(final, y_ref[b + i], ((1,), (0,)), lax.Precision.HIGHEST) for i in range(2)]
+            both = jnp.concatenate(both, axis=0).T
             z_ref[b * TILE:(b + 1) * TILE] = both[:, :K]
             z_ref[(b + 1) * TILE:(b + 2) * TILE] = both[:, K:]
     else:
-        for pair in range(4):
-            for part in range(2):
-                both = jnp.concatenate([solve(pair * 4 + part), solve(pair * 4 + 2 + part)], axis=0).T
-                xs_ref[part * 8:(part + 1) * 8, pair] = both.astype(BF).reshape(8, 16, TILE)
-        x_first(row, col, xs_ref, xc_ref, sems)
-        x_second(row, col, xs_ref, xc_ref, sems)
+        gram_ref[...] = total
         x_finish(row, col, xs_ref, xc_ref, sems)
+    for h in range(2):
+        for k in range(3):
+            wait_bytes(a1_ref.at[h, k], s1_send.at[h, k])
+            wait_bytes(a2_ref.at[h, k], s2_send.at[h, k])
     if first:
         wait_bytes(dg_ref.at[pl.ds(0, NC - 1)], dg_send)
-    wait_bytes(rs_ref.at[pl.ds(0, NC - 1)], rs_send)
-    wait_bytes(g1_ref.at[pl.ds(0, NC - 1)], g1_send)
-    wait_bytes(g2_ref.at[pl.ds(0, NR - 1)], g2_send)
-
-
-def normalize(first, last, part, degree):
+    for i in range(13):
+        wait_bytes(g1_ref.at[0], g_send.at[i])
+
+
+def normalize(first, last, part, degree, gram):
     dma = pltpu.SemaphoreType.DMA
+    half = (K // 2, TILE)
     out_shape, out_specs = [], []
     if last:
         out_shape.append(jax.ShapeDtypeStruct((16 * TILE, K), F32))
         out_specs.append(VMEM)
     else:
-        out_shape.append(jax.ShapeDtypeStruct((NR, NC, 4, 16, TILE), BF))
-        out_specs.append(ANY)
+        out_shape += [jax.ShapeDtypeStruct((NR, NC, 4, 16, TILE), BF), jax.ShapeDtypeStruct(half, F32)]
+        out_specs += [ANY, VMEM]
     if first:
         out_shape.append(jax.ShapeDtypeStruct((16, TILE), F32))
         out_specs.append(VMEM)
     scratch = [
-        pltpu.VMEM((16, K, TILE), F32), pltpu.VMEM((NC, 16, K, TILE), BF),
-        pltpu.VMEM((NC, K // 2, TILE), F32), pltpu.VMEM((NR, K // 2, TILE), F32),
-        dma, dma, dma((NC,)), dma, dma, dma, dma,
+        pltpu.VMEM((16, K, TILE), F32), pltpu.VMEM((2, 3, 4, 8, K, TILE), BF),
+        pltpu.VMEM((2, 3, 8, K, TILE), BF), pltpu.VMEM((2, 3, 8, K, TILE), BF),
+        pltpu.VMEM((4,) + half, F32), pltpu.VMEM((4,) + half, F32), pltpu.VMEM((NR,) + half, F32),
+        dma((2, 3)), dma((2, 3)), dma((2, 3)), dma((2, 3)), dma((13,)), dma((13,)),
     ]
     if first:
         scratch += [pltpu.VMEM((NC, 16, TILE), F32), dma, dma, dma]
     if not last:
-        scratch += [pltpu.VMEM((NC, 4, 16, TILE), BF), dma, dma, dma, dma, dma]
+        scratch += [pltpu.VMEM((NC, 4, 16, TILE), BF)] + x_sems()
+    args = [part.reshape(4, 4, 16, K, TILE), degree] + ([] if first else [gram])
     return pl.pallas_call(
         functools.partial(normalize_kernel, first, last),
         out_shape=out_shape,
-        in_specs=[ANY, ANY if first else VMEM],
+        in_specs=[VMEM, VMEM] + ([] if first else [VMEM]),
         out_specs=out_specs,
         scratch_shapes=scratch,
         compiler_params=pltpu.CompilerParams(
             collective_id=1 if first else (3 if last else 2), has_side_effects=True, vmem_limit_bytes=40 * MIB
         ),
         name="normalize",
-    )(part, degree)
+    )(*args)
 
 
 def block_index(block):
@@ -452,15 +510,15 @@
     cols = places[:, CAP:].reshape(DEV * CAP)
     own_rows = tile_rows % 256
     own_cols = block_index(tile_cols % 128)
-    degree = None
-    for iteration in range(ITERS):
-        first, last = iteration == 0, iteration == ITERS - 1
-        outs = product(first, rows, cols, own_rows, own_cols, xc, tiles, slots)
-        if first:
-            xc, degree = normalize(first, last, outs[0], outs[1])
-        else:
-            (xc,) = normalize(first, last, outs[0], degree)
-    return xc
+    part, degree = product(True, rows, cols, own_rows, own_cols, xc, tiles, slots)
+    xc, gram, degree = normalize(True, False, part, degree, None)
+    for iteration in range(1, ITERS):
+        (part,) = product(False, rows, cols, own_rows, own_cols, xc, tiles, slots)
+        last = iteration == ITERS - 1
+        outs = normalize(False, last, part, degree, gram)
+        if last:
+            return outs[0]
+        xc, gram = outs
 
 
 def solution(mesh):

time: 773 us -> 491 us (0.64)
  Pallas kernels: 750 us -> 467 us
    pallas_call x3, Pallas kernels: 476 us -> 195 us  [normalize(): pl.pallas_call(functools.partial(normalize_kernel, first, last), out_shap...]
where the time goes in v3:
time: 491 us; the launch traced here: 490 us
  Pallas kernels  467 us (95%)
  local copies, waits for them, and re-layouts  19.9 us (4%)
    pallas_call x3, Pallas kernels, normalize(): pl.pallas_call(functools.partial(normalize_kernel, first, last), out_shap...  195 us
    pallas_call x1, Pallas kernels, exchange(): pl.pallas_call(exchange_kernel, out_shape=(slots, slots, jax.ShapeDtypeSt...  185 us
    pallas_call x3, Pallas kernels, product(): pl.pallas_call(functools.partial(product_kernel, with_degree), grid=(DEV...  84.8 us
    unnamed x22, local copies, waits for them, and re-layouts  16.1 us

profile of v3, /device:TPU:1, one launch (start us, length us, event | category | flops | bytes accessed | tf_op | source)
XLA Modules:
  0.0 489.6 jit_solution(12960295526269940238)
XLA Ops:
  0.0 0.7 fusion.8
  0.7 0.2 convert_reduce_fusion
  0.9 0.1 select_reduce_fusion
  1.1 0.2 sub.45
  1.3 0.1 copy.25
  1.3 0.3 gt.10
  1.6 0.1 copy.29
  1.7 0.1 copy.35
  1.9 0.1 broadcast_in_dim.38.meta_ref
  2.0 0.0 copy-start.4
  2.0 2.8 copy-done.4
  4.8 0.0 copy-start.7
  4.8 2.5 pack.1
  7.3 0.0 copy-start
  7.3 4.7 copy-done
  12.0 0.0 copy-done.7
  12.0 0.3 copy.32
  12.3 0.5 copy.33
  12.9 1.0 reshape.56.xs_ref
  13.8 0.0 copy-start.8
  13.8 0.0 copy-start.9
  13.8 0.0 copy-start.1
  13.8 184.8 %exchange.1 = (bf16[8,16,400,128]{3,2,1,0:T(8,128)(2,1)}, bf16[8,16,400,128]{3,2,1,0:T(8,128)(2,1)}, bf16[8,16,4,16,128]{4,3,2,1,0:T(8,128)(2,1)}) custom-call(bf16[8,16,400,128]{3,2,1,0:T(8,128)(2,1)} %bitcast.12, bf16[16,4,16,128]{3,2,1,0:T(8,128)(2,1)} %reshape.56.xs_ref), custom_call_target="tpu_custom_call" | custom-call | tf_op jit(solution)/shard_map/exchange/pallas_call | solution.py:185
  198.6 1.0 slice_convert_fusion
  199.6 0.1 fusion.19
  199.7 0.2 reshape.58.rows_ref
  199.9 0.2 reshape.59.cols_ref
  200.1 0.0 copy-done.8
  200.1 0.0 copy-done.9
  200.2 0.0 copy-done.1
  200.2 0.0 copy-start.6
  200.2 1.6 copy-done.6
  201.8 29.6 %product.3 = (bf16[256,64,128]{2,1,0:T(8,128)(2,1)}, f32[256,128]{1,0:T(8,128)S(1)}) custom-call(s32[384]{0:T(512)S(1)} %reshape.58.rows_ref, s32[384]{0:T(512)S(1)} %reshape.59.cols_ref, s32[64]{0:T(128)S(1)} %get-tuple-element.31.own_rows_ref, s32[64]{0:T(128)S(1)} %get-tuple-element.32.own_cols_ref, bf16[128,4,16,128]{3,2,1,0:T(8,128)(2,1)S(1)} %bitcast.16, ...), custom_call_target="tpu_custom_call" | custom-call | flops 939524096 | bytes 14680064 | tf_op jit(solution)/shard_map/product/pallas_call | solution.py:284
  231.4 0.0 copy-start.5
  231.4 2.2 copy-done.5
  233.6 80.7 %normalize.3 = (bf16[8,16,4,16,128]{4,3,2,1,0:T(8,128)(2,1)S(1)}, f32[32,128]{1,0:T(8,128)S(1)}, f32[16,128]{1,0:T(8,128)S(1)}) custom-call(bf16[4,4,16,64,128]{4,3,2,1,0:T(8,128)(2,1)S(1)} %bitcast.15, f32[256,128]{1,0:T(8,128)S(1)} %get-tuple-element.17.degree_in_ref), custom_call_target="tpu_custom_call" | custom-call | tf_op jit(solution)/shard_map/normalize/pallas_call | solution.py:474
  314.2 27.6 %product.4 = bf16[256,64,128]{2,1,0:T(8,128)(2,1)} custom-call(s32[384]{0:T(512)S(1)} %reshape.58.rows_ref, s32[384]{0:T(512)S(1)} %reshape.59.cols_ref, s32[64]{0:T(128)S(1)} %get-tuple-element.31.own_rows_ref, s32[64]{0:T(128)S(1)} %get-tuple-element.32.own_cols_ref, bf16[128,4,16,128]{3,2,1,0:T(8,128)(2,1)S(1)} %bitcast.18, ...), custom_call_target="tpu_custom_call" | custom-call | flops 939524096 | bytes 14680064 | tf_op jit(solution)/shard_map/product/pallas_call | solution.py:284
  341.9 0.0 copy-start.3
  341.9 2.2 copy-done.3
  344.0 58.0 %normalize.4 = (bf16[8,16,4,16,128]{4,3,2,1,0:T(8,128)(2,1)S(1)}, f32[32,128]{1,0:T(8,128)S(1)}) custom-call(bf16[4,4,16,64,128]{4,3,2,1,0:T(8,128)(2,1)S(1)} %bitcast.14, f32[16,128]{1,0:T(8,128)S(1)} %get-tuple-element.19.degree_in_ref, f32[32,128]{1,0:T(8,128)S(1)} %get-tuple-element.20.rest_0_), custom_call_target="tpu_custom_call" | custom-call | tf_op jit(solution)/shard_map/normalize/pallas_call | solution.py:474
  402.0 27.6 %product.5 = bf16[256,64,128]{2,1,0:T(8,128)(2,1)} custom-call(s32[384]{0:T(512)S(1)} %reshape.58.rows_ref, s32[384]{0:T(512)S(1)} %reshape.59.cols_ref, s32[64]{0:T(128)S(1)} %get-tuple-element.31.own_rows_ref, s32[64]{0:T(128)S(1)} %get-tuple-element.32.own_cols_ref, bf16[128,4,16,128]{3,2,1,0:T(8,128)(2,1)S(1)} %bitcast.17, ...), custom_call_target="tpu_custom_call" | custom-call | flops 939524096 | bytes 14680064 | tf_op jit(solution)/shard_map/product/pallas_call | solution.py:284
  429.6 0.0 copy-start.2
  429.6 2.2 copy-done.2
  431.8 56.6 %normalize.5 = f32[2048,64]{1,0:T(8,128)S(1)} custom-call(bf16[4,4,16,64,128]{4,3,2,1,0:T(8,128)(2,1)S(1)} %bitcast.13, f32[16,128]{1,0:T(8,128)S(1)} %get-tuple-element.19.degree_in_ref, f32[32,128]{1,0:T(8,128)S(1)} %get-tuple-element.22.rest_0_), custom_call_target="tpu_custom_call" | custom-call | tf_op jit(solution)/shard_map/normalize/pallas_call | solution.py:474
  488.5 1.1 copy.34
  (7 shorter events, 0.1 us)
Async XLA Ops:
  2.0 2.8 copy-start.4
  4.8 7.3 %copy-start.7 = (bf16[2048,64]{0,1:T(8,128)(2,1)S(1)}, bf16[2048,64]{0,1:T(8,128)(2,1)}, u32[]{:S(2)}) copy-start(bf16[2048,64]{0,1:T(8,128)(2,1)} %param.7) | copy-start | bytes 786436
  7.3 4.7 copy-start
  13.8 186.3 %copy-start.8 = (s32[64]{0:T(128)S(1)}, s32[64]{0:T(128)}, u32[]{:S(2)}) copy-start(s32[64]{0:T(128)} %param.9) | copy-start | bytes 772
  13.8 186.3 %copy-start.9 = (s32[64]{0:T(128)S(1)}, s32[64]{0:T(128)}, u32[]{:S(2)}) copy-start(s32[64]{0:T(128)} %param.10) | copy-start | bytes 772
  13.8 186.4 %copy-start.1 = (bf16[64,128,128]{2,1,0:T(8,128)(2,1)S(1)}, bf16[64,128,128]{2,1,0:T(8,128)(2,1)}, u32[]{:S(2)}) copy-start(bf16[64,128,128]{2,1,0:T(8,128)(2,1)} %own_ref.5) | copy-start | bytes 6291460
  200.2 1.6 copy-start.6
  231.4 2.2 copy-start.5
  341.9 2.2 copy-start.3
  429.6 2.2 copy-start.2

commit v4 on v3

--- a/solution.py
+++ b/solution.py
@@ -15,12 +15,14 @@
 NC = 16
 DEV = NR * NC
 ROWS_BLK = 256
-SLOT_ROWS = CAP * TILE + 16
+SLOT_ROWS = CAP * TILE
+X_BLOCKS = 130
 OWN = 64
 NODES = 262144
 BF = jnp.bfloat16
 F32 = jnp.float32
 ANY = pl.BlockSpec(memory_space=pl.ANY)
+
 VMEM = pl.BlockSpec(memory_space=pltpu.VMEM)
 SMEM = pl.BlockSpec(memory_space=pltpu.SMEM)
 MIB = 1024 * 1024
@@ -29,32 +31,6 @@
 
 def dot(a, b, dims, precision=None):
     return lax.dot_general(a, b, (dims, ((), ())), precision=precision, preferred_element_type=F32)
-
-
-def pack_kernel(pick_ref, tiles_ref, meta_ref, out_ref):
-    step = pl.program_id(0)
-
-    def body(i, carry):
-        for slot in range(CAP):
-            tile = tiles_ref[pick_ref[(step * 8 + i) * CAP + slot]]
-            out_ref[i, slot * TILE:(slot + 1) * TILE] = tile
-        out_ref[i, CAP * TILE:] = meta_ref[i]
-        return carry
-
-    lax.fori_loop(0, 8, body, 0)
-
-
-def pack(pick, chg_tiles, meta):
-    return pl.pallas_call(
-        pack_kernel,
-        grid=(DEV // 8,),
-        out_shape=jax.ShapeDtypeStruct((DEV, SLOT_ROWS, TILE), BF),
-        in_specs=[SMEM, pl.BlockSpec(chg_tiles.shape, lambda i: (0, 0, 0)),
-                  pl.BlockSpec((8, 16, TILE), lambda i: (i, 0, 0))],
-        out_specs=pl.BlockSpec((8, SLOT_ROWS, TILE), lambda i: (i, 0, 0)),
-        compiler_params=pltpu.CompilerParams(vmem_limit_bytes=32 * MIB),
-        name="pack",
-    )(pick, chg_tiles, meta)
 
 
 def greet(row, col):
@@ -117,15 +93,26 @@
         remote(xc.at[source], xc.at[source], sems["xb_send"].at[4 + i], sems["xb_recv"].at[source], row=row_peer(row, 0, 1)).start()
 
 
-def x_finish(row, col, xs, xc, sems):
+def x_finish(row, col, xs, xc, xt, sems):
+    xt[X_BLOCKS - 2:] = jnp.zeros((2, K, TILE), BF)
     for dz in range(4):
+        turn(row_peer(row, dz), xc, xt)
+    for dz in (0, 1, 3, 2):
         source = row_peer(row, dz, 1)
         wait_bytes(xc.at[source], sems["xb_recv"].at[source])
+        turn(source, xc, xt)
     wait_bytes(xs.at[pl.ds(0, NC - 1)], sems["xa_send"])
     for i in range(7):
         wait_bytes(xc.at[row], sems["xb_send"].at[i])
 
 
+def turn(source, xc, xt):
+    for part in range(2):
+        for pair in range(4):
+            block = xc[source, part * 8:(part + 1) * 8, pair].reshape(TILE, TILE)
+            xt[pl.ds((pair * 16 + source * 2 + part) * 2, 2)] = block.T.reshape(2, K, TILE)
+
+
 X_SEMS = ("x_own", "xa_send", "xa_recv", "xb_send", "xb_recv")
 
 
@@ -134,43 +121,73 @@
     return [dma, dma, dma, dma((7,)), dma((NR,))]
 
 
-def exchange_kernel(send_ref, xs_ref, recv_ref, mid_ref, xc_ref,
-                    x_own, xa_send, xa_recv, xb_send, xb_recv,
-                    a_own, a_send, a_recv, b_send, b_recv):
+def exchange_kernel(pick_ref, tiles_ref, own_ref, meta_ref, xs_ref,
+                    recv_ref, mid_ref, own_out_ref, places_ref, xt_ref,
+                    send_ref, xc_ref, meta_mid_ref, meta_next_ref, *sem_refs):
+    sems = dict(zip(X_SEMS, sem_refs))
+    a_send, a_recv, b_send, b_recv, m_send, m_recv, n_send, n_recv, own_sem = sem_refs[len(X_SEMS):]
     row = lax.axis_index("row")
     col = lax.axis_index("col")
-    sems = dict(x_own=x_own, xa_send=xa_send, xa_recv=xa_recv, xb_send=xb_send, xb_recv=xb_recv)
     greet(row, col)
     x_first(row, col, xs_ref, xc_ref, sems)
-    plane, core = row // 2, lax.rem(row, 2)
-    targets = [
-        lax.rem(plane + dz, 4) * 2 + (lax.rem(core + flip, 2)) for dz, flip in ROW_ORDER
-    ]
-
-    def first(step, target, dst_ref):
-        pltpu.make_async_copy(send_ref.at[target, col], dst_ref.at[target, col], a_own.at[step]).start()
-
-        def send(k, carry):
+    targets = [row_peer(row, dz, flip) for dz, flip in ROW_ORDER] + [row]
+
+    def send_meta(k, carry):
+        peer = col_peer(col, k)
+        remote(meta_ref.at[peer], meta_mid_ref.at[col], m_send, m_recv, col=peer).start()
+        return carry
+
+    lax.fori_loop(1, NC, send_meta, 0)
+    meta_mid_ref[col] = meta_ref[col]
+
+    def first(step):
+        target = targets[step]
+        dst_ref = mid_ref if step < NR - 1 else recv_ref
+
+        def fill(k, carry):
             peer = col_peer(col, k)
-            remote(send_ref.at[target, peer], dst_ref.at[target, col], a_send.at[step], a_recv.at[step], col=peer).start()
+            for slot in range(CAP):
+                send_ref[target, peer, slot * TILE:(slot + 1) * TILE] = tiles_ref[pick_ref[(target * NC + peer) * CAP + slot]]
+
+            @pl.when(k > 0)
+            def _():
+                remote(send_ref.at[target, peer], dst_ref.at[target, col], a_send.at[step], a_recv.at[step], col=peer).start()
+
             return carry
 
-        lax.fori_loop(1, NC, send, 0)
-
-    first(0, targets[0], mid_ref)
+        lax.fori_loop(0, NC, fill, 0)
+        pltpu.make_async_copy(send_ref.at[target, col], dst_ref.at[target, col], own_sem.at[step]).start()
+
+    first(0)
     x_second(row, col, xs_ref, xc_ref, sems)
-    for step in range(1, NR - 1):
-        first(step, targets[step], mid_ref)
-    first(NR - 1, row, recv_ref)
+    for step in range(1, NR):
+        first(step)
+    wait_bytes(meta_mid_ref.at[pl.ds(0, NC - 1)], m_recv)
+    for c in range(NC):
+        for r in range(NR):
+            meta_next_ref[r, c:c + 1] = meta_mid_ref[c, r:r + 1]
+    for step in range(NR - 1):
+        remote(meta_next_ref.at[targets[step]], places_ref.at[row], n_send, n_recv, row=targets[step]).start()
+    places_ref[row] = meta_next_ref[row]
     x_third(row, col, xs_ref, xc_ref, sems)
+
+    def flip_own(i, carry):
+        for u in range(4):
+            own_out_ref[i * 4 + u] = own_ref[i * 4 + u].T
+        return carry
+
+    lax.fori_loop(0, OWN // 4, flip_own, 0)
     for step in range(NR - 1):
         target = targets[step]
         wait_bytes(mid_ref.at[target, pl.ds(0, NC - 1)], a_recv.at[step])
-        pltpu.make_async_copy(send_ref.at[target, col], mid_ref.at[target, col], a_own.at[step]).wait()
+        pltpu.make_async_copy(send_ref.at[target, col], mid_ref.at[target, col], own_sem.at[step]).wait()
         remote(mid_ref.at[target], recv_ref.at[row], b_send.at[step], b_recv.at[row], row=target).start()
+    x_finish(row, col, xs_ref, xc_ref, xt_ref, sems)
     wait_bytes(recv_ref.at[row, pl.ds(0, NC - 1)], a_recv.at[NR - 1])
-    pltpu.make_async_copy(send_ref.at[row, col], recv_ref.at[row, col], a_own.at[NR - 1]).wait()
-    x_finish(row, col, xs_ref, xc_ref, sems)
+    pltpu.make_async_copy(send_ref.at[row, col], recv_ref.at[row, col], own_sem.at[NR - 1]).wait()
+    wait_bytes(meta_mid_ref.at[pl.ds(0, NC - 1)], m_send)
+    wait_bytes(places_ref.at[pl.ds(0, NR - 1)], n_send)
+    wait_bytes(places_ref.at[pl.ds(0, NR - 1)], n_recv)
     for step in range(NR):
         wait_bytes(send_ref.at[0, pl.ds(0, NC - 1)], a_send.at[step])
     for step in range(NR - 1):
@@ -179,120 +196,96 @@
         wait_bytes(recv_ref.at[source], b_recv.at[source])
 
 
-def exchange(send, xs):
+def exchange(pick, chg_tiles, own, meta, xs):
     dma = pltpu.SemaphoreType.DMA
-    slots = jax.ShapeDtypeStruct((NR, NC, SLOT_ROWS, TILE), BF)
-    recv, _, xc = pl.pallas_call(
+    slots = (NR, NC, SLOT_ROWS, TILE)
+    recv, _, own, places, xt = pl.pallas_call(
         exchange_kernel,
-        out_shape=(slots, slots, jax.ShapeDtypeStruct((NR, NC, 4, 16, TILE), BF)),
-        in_specs=[ANY, ANY],
-        out_specs=(ANY, ANY, ANY),
-        scratch_shapes=x_sems() + [dma((NR,)), dma((NR,)), dma((NR,)), dma((NR,)), dma((NR,))],
-        compiler_params=pltpu.CompilerParams(collective_id=0, has_side_effects=True),
+        out_shape=(jax.ShapeDtypeStruct(slots, BF), jax.ShapeDtypeStruct(slots, BF), pltpu.VMEM((OWN, TILE, TILE), BF),
+                   jax.ShapeDtypeStruct((NR, NC, TILE), F32), pltpu.VMEM((X_BLOCKS, K, TILE), BF)),
+        in_specs=[SMEM, VMEM, VMEM, VMEM, VMEM],
+        out_specs=(ANY, ANY, VMEM, VMEM, VMEM),
+        scratch_shapes=[
+            pltpu.VMEM(slots, BF), pltpu.VMEM((NR, NC, 4, 16, TILE), BF),
+            pltpu.VMEM((NC, NR, TILE), F32), pltpu.VMEM((NR, NC, TILE), F32),
+        ] + x_sems() + [dma((NR,)), dma((NR,)), dma((NR,)), dma((NR,)), dma, dma, dma, dma, dma((NR,))],
+        compiler_params=pltpu.CompilerParams(collective_id=0, has_side_effects=True, vmem_limit_bytes=42 * MIB),
         name="exchange",
-    )(send.reshape(NR, NC, SLOT_ROWS, TILE), xs)
-    return recv, xc
-
-
-def product_kernel(with_degree, rows_ref, cols_ref, own_rows_ref, own_cols_ref, x_ref, own_ref, slots_ref, *rest):
+    )(pick, chg_tiles, own, meta, xs)
+    return recv, own, places, xt
+
+
+def product_kernel(with_degree, rows_ref, cols_ref, own_rows_ref, own_cols_ref, xt_ref, own_ref, slots_in_ref, acc_ref, *rest):
+    slots_ref, slot_sem = rest[-2:]
+    loads = [
+        pltpu.make_async_copy(slots_in_ref.at[pl.ds(i * 16, 16)], slots_ref.at[pl.ds(i * 16, 16)], slot_sem.at[i])
+        for i in range(DEV // 16)
+    ]
+    for load in loads:
+        load.start()
+    ones = jnp.ones((8, TILE), BF)
+    plain = ((1,), (0,))
     if with_degree:
-        part_ref, degree_out_ref, xt_ref, acc_ref, degree_ref = rest
-    else:
-        part_ref, xt_ref, acc_ref = rest
-        degree_ref = None
-    step = pl.program_id(0)
-    ones = jnp.ones((8, TILE), BF)
-
-    def run(terms):
-        products = []
-        for load, _, x_index, dims, valid in terms:
-            tile = load()
-            value = dot(xt_ref[x_index], tile, dims)
-            sums = None
-            if with_degree:
-                scale = ones if valid is None else jnp.where(valid, ones, jnp.zeros_like(ones))
-                sums = dot(scale, jnp.abs(tile), dims)[0:1]
-            products.append((value, sums))
-        for (_, target, _, _, _), (value, sums) in zip(terms, products):
-            acc_ref[target] += value
-            if with_degree:
-                degree_ref[target] += sums
-
-    @pl.when(step == 0)
-    def _():
-        acc_ref[...] = jnp.zeros_like(acc_ref)
+        degree_out_ref, degree_ref = rest[:2]
+        degree_ref[...] = jnp.zeros_like(degree_ref)
+
+    def clear(i, carry):
+        acc_ref[pl.ds(i * 8, 8)] = jnp.zeros((8, K, TILE), F32)
+        return carry
+
+    lax.fori_loop(0, ROWS_BLK // 8, clear, 0)
+
+    def run(tiles, rows, cols):
+        values = [dot(xt_ref[col], tile, plain) for tile, col in zip(tiles, cols)]
+        sums = []
         if with_degree:
-            degree_ref[...] = jnp.zeros_like(degree_ref)
-
-        def turn(q, carry):
-            pair, j = q // 16, lax.rem(q, 16)
-            block = x_ref[pl.ds(j * 8, 8), pair].reshape(TILE, TILE)
-            xt_ref[pl.ds(q * 2, 2)] = block.T.reshape(2, K, TILE)
-            return carry
-
-        lax.fori_loop(0, 64, turn, 0)
-        xt_ref[pl.ds(128, 2)] = jnp.zeros((2, K, TILE), BF)
-
-        def own(i, carry):
-            run([
-                (functools.partial(lambda n: own_ref[n], i * 4 + u), own_rows_ref[i * 4 + u],
-                 own_cols_ref[i * 4 + u], ((1,), (1,)), None)
-                for u in range(4)
-            ])
-            return carry
-
-        lax.fori_loop(0, OWN // 4, own, 0)
+            sums = [
+                dot(jnp.where(col < 128, ones, jnp.zeros_like(ones)), jnp.abs(tile), plain)[0:1]
+                for tile, col in zip(tiles, cols)
+            ]
+        for row, value in zip(rows, values):
+            acc_ref[row] += value
+        for row, value in zip(rows, sums):
+            degree_ref[row] += value
+
+    def own(i, carry):
+        places = [i * 4 + u for u in range(4)]
+        run([own_ref[n] for n in places], [own_rows_ref[n] for n in places], [own_cols_ref[n] for n in places])
+        return carry
 
     def taken(i, carry):
-        terms = []
         for u in range(2):
-            for slot in range(CAP):
-                source = i * 2 + u
-                n = (step * 8 + source) * CAP + slot
-                x_index = cols_ref[n]
-                terms.append((
-                    functools.partial(lambda s, k: slots_ref[s, pl.ds(k * TILE, TILE)], source, slot),
-                    rows_ref[n], x_index, ((1,), (0,)), x_index < 128,
-                ))
-        run(terms)
-        return carry
-
-    lax.fori_loop(0, 4, taken, 0)
-
-    @pl.when(step == pl.num_programs(0) - 1)
-    def _():
-        def flush(i, carry):
-            part_ref[pl.ds(i * 8, 8)] = acc_ref[pl.ds(i * 8, 8)].astype(BF)
-            return carry
-
-        lax.fori_loop(0, ROWS_BLK // 8, flush, 0)
-        if with_degree:
-            degree_out_ref[...] = degree_ref[...].reshape(ROWS_BLK, TILE)
-
-
-def product(with_degree, rows, cols, own_rows, own_cols, xc, own, slots):
-    whole = lambda shape: pl.BlockSpec(shape, lambda i: (0,) * len(shape))
-    out_shape = [jax.ShapeDtypeStruct((ROWS_BLK, K, TILE), BF)]
-    out_specs = [whole((ROWS_BLK, K, TILE))]
+            source = i * 2 + u
+            places = [source * CAP + slot for slot in range(CAP)]
+            run([slots_ref[source, slot * TILE:(slot + 1) * TILE] for slot in range(CAP)],
+                [rows_ref[n] for n in places], [cols_ref[n] for n in places])
+        return carry
+
+    lax.fori_loop(0, OWN // 4, own, 0)
+    for i, load in enumerate(loads):
+        load.wait()
+        lax.fori_loop(i * 8, i * 8 + 8, taken, 0)
+    if with_degree:
+        degree_out_ref[...] = degree_ref[...].reshape(ROWS_BLK, TILE)
+
+
+def product(with_degree, rows, cols, own_rows, own_cols, xt, own, slots):
+    out_shape = [pltpu.VMEM((ROWS_BLK, K, TILE), F32)]
     if with_degree:
         out_shape.append(jax.ShapeDtypeStruct((ROWS_BLK, TILE), F32))
-        out_specs.append(whole((ROWS_BLK, TILE)))
-    scratch = [pltpu.VMEM((130, K, TILE), BF), pltpu.VMEM((ROWS_BLK, K, TILE), F32)]
-    if with_degree:
-        scratch.append(pltpu.VMEM((ROWS_BLK, 1, TILE), F32))
     terms = DEV * CAP + OWN
     return pl.pallas_call(
         functools.partial(product_kernel, with_degree),
-        grid=(DEV // 8,),
         out_shape=out_shape,
-        in_specs=[SMEM, SMEM, SMEM, SMEM, whole((DEV, 4, 16, TILE)), whole((OWN, TILE, TILE)),
-                  pl.BlockSpec((8, SLOT_ROWS, TILE), lambda i: (i, 0, 0))],
-        out_specs=out_specs,
-        scratch_shapes=scratch,
-        compiler_params=pltpu.CompilerParams(vmem_limit_bytes=48 * MIB),
+        in_specs=[SMEM, SMEM, SMEM, SMEM, VMEM, VMEM, ANY],
+        out_specs=[VMEM] * len(out_shape),
+        scratch_shapes=([pltpu.VMEM((ROWS_BLK, 1, TILE), F32)] if with_degree else []) + [
+            pltpu.VMEM((DEV, SLOT_ROWS, TILE), BF), pltpu.SemaphoreType.DMA((DEV // 16,)),
+        ],
+        compiler_params=pltpu.CompilerParams(vmem_limit_bytes=40 * MIB),
         cost_estimate=pl.CostEstimate(flops=terms * 2 * K * TILE * TILE, bytes_accessed=terms * TILE * TILE * 2, transcendentals=0),
         name="product",
-    )(rows, cols, own_rows, own_cols, xc.reshape(DEV, 4, 16, TILE), own, slots.reshape(DEV, SLOT_ROWS, TILE))
+    )(rows, cols, own_rows, own_cols, xt, own, slots.reshape(DEV, SLOT_ROWS, TILE))
 
 
 def inverse_factor(gram):
@@ -323,14 +316,14 @@
     if last:
         (z_ref,) = take(1)
     else:
-        xc_ref, gram_ref = take(2)
+        xt_ref, gram_ref = take(2)
     degree_ref = rest.pop(0) if first else degree_in_ref
-    y_ref, a1_ref, r1_ref, a2_ref, g1_ref, g2_ref, g3_ref = take(7)
+    y_ref, s1_ref, a1_ref, r1_ref, a2_ref, g1_ref, g2_ref, g3_ref = take(8)
     s1_send, s1_recv, s2_send, s2_recv, g_send, g_recv = take(6)
     if first:
         dg_ref, dg_own, dg_send, dg_recv = take(4)
     if not last:
-        xs_ref = rest.pop(0)
+        xs_ref, xc_ref = take(2)
         sems = dict(zip(X_SEMS, rest))
     row = lax.axis_index("row")
     col = lax.axis_index("col")
@@ -340,10 +333,17 @@
     greet(row, col)
 
     for k in (1, 3, 2):
-        remote(part_ref.at[lax.rem(x + k, 4), :, pl.ds(0, 8)], a1_ref.at[0, k - 1],
-               s1_send.at[0, k - 1], s1_recv.at[0, k - 1], col=x_peer(k)).start()
-        remote(part_ref.at[:, lax.rem(y + k, 4), pl.ds(8, 8)], a1_ref.at[1, k - 1],
-               s1_send.at[1, k - 1], s1_recv.at[1, k - 1], col=y_peer(k)).start()
+        for h in range(2):
+            target = lax.rem((y if h else x) + k, 4)
+
+            def narrow(other, carry):
+                chunk = part_ref[other, target, 8:16] if h else part_ref[target, other, 0:8]
+                s1_ref[h, k - 1, other] = chunk.astype(BF)
+                return carry
+
+            lax.fori_loop(0, 4, narrow, 0)
+            remote(s1_ref.at[h, k - 1], a1_ref.at[h, k - 1], s1_send.at[h, k - 1], s1_recv.at[h, k - 1],
+                   col=y_peer(k) if h else x_peer(k)).start()
     if first:
         pltpu.make_async_copy(degree_in_ref.at[pl.ds(col * 16, 16)], dg_ref.at[col], dg_own).start()
 
@@ -363,7 +363,7 @@
 
             def add(b, carry):
                 mine = part_ref[target, y, 8 + b] if h else part_ref[x, target, b]
-                value = mine.astype(F32)
+                value = mine
                 for source in range(3):
                     value = value + a1_ref[h, source, target, b].astype(F32)
                 if k:
@@ -436,7 +436,7 @@
             z_ref[(b + 1) * TILE:(b + 2) * TILE] = both[:, K:]
     else:
         gram_ref[...] = total
-        x_finish(row, col, xs_ref, xc_ref, sems)
+        x_finish(row, col, xs_ref, xc_ref, xt_ref, sems)
     for h in range(2):
         for k in range(3):
             wait_bytes(a1_ref.at[h, k], s1_send.at[h, k])
@@ -455,13 +455,13 @@
         out_shape.append(jax.ShapeDtypeStruct((16 * TILE, K), F32))
         out_specs.append(VMEM)
     else:
-        out_shape += [jax.ShapeDtypeStruct((NR, NC, 4, 16, TILE), BF), jax.ShapeDtypeStruct(half, F32)]
-        out_specs += [ANY, VMEM]
+        out_shape += [pltpu.VMEM((X_BLOCKS, K, TILE), BF), jax.ShapeDtypeStruct(half, F32)]
+        out_specs += [VMEM, VMEM]
     if first:
         out_shape.append(jax.ShapeDtypeStruct((16, TILE), F32))
         out_specs.append(VMEM)
     scratch = [
-        pltpu.VMEM((16, K, TILE), F32), pltpu.VMEM((2, 3, 4, 8, K, TILE), BF),
+        pltpu.VMEM((16, K, TILE), F32), pltpu.VMEM((2, 3, 4, 8, K, TILE), BF), pltpu.VMEM((2, 3, 4, 8, K, TILE), BF),
         pltpu.VMEM((2, 3, 8, K, TILE), BF), pltpu.VMEM((2, 3, 8, K, TILE), BF),
         pltpu.VMEM((4,) + half, F32), pltpu.VMEM((4,) + half, F32), pltpu.VMEM((NR,) + half, F32),
         dma((2, 3)), dma((2, 3)), dma((2, 3)), dma((2, 3)), dma((13,)), dma((13,)),
@@ -469,7 +469,7 @@
     if first:
         scratch += [pltpu.VMEM((NC, 16, TILE), F32), dma, dma, dma]
     if not last:
-        scratch += [pltpu.VMEM((NC, 4, 16, TILE), BF)] + x_sems()
+        scratch += [pltpu.VMEM((NC, 4, 16, TILE), BF), pltpu.VMEM((NR, NC, 4, 16, TILE), BF)] + x_sems()
     args = [part.reshape(4, 4, 16, K, TILE), degree] + ([] if first else [gram])
     return pl.pallas_call(
         functools.partial(normalize_kernel, first, last),
@@ -478,7 +478,7 @@
         out_specs=out_specs,
         scratch_shapes=scratch,
         compiler_params=pltpu.CompilerParams(
-            collective_id=1 if first else (3 if last else 2), has_side_effects=True, vmem_limit_bytes=40 * MIB
+            collective_id=1 if first else (3 if last else 2), has_side_effects=True, vmem_limit_bytes=16 * MIB
         ),
         name="normalize",
     )(*args)
@@ -500,12 +500,11 @@
     code = jnp.sum(jnp.where(hit, (1 + chg_cols % 256 * 128 + block_index(chg_rows % 128))[None, :], 0), axis=1)
     slot_rows = jnp.where(code > 0, (code - 1) // 128, 0).reshape(DEV, CAP)
     slot_cols = jnp.where(code > 0, (code - 1) % 128, 128).reshape(DEV, CAP)
-    meta = jnp.pad(jnp.concatenate([slot_rows, slot_cols], axis=1).astype(BF), ((0, 0), (0, TILE - 2 * CAP)))
-    meta = jnp.broadcast_to(meta[:, None, :], (DEV, 16, TILE))
-    send = pack(pick, chg_tiles, meta)
+    meta = jnp.concatenate([slot_rows, slot_cols], axis=1).reshape(NR, NC, 2 * CAP).transpose(1, 0, 2)
+    meta = jnp.pad(meta.astype(F32), ((0, 0), (0, 0), (0, TILE - 2 * CAP)))
     xs = embed.reshape(4, 2, NC, 16, K).transpose(2, 0, 3, 1, 4).reshape(NC, 4, 16, TILE)
-    slots, xc = exchange(send, xs)
-    places = slots.reshape(DEV, SLOT_ROWS, TILE)[:, CAP * TILE, :2 * CAP].astype(jnp.int32)
+    slots, tiles, places, xc = exchange(pick, chg_tiles, tiles, meta, xs)
+    places = places.reshape(DEV, TILE)[:, :2 * CAP].astype(jnp.int32)
     rows = places[:, :CAP].reshape(DEV * CAP)
     cols = places[:, CAP:].reshape(DEV * CAP)
     own_rows = tile_rows % 256

time: 491 us -> 437 us (0.89)
  Pallas kernels: 467 us -> 426 us
  local copies, waits for them, and re-layouts: 19.9 us -> 8.57 us
    pallas_call x5 -> x4, Pallas kernels: 272 us -> 233 us  [the longest x1 181 us: exchange(): pl.pallas_call(exchange_kernel, out_shape=(jax.ShapeDtypeStruct(slots, BF...]
    unnamed x22 -> x11, local copies, waits for them, and re-layouts: 16.1 us -> 5.74 us
where the time goes in v4:
time: 437 us; the launch traced here: 436 us
  Pallas kernels  426 us (97%)
  local copies, waits for them, and re-layouts  8.57 us (2%)
    pallas_call x3, Pallas kernels, normalize(): pl.pallas_call(functools.partial(normalize_kernel, first, last), out_shap...  193 us
    pallas_call x1, Pallas kernels, exchange(): pl.pallas_call(exchange_kernel, out_shape=(jax.ShapeDtypeStruct(slots, BF...  181 us
    pallas_call x3, Pallas kernels, product(): pl.pallas_call(functools.partial(product_kernel, with_degree), out_shape=...  52.2 us

profile of v4, /device:TPU:1, one launch (start us, length us, event | category | flops | bytes accessed | tf_op | source)
XLA Modules:
  0.0 436.3 jit_solution(6450131005632114318)
XLA Ops:
  0.0 0.0 copy-start.4
  0.0 0.0 copy-start.3
  0.0 0.7 fusion.8
  0.8 0.2 convert_reduce_fusion
  0.9 0.1 select_reduce_fusion
  1.1 0.2 sub.45
  1.3 0.2 gt.12
  1.6 0.1 fusion.1
  1.6 0.1 fusion.3
  1.7 1.2 copy.31
  3.0 0.5 copy.32
  3.5 0.2 reshape.47.xs_ref
  3.8 0.0 copy-start.2
  3.8 1.6 copy-done.2
  5.4 181.2 %exchange.1 = (bf16[8,16,384,128]{3,2,1,0:T(8,128)(2,1)}, bf16[8,16,384,128]{3,2,1,0:T(8,128)(2,1)}, bf16[64,128,128]{2,1,0:T(8,128)(2,1)S(1)}, f32[8,16,128]{2,1,0:T(8,128)S(1)}, bf16[130,64,128]{2,1,0:T(8,128)(2,1)S(1)}) custom-call(s32[384]{0:T(512)S(1)} %get-tuple-element.28.pick_ref, bf16[192,128,128]{2,1,0:T(8,128)(2,1)} %tiles_ref.1, ...), custom_call_target="tpu_custom_call" | custom-call | tf_op jit(solution)/shard_map/exchange/pallas_call | solution.py:202
  186.5 0.0 copy-start
  186.5 1.3 copy-done
  187.9 0.1 fusion.19
  188.0 0.2 reshape.49.rows_ref
  188.2 0.2 reshape.50.cols_ref
  188.4 0.0 copy-done.4
  188.4 0.0 copy-done.3
  188.4 0.0 copy-start.1
  188.4 1.6 copy-done.1
  190.0 19.6 %product.3 = (f32[256,64,128]{2,1,0:T(8,128)S(1)}, f32[256,128]{1,0:T(8,128)S(1)}) custom-call(s32[384]{0:T(512)S(1)} %reshape.49.rows_ref, s32[384]{0:T(512)S(1)} %reshape.50.cols_ref, s32[64]{0:T(128)S(1)} %get-tuple-element.35.own_rows_ref, s32[64]{0:T(128)S(1)} %get-tuple-element.36.own_cols_ref, bf16[130,64,128]{2,1,0:T(8,128)(2,1)S(1)} %copy-done.1, ...), custom_call_target="tpu_custom_call" | custom-call | flops 939524096 | bytes 14680064 | tf_op jit(solution)/shard_map/product/pallas_call | solution.py:277
  209.7 76.6 %normalize.3 = (bf16[130,64,128]{2,1,0:T(8,128)(2,1)S(1)}, f32[32,128]{1,0:T(8,128)S(1)}, f32[16,128]{1,0:T(8,128)S(1)}) custom-call(f32[4,4,16,64,128]{4,3,2,1,0:T(8,128)S(1)} %bitcast.12, f32[256,128]{1,0:T(8,128)S(1)} %get-tuple-element.21.degree_in_ref), custom_call_target="tpu_custom_call" | custom-call | tf_op jit(solution)/shard_map/normalize/pallas_call | solution.py:474
  286.2 16.3 %product.4 = f32[256,64,128]{2,1,0:T(8,128)S(1)} custom-call(s32[384]{0:T(512)S(1)} %reshape.49.rows_ref, s32[384]{0:T(512)S(1)} %reshape.50.cols_ref, s32[64]{0:T(128)S(1)} %get-tuple-element.35.own_rows_ref, s32[64]{0:T(128)S(1)} %get-tuple-element.36.own_cols_ref, bf16[130,64,128]{2,1,0:T(8,128)(2,1)S(1)} %get-tuple-element.22.xt_ref, ...), custom_call_target="tpu_custom_call" | custom-call | flops 939524096 | bytes 14680064 | tf_op jit(solution)/shard_map/product/pallas_call | solution.py:277
  302.6 59.7 %normalize.4 = (bf16[130,64,128]{2,1,0:T(8,128)(2,1)S(1)}, f32[32,128]{1,0:T(8,128)S(1)}) custom-call(f32[4,4,16,64,128]{4,3,2,1,0:T(8,128)S(1)} %bitcast.11, f32[16,128]{1,0:T(8,128)S(1)} %get-tuple-element.23.degree_in_ref, f32[32,128]{1,0:T(8,128)S(1)} %get-tuple-element.24.rest_0_), custom_call_target="tpu_custom_call" | custom-call | tf_op jit(solution)/shard_map/normalize/pallas_call | solution.py:474
  362.3 16.3 %product.5 = f32[256,64,128]{2,1,0:T(8,128)S(1)} custom-call(s32[384]{0:T(512)S(1)} %reshape.49.rows_ref, s32[384]{0:T(512)S(1)} %reshape.50.cols_ref, s32[64]{0:T(128)S(1)} %get-tuple-element.35.own_rows_ref, s32[64]{0:T(128)S(1)} %get-tuple-element.36.own_cols_ref, bf16[130,64,128]{2,1,0:T(8,128)(2,1)S(1)} %get-tuple-element.25.xt_ref, ...), custom_call_target="tpu_custom_call" | custom-call | flops 939524096 | bytes 14680064 | tf_op jit(solution)/shard_map/product/pallas_call | solution.py:277
  378.6 56.6 %normalize.5 = f32[2048,64]{1,0:T(8,128)S(1)} custom-call(f32[4,4,16,64,128]{4,3,2,1,0:T(8,128)S(1)} %bitcast.10, f32[16,128]{1,0:T(8,128)S(1)} %get-tuple-element.23.degree_in_ref, f32[32,128]{1,0:T(8,128)S(1)} %get-tuple-element.26.rest_0_), custom_call_target="tpu_custom_call" | custom-call | tf_op jit(solution)/shard_map/normalize/pallas_call | solution.py:474
  435.2 1.1 copy.33
  (6 shorter events, 0.1 us)
Async XLA Ops:
  0.0 188.4 %copy-start.4 = (s32[64]{0:T(128)S(1)}, s32[64]{0:T(128)}, u32[]{:S(2)}) copy-start(s32[64]{0:T(128)} %param.10) | copy-start | bytes 772
  0.0 188.4 %copy-start.3 = (s32[64]{0:T(128)S(1)}, s32[64]{0:T(128)}, u32[]{:S(2)}) copy-start(s32[64]{0:T(128)} %param.9) | copy-start | bytes 772
  3.8 1.6 copy-start.2
  186.5 1.3 copy-start
  188.4 1.6 copy-start.1

commit v5 on v4

--- a/solution.py
+++ b/solution.py
@@ -249,22 +249,21 @@
             degree_ref[row] += value
 
     def own(i, carry):
-        places = [i * 4 + u for u in range(4)]
+        places = [i * 16 + u for u in range(16)]
         run([own_ref[n] for n in places], [own_rows_ref[n] for n in places], [own_cols_ref[n] for n in places])
         return carry
 
     def taken(i, carry):
-        for u in range(2):
-            source = i * 2 + u
-            places = [source * CAP + slot for slot in range(CAP)]
-            run([slots_ref[source, slot * TILE:(slot + 1) * TILE] for slot in range(CAP)],
-                [rows_ref[n] for n in places], [cols_ref[n] for n in places])
-        return carry
-
-    lax.fori_loop(0, OWN // 4, own, 0)
+        sources = [i * 16 + u for u in range(16)]
+        places = [source * CAP + slot for source in sources for slot in range(CAP)]
+        run([slots_ref[source, slot * TILE:(slot + 1) * TILE] for source in sources for slot in range(CAP)],
+            [rows_ref[n] for n in places], [cols_ref[n] for n in places])
+        return carry
+
+    lax.fori_loop(0, OWN // 16, own, 0)
     for i, load in enumerate(loads):
         load.wait()
-        lax.fori_loop(i * 8, i * 8 + 8, taken, 0)
+        lax.fori_loop(i, i + 1, taken, 0)
     if with_degree:
         degree_out_ref[...] = degree_ref[...].reshape(ROWS_BLK, TILE)
 
@@ -318,7 +317,7 @@
     else:
         xt_ref, gram_ref = take(2)
     degree_ref = rest.pop(0) if first else degree_in_ref
-    y_ref, s1_ref, a1_ref, r1_ref, a2_ref, g1_ref, g2_ref, g3_ref = take(8)
+    y_ref, s1_ref, a1_ref, s2_ref, a2_ref, v_ref, g1_ref, g2_ref, g3_ref = take(9)
     s1_send, s1_recv, s2_send, s2_recv, g_send, g_recv = take(6)
     if first:
         dg_ref, dg_own, dg_send, dg_recv = take(4)
@@ -332,18 +331,33 @@
     y_peer = lambda k: x * 4 + lax.rem(y + k, 4)
     greet(row, col)
 
-    for k in (1, 3, 2):
+    ways = ((1, 3) * 3)
+
+    def ring(stage, h, message):
+        along_x = (h == 0) == (stage == 1)
+        k = ways[message]
+        src, dst, send_sem, recv_sem = (s1_ref, a1_ref, s1_send, s1_recv) if stage == 1 else (s2_ref, a2_ref, s2_send, s2_recv)
+        return remote(src.at[h, message], dst.at[h, message], send_sem.at[h, message], recv_sem.at[h, message],
+                      col=x_peer(k) if along_x else y_peer(k))
+
+    def arrived(stage, h, message):
+        dst, recv_sem = (a1_ref, s1_recv) if stage == 1 else (a2_ref, s2_recv)
+        wait_bytes(dst.at[h, message], recv_sem.at[h, message])
+
+    def mine(h, k, other, half):
+        target = lax.rem((y if h else x) + k, 4)
+        blocks = slice(h * 8 + half * 4, h * 8 + half * 4 + 4)
+        return part_ref[other, target, blocks] if h else part_ref[target, other, blocks]
+
+    plan = ((0, 2, 0), (1, 2, 1), (2, 1, 1), (3, 3, 0))
+    for message, k, half in plan:
         for h in range(2):
-            target = lax.rem((y if h else x) + k, 4)
-
             def narrow(other, carry):
-                chunk = part_ref[other, target, 8:16] if h else part_ref[target, other, 0:8]
-                s1_ref[h, k - 1, other] = chunk.astype(BF)
+                s1_ref[h, message, other] = mine(h, k, other, half).astype(BF)
                 return carry
 
             lax.fori_loop(0, 4, narrow, 0)
-            remote(s1_ref.at[h, k - 1], a1_ref.at[h, k - 1], s1_send.at[h, k - 1], s1_recv.at[h, k - 1],
-                   col=y_peer(k) if h else x_peer(k)).start()
+            ring(1, h, message).start()
     if first:
         pltpu.make_async_copy(degree_in_ref.at[pl.ds(col * 16, 16)], dg_ref.at[col], dg_own).start()
 
@@ -355,27 +369,38 @@
         lax.fori_loop(1, NC, send, 0)
     else:
         inverse = inverse_factor(gram_unpack(gram_in_ref[...]))
+    for message, k, half in ((4, 1, 0), (5, 3, 1)):
+        for h in range(2):
+            arrived(1, h, message - 4)
+
+            def pass_on(other, carry):
+                s1_ref[h, message, other] = (mine(h, k, other, half) + a1_ref[h, message - 4, other].astype(F32)).astype(BF)
+                return carry
+
+            lax.fori_loop(0, 4, pass_on, 0)
+            ring(1, h, message).start()
     for h in range(2):
-        for k in range(3):
-            wait_bytes(a1_ref.at[h, k], s1_recv.at[h, k])
-        for k in (1, 3, 2, 0):
-            target = lax.rem((x if h else y) + k, 4)
-
-            def add(b, carry):
-                mine = part_ref[target, y, 8 + b] if h else part_ref[x, target, b]
-                value = mine
-                for source in range(3):
-                    value = value + a1_ref[h, source, target, b].astype(F32)
-                if k:
-                    r1_ref[h, k - 1, b] = value.astype(BF)
-                else:
-                    y_ref[h * 8 + b] = value
-                return carry
-
-            lax.fori_loop(0, 8, add, 0)
-            if k:
-                remote(r1_ref.at[h, k - 1], a2_ref.at[h, k - 1], s2_send.at[h, k - 1], s2_recv.at[h, k - 1],
-                       col=x_peer(k) if h else y_peer(k)).start()
+        for message in range(2, 6):
+            arrived(1, h, message)
+        place = x if h else y
+
+        def value(k, half):
+            other = lax.rem(place + k, 4)
+            near, far = (3, 4) if half == 0 else (2, 5)
+            return mine(h, 0, other, half) + a1_ref[h, near, other].astype(F32) + a1_ref[h, far, other].astype(F32)
+
+        for message, k, half in plan:
+            s2_ref[h, message] = value(k, half).astype(BF)
+            ring(2, h, message).start()
+        v_ref[h, 0] = value(1, 0)
+        v_ref[h, 1] = value(3, 1)
+        for half in range(2):
+            y_ref[h * 8 + half * 4:h * 8 + half * 4 + 4] = value(0, half)
+    for h in range(2):
+        for message in (4, 5):
+            arrived(2, h, message - 4)
+            s2_ref[h, message] = (v_ref[h, message - 4] + a2_ref[h, message - 4].astype(F32)).astype(BF)
+            ring(2, h, message).start()
     if first:
         pltpu.make_async_copy(degree_in_ref.at[pl.ds(col * 16, 16)], dg_ref.at[col], dg_own).wait()
         wait_bytes(dg_ref.at[pl.ds(0, NC - 1)], dg_recv)
@@ -384,12 +409,11 @@
             degree = degree + dg_ref[k]
         degree_ref[...] = 1.0 + degree
     for h in range(2):
-        for k in range(3):
-            wait_bytes(a2_ref.at[h, k], s2_recv.at[h, k])
+        for message in range(2, 6):
+            arrived(2, h, message)
         for b in range(8):
-            value = y_ref[h * 8 + b]
-            for k in range(3):
-                value = value + a2_ref[h, k, b].astype(F32)
+            near, far = (3, 4) if b < 4 else (2, 5)
+            value = y_ref[h * 8 + b] + a2_ref[h, near, b % 4].astype(F32) + a2_ref[h, far, b % 4].astype(F32)
             value = value * (1.0 / degree_ref[h * 8 + b:h * 8 + b + 1])
             if not first:
                 value = dot(inverse, value, ((1,), (0,)), lax.Precision.HIGHEST)
@@ -438,9 +462,9 @@
         gram_ref[...] = total
         x_finish(row, col, xs_ref, xc_ref, xt_ref, sems)
     for h in range(2):
-        for k in range(3):
-            wait_bytes(a1_ref.at[h, k], s1_send.at[h, k])
-            wait_bytes(a2_ref.at[h, k], s2_send.at[h, k])
+        for message in range(6):
+            wait_bytes(a1_ref.at[h, message], s1_send.at[h, message])
+            wait_bytes(a2_ref.at[h, message], s2_send.at[h, message])
     if first:
         wait_bytes(dg_ref.at[pl.ds(0, NC - 1)], dg_send)
     for i in range(13):
@@ -461,10 +485,10 @@
         out_shape.append(jax.ShapeDtypeStruct((16, TILE), F32))
         out_specs.append(VMEM)
     scratch = [
-        pltpu.VMEM((16, K, TILE), F32), pltpu.VMEM((2, 3, 4, 8, K, TILE), BF), pltpu.VMEM((2, 3, 4, 8, K, TILE), BF),
-        pltpu.VMEM((2, 3, 8, K, TILE), BF), pltpu.VMEM((2, 3, 8, K, TILE), BF),
+        pltpu.VMEM((16, K, TILE), F32), pltpu.VMEM((2, 6, 4, 4, K, TILE), BF), pltpu.VMEM((2, 6, 4, 4, K, TILE), BF),
+        pltpu.VMEM((2, 6, 4, K, TILE), BF), pltpu.VMEM((2, 6, 4, K, TILE), BF), pltpu.VMEM((2, 2, 4, K, TILE), F32),
         pltpu.VMEM((4,) + half, F32), pltpu.VMEM((4,) + half, F32), pltpu.VMEM((NR,) + half, F32),
-        dma((2, 3)), dma((2, 3)), dma((2, 3)), dma((2, 3)), dma((13,)), dma((13,)),
+        dma((2, 6)), dma((2, 6)), dma((2, 6)), dma((2, 6)), dma((13,)), dma((13,)),
     ]
     if first:
         scratch += [pltpu.VMEM((NC, 16, TILE), F32), dma, dma, dma]

time: 437 us -> 391 us (0.89)
  Pallas kernels: 426 us -> 381 us
    pallas_call x3, Pallas kernels: 52.2 us -> 25 us  [product(): pl.pallas_call(functools.partial(product_kernel, with_degree), out_shape=...]
    pallas_call x3, Pallas kernels: 193 us -> 174 us  [normalize(): pl.pallas_call(functools.partial(normalize_kernel, first, last), out_shap...]
where the time goes in v5:
time: 391 us
  Pallas kernels  381 us (97%)
  local copies, waits for them, and re-layouts  8.57 us (2%)
    pallas_call x1, Pallas kernels, exchange(): pl.pallas_call(exchange_kernel, out_shape=(jax.ShapeDtypeStruct(slots, BF...  181 us
    pallas_call x3, Pallas kernels, normalize(): pl.pallas_call(functools.partial(normalize_kernel, first, last), out_shap...  174 us
    pallas_call x3, Pallas kernels, product(): pl.pallas_call(functools.partial(product_kernel, with_degree), out_shape=...  25 us

profile of v5, /device:TPU:1, one launch (start us, length us, event | category | flops | bytes accessed | tf_op | source)
XLA Modules:
  0.0 390.6 jit_solution(14452815060115699714)
XLA Ops:
  0.0 0.0 copy-start.4
  0.0 0.0 copy-start.3
  0.0 0.7 fusion.8
  0.8 0.2 convert_reduce_fusion
  0.9 0.1 select_reduce_fusion
  1.1 0.2 sub.45
  1.3 0.2 gt.12
  1.6 0.1 fusion.1
  1.6 0.1 fusion.3
  1.7 1.2 copy.31
  3.0 0.5 copy.32
  3.5 0.2 reshape.47.xs_ref
  3.8 0.0 copy-start.2
  3.8 1.6 copy-done.2
  5.4 181.2 %exchange.1 = (bf16[8,16,384,128]{3,2,1,0:T(8,128)(2,1)}, bf16[8,16,384,128]{3,2,1,0:T(8,128)(2,1)}, bf16[64,128,128]{2,1,0:T(8,128)(2,1)S(1)}, f32[8,16,128]{2,1,0:T(8,128)S(1)}, bf16[130,64,128]{2,1,0:T(8,128)(2,1)S(1)}) custom-call(s32[384]{0:T(512)S(1)} %get-tuple-element.28.pick_ref, bf16[192,128,128]{2,1,0:T(8,128)(2,1)} %tiles_ref.1, ...), custom_call_target="tpu_custom_call" | custom-call | tf_op jit(solution)/shard_map/exchange/pallas_call | solution.py:202
  186.5 0.0 copy-start
  186.5 1.3 copy-done
  187.9 0.1 fusion.19
  188.0 0.2 reshape.49.rows_ref
  188.2 0.2 reshape.50.cols_ref
  188.4 0.0 copy-done.4
  188.4 0.0 copy-done.3
  188.4 0.0 copy-start.1
  188.4 1.6 copy-done.1
  190.0 11.2 %product.3 = (f32[256,64,128]{2,1,0:T(8,128)S(1)}, f32[256,128]{1,0:T(8,128)S(1)}) custom-call(s32[384]{0:T(512)S(1)} %reshape.49.rows_ref, s32[384]{0:T(512)S(1)} %reshape.50.cols_ref, s32[64]{0:T(128)S(1)} %get-tuple-element.35.own_rows_ref, s32[64]{0:T(128)S(1)} %get-tuple-element.36.own_cols_ref, bf16[130,64,128]{2,1,0:T(8,128)(2,1)S(1)} %copy-done.1, ...), custom_call_target="tpu_custom_call" | custom-call | flops 939524096 | bytes 14680064 | tf_op jit(solution)/shard_map/product/pallas_call | solution.py:276
  201.2 70.5 %normalize.3 = (bf16[130,64,128]{2,1,0:T(8,128)(2,1)S(1)}, f32[32,128]{1,0:T(8,128)S(1)}, f32[16,128]{1,0:T(8,128)S(1)}) custom-call(f32[4,4,16,64,128]{4,3,2,1,0:T(8,128)S(1)} %bitcast.12, f32[256,128]{1,0:T(8,128)S(1)} %get-tuple-element.21.degree_in_ref), custom_call_target="tpu_custom_call" | custom-call | tf_op jit(solution)/shard_map/normalize/pallas_call | solution.py:498
  271.7 6.8 %product.4 = f32[256,64,128]{2,1,0:T(8,128)S(1)} custom-call(s32[384]{0:T(512)S(1)} %reshape.49.rows_ref, s32[384]{0:T(512)S(1)} %reshape.50.cols_ref, s32[64]{0:T(128)S(1)} %get-tuple-element.35.own_rows_ref, s32[64]{0:T(128)S(1)} %get-tuple-element.36.own_cols_ref, bf16[130,64,128]{2,1,0:T(8,128)(2,1)S(1)} %get-tuple-element.22.xt_ref, ...), custom_call_target="tpu_custom_call" | custom-call | flops 939524096 | bytes 14680064 | tf_op jit(solution)/shard_map/product/pallas_call | solution.py:276
  278.5 52.9 %normalize.4 = (bf16[130,64,128]{2,1,0:T(8,128)(2,1)S(1)}, f32[32,128]{1,0:T(8,128)S(1)}) custom-call(f32[4,4,16,64,128]{4,3,2,1,0:T(8,128)S(1)} %bitcast.11, f32[16,128]{1,0:T(8,128)S(1)} %get-tuple-element.23.degree_in_ref, f32[32,128]{1,0:T(8,128)S(1)} %get-tuple-element.24.rest_0_), custom_call_target="tpu_custom_call" | custom-call | tf_op jit(solution)/shard_map/normalize/pallas_call | solution.py:498
  331.4 7.0 %product.5 = f32[256,64,128]{2,1,0:T(8,128)S(1)} custom-call(s32[384]{0:T(512)S(1)} %reshape.49.rows_ref, s32[384]{0:T(512)S(1)} %reshape.50.cols_ref, s32[64]{0:T(128)S(1)} %get-tuple-element.35.own_rows_ref, s32[64]{0:T(128)S(1)} %get-tuple-element.36.own_cols_ref, bf16[130,64,128]{2,1,0:T(8,128)(2,1)S(1)} %get-tuple-element.25.xt_ref, ...), custom_call_target="tpu_custom_call" | custom-call | flops 939524096 | bytes 14680064 | tf_op jit(solution)/shard_map/product/pallas_call | solution.py:276
  338.4 51.1 %normalize.5 = f32[2048,64]{1,0:T(8,128)S(1)} custom-call(f32[4,4,16,64,128]{4,3,2,1,0:T(8,128)S(1)} %bitcast.10, f32[16,128]{1,0:T(8,128)S(1)} %get-tuple-element.23.degree_in_ref, f32[32,128]{1,0:T(8,128)S(1)} %get-tuple-element.26.rest_0_), custom_call_target="tpu_custom_call" | custom-call | tf_op jit(solution)/shard_map/normalize/pallas_call | solution.py:498
  389.5 1.1 copy.33
  (6 shorter events, 0.1 us)
Async XLA Ops:
  0.0 188.4 %copy-start.4 = (s32[64]{0:T(128)S(1)}, s32[64]{0:T(128)}, u32[]{:S(2)}) copy-start(s32[64]{0:T(128)} %param.10) | copy-start | bytes 772
  0.0 188.4 %copy-start.3 = (s32[64]{0:T(128)S(1)}, s32[64]{0:T(128)}, u32[]{:S(2)}) copy-start(s32[64]{0:T(128)} %param.9) | copy-start | bytes 772
  3.8 1.6 copy-start.2
  186.5 1.3 copy-start
  188.4 1.6 copy-start.1

commit v6 on v5

--- a/solution.py
+++ b/solution.py
@@ -122,15 +122,19 @@
 
 
 def exchange_kernel(pick_ref, tiles_ref, own_ref, meta_ref, xs_ref,
-                    recv_ref, mid_ref, own_out_ref, places_ref, xt_ref,
+                    recv_ref, mid_ref, far_ref, own_out_ref, places_ref, xt_ref,
                     send_ref, xc_ref, meta_mid_ref, meta_next_ref, *sem_refs):
     sems = dict(zip(X_SEMS, sem_refs))
-    a_send, a_recv, b_send, b_recv, m_send, m_recv, n_send, n_recv, own_sem = sem_refs[len(X_SEMS):]
+    (a_send, a_recv, b_send, b_recv, c_send, c_recv, d_send, d_recv,
+     m_send, m_recv, n_send, n_recv, own_sem, far_sem) = sem_refs[len(X_SEMS):]
+    half = SLOT_ROWS // 2
+    head, tail = pl.ds(0, half), pl.ds(half, half)
     row = lax.axis_index("row")
     col = lax.axis_index("col")
     greet(row, col)
     x_first(row, col, xs_ref, xc_ref, sems)
     targets = [row_peer(row, dz, flip) for dz, flip in ROW_ORDER] + [row]
+    sources = [row_peer(row, (4 - dz) % 4, flip) for dz, flip in ROW_ORDER]
 
     def send_meta(k, carry):
         peer = col_peer(col, k)
@@ -140,28 +144,55 @@
     lax.fori_loop(1, NC, send_meta, 0)
     meta_mid_ref[col] = meta_ref[col]
 
+    def fill(target):
+        def tiles(c, carry):
+            for slot in range(CAP):
+                send_ref[target, c, slot * TILE:(slot + 1) * TILE] = tiles_ref[pick_ref[(target * NC + c) * CAP + slot]]
+            return carry
+
+        lax.fori_loop(0, NC, tiles, 0)
+
+    def first_own(step):
+        target = targets[step]
+        if step < NR - 1:
+            return pltpu.make_async_copy(send_ref.at[target, col, head], mid_ref.at[target, col], own_sem.at[step])
+        return pltpu.make_async_copy(send_ref.at[target, col, head], recv_ref.at[target, col, head], own_sem.at[step])
+
     def first(step):
         target = targets[step]
-        dst_ref = mid_ref if step < NR - 1 else recv_ref
-
-        def fill(k, carry):
+
+        def send(k, carry):
             peer = col_peer(col, k)
-            for slot in range(CAP):
-                send_ref[target, peer, slot * TILE:(slot + 1) * TILE] = tiles_ref[pick_ref[(target * NC + peer) * CAP + slot]]
-
-            @pl.when(k > 0)
-            def _():
-                remote(send_ref.at[target, peer], dst_ref.at[target, col], a_send.at[step], a_recv.at[step], col=peer).start()
-
+            dst = mid_ref.at[target, col] if step < NR - 1 else recv_ref.at[target, col, head]
+            remote(send_ref.at[target, peer, head], dst, a_send.at[step], a_recv.at[step], col=peer).start()
             return carry
 
-        lax.fori_loop(0, NC, fill, 0)
-        pltpu.make_async_copy(send_ref.at[target, col], dst_ref.at[target, col], own_sem.at[step]).start()
-
-    first(0)
-    x_second(row, col, xs_ref, xc_ref, sems)
-    for step in range(1, NR):
-        first(step)
+        lax.fori_loop(1, NC, send, 0)
+        first_own(step).start()
+
+    def second_own(step):
+        if step < NR - 1:
+            return pltpu.make_async_copy(far_ref.at[sources[step], col], recv_ref.at[sources[step], col, tail], far_sem.at[step])
+        return pltpu.make_async_copy(send_ref.at[row, col, tail], recv_ref.at[row, col, tail], far_sem.at[step])
+
+    def second(step):
+        def send(k, carry):
+            peer = col_peer(col, k)
+            source = sources[step] if step < NR - 1 else row
+            src = far_ref.at[source, peer] if step < NR - 1 else send_ref.at[row, peer, tail]
+            remote(src, recv_ref.at[source, col, tail], d_send.at[step], d_recv.at[source], col=peer).start()
+            return carry
+
+        lax.fori_loop(1, NC, send, 0)
+        second_own(step).start()
+
+    for step in range(NR):
+        fill(targets[step])
+        if step < NR - 1:
+            remote(send_ref.at[targets[step], :, tail], far_ref.at[row], c_send.at[step], c_recv.at[row], row=targets[step]).start()
+            first(step)
+        if step == 0:
+            x_second(row, col, xs_ref, xc_ref, sems)
     wait_bytes(meta_mid_ref.at[pl.ds(0, NC - 1)], m_recv)
     for c in range(NC):
         for r in range(NR):
@@ -178,37 +209,46 @@
 
     lax.fori_loop(0, OWN // 4, flip_own, 0)
     for step in range(NR - 1):
-        target = targets[step]
+        target, source = targets[step], sources[step]
         wait_bytes(mid_ref.at[target, pl.ds(0, NC - 1)], a_recv.at[step])
-        pltpu.make_async_copy(send_ref.at[target, col], mid_ref.at[target, col], own_sem.at[step]).wait()
-        remote(mid_ref.at[target], recv_ref.at[row], b_send.at[step], b_recv.at[row], row=target).start()
+        first_own(step).wait()
+        remote(mid_ref.at[target], recv_ref.at[row, :, head], b_send.at[step], b_recv.at[row], row=target).start()
+        wait_bytes(far_ref.at[source], c_recv.at[source])
+        second(step)
+    first(NR - 1)
+    second(NR - 1)
     x_finish(row, col, xs_ref, xc_ref, xt_ref, sems)
-    wait_bytes(recv_ref.at[row, pl.ds(0, NC - 1)], a_recv.at[NR - 1])
-    pltpu.make_async_copy(send_ref.at[row, col], recv_ref.at[row, col], own_sem.at[NR - 1]).wait()
+    some = mid_ref.at[0, pl.ds(0, NC - 1)]
+    wait_bytes(some, a_recv.at[NR - 1])
+    first_own(NR - 1).wait()
     wait_bytes(meta_mid_ref.at[pl.ds(0, NC - 1)], m_send)
     wait_bytes(places_ref.at[pl.ds(0, NR - 1)], n_send)
     wait_bytes(places_ref.at[pl.ds(0, NR - 1)], n_recv)
     for step in range(NR):
-        wait_bytes(send_ref.at[0, pl.ds(0, NC - 1)], a_send.at[step])
+        wait_bytes(some, a_send.at[step])
+        wait_bytes(some, d_send.at[step])
+        wait_bytes(some, d_recv.at[sources[step] if step < NR - 1 else row])
+        second_own(step).wait()
     for step in range(NR - 1):
-        source = targets[step]
-        wait_bytes(mid_ref.at[source], b_send.at[step])
-        wait_bytes(recv_ref.at[source], b_recv.at[source])
+        wait_bytes(mid_ref.at[0], b_send.at[step])
+        wait_bytes(mid_ref.at[0], c_send.at[step])
+        wait_bytes(mid_ref.at[0], b_recv.at[targets[step]])
 
 
 def exchange(pick, chg_tiles, own, meta, xs):
     dma = pltpu.SemaphoreType.DMA
     slots = (NR, NC, SLOT_ROWS, TILE)
-    recv, _, own, places, xt = pl.pallas_call(
+    halves = jax.ShapeDtypeStruct((NR, NC, SLOT_ROWS // 2, TILE), BF)
+    recv, _, _, own, places, xt = pl.pallas_call(
         exchange_kernel,
-        out_shape=(jax.ShapeDtypeStruct(slots, BF), jax.ShapeDtypeStruct(slots, BF), pltpu.VMEM((OWN, TILE, TILE), BF),
+        out_shape=(jax.ShapeDtypeStruct(slots, BF), halves, halves, pltpu.VMEM((OWN, TILE, TILE), BF),
                    jax.ShapeDtypeStruct((NR, NC, TILE), F32), pltpu.VMEM((X_BLOCKS, K, TILE), BF)),
         in_specs=[SMEM, VMEM, VMEM, VMEM, VMEM],
-        out_specs=(ANY, ANY, VMEM, VMEM, VMEM),
+        out_specs=(ANY, ANY, ANY, VMEM, VMEM, VMEM),
         scratch_shapes=[
             pltpu.VMEM(slots, BF), pltpu.VMEM((NR, NC, 4, 16, TILE), BF),
             pltpu.VMEM((NC, NR, TILE), F32), pltpu.VMEM((NR, NC, TILE), F32),
-        ] + x_sems() + [dma((NR,)), dma((NR,)), dma((NR,)), dma((NR,)), dma, dma, dma, dma, dma((NR,))],
+        ] + x_sems() + [dma((NR,))] * 8 + [dma, dma, dma, dma, dma((NR,)), dma((NR,))],
         compiler_params=pltpu.CompilerParams(collective_id=0, has_side_effects=True, vmem_limit_bytes=42 * MIB),
         name="exchange",
     )(pick, chg_tiles, own, meta, xs)

time: 391 us -> 358 us (0.916)
  Pallas kernels: 381 us -> 348 us
    pallas_call x1, Pallas kernels: 181 us -> 162 us  [exchange(): pl.pallas_call(exchange_kernel, out_shape=(jax.ShapeDtypeStruct(slots, BF...]
    pallas_call x3, Pallas kernels: 174 us -> 161 us  [normalize(): pl.pallas_call(functools.partial(normalize_kernel, first, last), out_shap...]
where the time goes in v6:
time: 358 us
  Pallas kernels  348 us (97%)
  local copies, waits for them, and re-layouts  8.57 us (2%)
    pallas_call x1, Pallas kernels, exchange(): pl.pallas_call(exchange_kernel, out_shape=(jax.ShapeDtypeStruct(slots, BF...  162 us
    pallas_call x3, Pallas kernels, normalize(): pl.pallas_call(functools.partial(normalize_kernel, first, last), out_shap...  161 us
    pallas_call x3, Pallas kernels, product(): pl.pallas_call(functools.partial(product_kernel, with_degree), out_shape=...  25.1 us

profile of v6, /device:TPU:1, one launch (start us, length us, event | category | flops | bytes accessed | tf_op | source)
XLA Modules:
  0.0 358.1 jit_solution(4673957412176350365)
XLA Ops:
  0.0 0.0 copy-start.4
  0.0 0.0 copy-start.3
  0.0 0.7 fusion.8
  0.8 0.2 convert_reduce_fusion
  0.9 0.1 select_reduce_fusion
  1.1 0.2 sub.45
  1.3 0.2 gt.12
  1.6 0.1 fusion.1
  1.6 0.1 fusion.3
  1.7 1.2 copy.31
  3.0 0.5 copy.32
  3.5 0.2 reshape.47.xs_ref
  3.8 0.0 copy-start.2
  3.8 1.6 copy-done.2
  5.4 162.3 %exchange.1 = (bf16[8,16,384,128]{3,2,1,0:T(8,128)(2,1)}, bf16[8,16,192,128]{3,2,1,0:T(8,128)(2,1)}, bf16[8,16,192,128]{3,2,1,0:T(8,128)(2,1)}, bf16[64,128,128]...) custom-call(s32[384]{0:T(512)S(1)} %get-tuple-element.28.pick_ref, ...), custom_call_target="tpu_custom_call" | custom-call | tf_op jit(solution)/shard_map/exchange/pallas_call | solution.py:242
  167.7 0.0 copy-start
  167.7 1.3 copy-done
  169.0 0.1 fusion.19
  169.1 0.2 reshape.49.rows_ref
  169.3 0.2 reshape.50.cols_ref
  169.5 0.0 copy-done.4
  169.5 0.0 copy-done.3
  169.5 0.0 copy-start.1
  169.6 1.6 copy-done.1
  171.1 11.3 %product.3 = (f32[256,64,128]{2,1,0:T(8,128)S(1)}, f32[256,128]{1,0:T(8,128)S(1)}) custom-call(s32[384]{0:T(512)S(1)} %reshape.49.rows_ref, s32[384]{0:T(512)S(1)} %reshape.50.cols_ref, s32[64]{0:T(128)S(1)} %get-tuple-element.35.own_rows_ref, s32[64]{0:T(128)S(1)} %get-tuple-element.36.own_cols_ref, bf16[130,64,128]{2,1,0:T(8,128)(2,1)S(1)} %copy-done.1, ...), custom_call_target="tpu_custom_call" | custom-call | flops 939524096 | bytes 14680064 | tf_op jit(solution)/shard_map/product/pallas_call | solution.py:316
  182.4 57.8 %normalize.3 = (bf16[130,64,128]{2,1,0:T(8,128)(2,1)S(1)}, f32[32,128]{1,0:T(8,128)S(1)}, f32[16,128]{1,0:T(8,128)S(1)}) custom-call(f32[4,4,16,64,128]{4,3,2,1,0:T(8,128)S(1)} %bitcast.12, f32[256,128]{1,0:T(8,128)S(1)} %get-tuple-element.21.degree_in_ref), custom_call_target="tpu_custom_call" | custom-call | tf_op jit(solution)/shard_map/normalize/pallas_call | solution.py:538
  240.2 6.8 %product.4 = f32[256,64,128]{2,1,0:T(8,128)S(1)} custom-call(s32[384]{0:T(512)S(1)} %reshape.49.rows_ref, s32[384]{0:T(512)S(1)} %reshape.50.cols_ref, s32[64]{0:T(128)S(1)} %get-tuple-element.35.own_rows_ref, s32[64]{0:T(128)S(1)} %get-tuple-element.36.own_cols_ref, bf16[130,64,128]{2,1,0:T(8,128)(2,1)S(1)} %get-tuple-element.22.xt_ref, ...), custom_call_target="tpu_custom_call" | custom-call | flops 939524096 | bytes 14680064 | tf_op jit(solution)/shard_map/product/pallas_call | solution.py:316
  247.0 52.2 %normalize.4 = (bf16[130,64,128]{2,1,0:T(8,128)(2,1)S(1)}, f32[32,128]{1,0:T(8,128)S(1)}) custom-call(f32[4,4,16,64,128]{4,3,2,1,0:T(8,128)S(1)} %bitcast.11, f32[16,128]{1,0:T(8,128)S(1)} %get-tuple-element.23.degree_in_ref, f32[32,128]{1,0:T(8,128)S(1)} %get-tuple-element.24.rest_0_), custom_call_target="tpu_custom_call" | custom-call | tf_op jit(solution)/shard_map/normalize/pallas_call | solution.py:538
  299.3 7.0 %product.5 = f32[256,64,128]{2,1,0:T(8,128)S(1)} custom-call(s32[384]{0:T(512)S(1)} %reshape.49.rows_ref, s32[384]{0:T(512)S(1)} %reshape.50.cols_ref, s32[64]{0:T(128)S(1)} %get-tuple-element.35.own_rows_ref, s32[64]{0:T(128)S(1)} %get-tuple-element.36.own_cols_ref, bf16[130,64,128]{2,1,0:T(8,128)(2,1)S(1)} %get-tuple-element.25.xt_ref, ...), custom_call_target="tpu_custom_call" | custom-call | flops 939524096 | bytes 14680064 | tf_op jit(solution)/shard_map/product/pallas_call | solution.py:316
  306.3 50.7 %normalize.5 = f32[2048,64]{1,0:T(8,128)S(1)} custom-call(f32[4,4,16,64,128]{4,3,2,1,0:T(8,128)S(1)} %bitcast.10, f32[16,128]{1,0:T(8,128)S(1)} %get-tuple-element.23.degree_in_ref, f32[32,128]{1,0:T(8,128)S(1)} %get-tuple-element.26.rest_0_), custom_call_target="tpu_custom_call" | custom-call | tf_op jit(solution)/shard_map/normalize/pallas_call | solution.py:538
  357.0 1.1 copy.33
  (6 shorter events, 0.1 us)
Async XLA Ops:
  0.0 169.5 %copy-start.4 = (s32[64]{0:T(128)S(1)}, s32[64]{0:T(128)}, u32[]{:S(2)}) copy-start(s32[64]{0:T(128)} %param.10) | copy-start | bytes 772
  0.0 169.5 %copy-start.3 = (s32[64]{0:T(128)S(1)}, s32[64]{0:T(128)}, u32[]{:S(2)}) copy-start(s32[64]{0:T(128)} %param.9) | copy-start | bytes 772
  3.8 1.6 copy-start.2
  167.7 1.3 copy-start
  169.5 1.6 copy-start.1

commit v7 on v6

--- a/solution.py
+++ b/solution.py
@@ -26,7 +26,7 @@
 VMEM = pl.BlockSpec(memory_space=pltpu.VMEM)
 SMEM = pl.BlockSpec(memory_space=pltpu.SMEM)
 MIB = 1024 * 1024
-ROW_ORDER = ((1, 0), (3, 1), (2, 0), (1, 1), (3, 0), (2, 1), (0, 1))
+ROW_ORDER = ((2, 0), (1, 1), (3, 0), (2, 1), (1, 0), (3, 1), (0, 1))
 
 
 def dot(a, b, dims, precision=None):
@@ -66,6 +66,13 @@
 
 def row_peer(row, dz, flip=0):
     return lax.rem(row // 2 + dz, 4) * 2 + lax.rem(row + flip, 2)
+
+
+def x_pieces(block, xs):
+    for pair in range(4):
+        for part in range(2):
+            both = jnp.concatenate([block(pair * 4 + part), block(pair * 4 + 2 + part)], axis=0).T
+            xs[part * 8:(part + 1) * 8, pair] = both.astype(BF).reshape(8, 16, TILE)
 
 
 def x_first(row, col, xs, xc, sems):
@@ -121,17 +128,22 @@
     return [dma, dma, dma, dma((7,)), dma((NR,))]
 
 
-def exchange_kernel(pick_ref, tiles_ref, own_ref, meta_ref, xs_ref,
+def exchange_kernel(pick_ref, tiles_in_ref, own_in_ref, meta_ref, embed_ref,
                     recv_ref, mid_ref, far_ref, own_out_ref, places_ref, xt_ref,
-                    send_ref, xc_ref, meta_mid_ref, meta_next_ref, *sem_refs):
+                    send_ref, xc_ref, meta_mid_ref, meta_next_ref, xs_ref, tiles_ref, own_ref, tiles_sem, own_load_sem, *sem_refs):
     sems = dict(zip(X_SEMS, sem_refs))
     (a_send, a_recv, b_send, b_recv, c_send, c_recv, d_send, d_recv,
      m_send, m_recv, n_send, n_recv, own_sem, far_sem) = sem_refs[len(X_SEMS):]
+    load_tiles = pltpu.make_async_copy(tiles_in_ref, tiles_ref, tiles_sem)
+    load_own = pltpu.make_async_copy(own_in_ref, own_ref, own_load_sem)
+    load_tiles.start()
+    load_own.start()
     half = SLOT_ROWS // 2
     head, tail = pl.ds(0, half), pl.ds(half, half)
     row = lax.axis_index("row")
     col = lax.axis_index("col")
     greet(row, col)
+    x_pieces(lambda b: embed_ref[:, b * TILE:(b + 1) * TILE], xs_ref)
     x_first(row, col, xs_ref, xc_ref, sems)
     targets = [row_peer(row, dz, flip) for dz, flip in ROW_ORDER] + [row]
     sources = [row_peer(row, (4 - dz) % 4, flip) for dz, flip in ROW_ORDER]
@@ -186,6 +198,7 @@
         lax.fori_loop(1, NC, send, 0)
         second_own(step).start()
 
+    load_tiles.wait()
     for step in range(NR):
         fill(targets[step])
         if step < NR - 1:
@@ -207,6 +220,7 @@
             own_out_ref[i * 4 + u] = own_ref[i * 4 + u].T
         return carry
 
+    load_own.wait()
     lax.fori_loop(0, OWN // 4, flip_own, 0)
     for step in range(NR - 1):
         target, source = targets[step], sources[step]
@@ -242,24 +256,27 @@
     recv, _, _, own, places, xt = pl.pallas_call(
         exchange_kernel,
         out_shape=(jax.ShapeDtypeStruct(slots, BF), halves, halves, pltpu.VMEM((OWN, TILE, TILE), BF),
-                   jax.ShapeDtypeStruct((NR, NC, TILE), F32), pltpu.VMEM((X_BLOCKS, K, TILE), BF)),
-        in_specs=[SMEM, VMEM, VMEM, VMEM, VMEM],
+                   jax.ShapeDtypeStruct((NR, NC, TILE), jnp.int32), pltpu.VMEM((X_BLOCKS, K, TILE), BF)),
+        in_specs=[SMEM, ANY, ANY, VMEM, VMEM],
         out_specs=(ANY, ANY, ANY, VMEM, VMEM, VMEM),
         scratch_shapes=[
             pltpu.VMEM(slots, BF), pltpu.VMEM((NR, NC, 4, 16, TILE), BF),
-            pltpu.VMEM((NC, NR, TILE), F32), pltpu.VMEM((NR, NC, TILE), F32),
+            pltpu.VMEM((NC, NR, TILE), jnp.int32), pltpu.VMEM((NR, NC, TILE), jnp.int32),
+            pltpu.VMEM((NC, 4, 16, TILE), BF), pltpu.VMEM(chg_tiles.shape, BF), pltpu.VMEM(own.shape, BF), dma, dma,
         ] + x_sems() + [dma((NR,))] * 8 + [dma, dma, dma, dma, dma((NR,)), dma((NR,))],
-        compiler_params=pltpu.CompilerParams(collective_id=0, has_side_effects=True, vmem_limit_bytes=42 * MIB),
+        compiler_params=pltpu.CompilerParams(collective_id=0, has_side_effects=True, vmem_limit_bytes=58 * MIB),
         name="exchange",
     )(pick, chg_tiles, own, meta, xs)
     return recv, own, places, xt
 
 
-def product_kernel(with_degree, rows_ref, cols_ref, own_rows_ref, own_cols_ref, xt_ref, own_ref, slots_in_ref, acc_ref, *rest):
-    slots_ref, slot_sem = rest[-2:]
+def product_kernel(with_degree, places_ref, own_rows_ref, own_cols_ref, xt_ref, own_ref, slots_in_ref, acc_ref, *rest):
+    slots_ref, slot_sem, table_ref, table_sem = rest[-4:]
+    load_table = pltpu.make_async_copy(places_ref, table_ref, table_sem)
+    load_table.start()
     loads = [
-        pltpu.make_async_copy(slots_in_ref.at[pl.ds(i * 16, 16)], slots_ref.at[pl.ds(i * 16, 16)], slot_sem.at[i])
-        for i in range(DEV // 16)
+        pltpu.make_async_copy(slots_in_ref.at[i], slots_ref.at[i], slot_sem.at[i])
+        for i in range(NR)
     ]
     for load in loads:
         load.start()
@@ -293,14 +310,15 @@
         run([own_ref[n] for n in places], [own_rows_ref[n] for n in places], [own_cols_ref[n] for n in places])
         return carry
 
-    def taken(i, carry):
-        sources = [i * 16 + u for u in range(16)]
-        places = [source * CAP + slot for source in sources for slot in range(CAP)]
-        run([slots_ref[source, slot * TILE:(slot + 1) * TILE] for source in sources for slot in range(CAP)],
-            [rows_ref[n] for n in places], [cols_ref[n] for n in places])
+    def taken(group, carry):
+        places = [(source, slot) for source in range(NC) for slot in range(CAP)]
+        run([slots_ref[group, source, slot * TILE:(slot + 1) * TILE] for source, slot in places],
+            [table_ref[group, source, slot] for source, slot in places],
+            [table_ref[group, source, CAP + slot] for source, slot in places])
         return carry
 
     lax.fori_loop(0, OWN // 16, own, 0)
+    load_table.wait()
     for i, load in enumerate(loads):
         load.wait()
         lax.fori_loop(i, i + 1, taken, 0)
@@ -308,7 +326,7 @@
         degree_out_ref[...] = degree_ref[...].reshape(ROWS_BLK, TILE)
 
 
-def product(with_degree, rows, cols, own_rows, own_cols, xt, own, slots):
+def product(with_degree, places, own_rows, own_cols, xt, own, slots):
     out_shape = [pltpu.VMEM((ROWS_BLK, K, TILE), F32)]
     if with_degree:
         out_shape.append(jax.ShapeDtypeStruct((ROWS_BLK, TILE), F32))
@@ -316,15 +334,16 @@
     return pl.pallas_call(
         functools.partial(product_kernel, with_degree),
         out_shape=out_shape,
-        in_specs=[SMEM, SMEM, SMEM, SMEM, VMEM, VMEM, ANY],
+        in_specs=[VMEM, SMEM, SMEM, VMEM, VMEM, ANY],
         out_specs=[VMEM] * len(out_shape),
         scratch_shapes=([pltpu.VMEM((ROWS_BLK, 1, TILE), F32)] if with_degree else []) + [
-            pltpu.VMEM((DEV, SLOT_ROWS, TILE), BF), pltpu.SemaphoreType.DMA((DEV // 16,)),
+            pltpu.VMEM((NR, NC, SLOT_ROWS, TILE), BF), pltpu.SemaphoreType.DMA((NR,)),
+            pltpu.SMEM((NR, NC, TILE), jnp.int32), pltpu.SemaphoreType.DMA,
         ],
         compiler_params=pltpu.CompilerParams(vmem_limit_bytes=40 * MIB),
         cost_estimate=pl.CostEstimate(flops=terms * 2 * K * TILE * TILE, bytes_accessed=terms * TILE * TILE * 2, transcendentals=0),
         name="product",
-    )(rows, cols, own_rows, own_cols, xt, own, slots.reshape(DEV, SLOT_ROWS, TILE))
+    )(places, own_rows, own_cols, xt, own, slots)
 
 
 def inverse_factor(gram):
@@ -332,11 +351,19 @@
     work = jnp.concatenate([gram, eye], axis=1)
     index = lax.broadcasted_iota(jnp.int32, (K, 1), 0)
     pivots = jnp.ones((K, 1), F32)
-    for j in range(K):
-        pivot = work[j:j + 1, j:j + 1]
-        pivots = jnp.where(index == j, pivot, pivots)
-        factor = jnp.where(index > j, work[:, j:j + 1] * (1.0 / pivot), 0.0)
-        work = work - factor * work[j:j + 1, :]
+    for j in range(0, K, 2):
+        first_row, first_col = work[j:j + 1, :], work[:, j:j + 1]
+        second_col = work[:, j + 1:j + 2]
+        pivot, below = first_col[j:j + 1], first_col[j + 1:j + 2]
+        beside = second_col[j:j + 1]
+        inverse = 1.0 / pivot
+        step = below * inverse
+        second_row = work[j + 1:j + 2, :] - step * first_row
+        second_pivot = second_col[j + 1:j + 2] - step * beside
+        first_factor = jnp.where(index > j, first_col * inverse, 0.0)
+        second_factor = jnp.where(index > j + 1, (second_col - first_factor * beside) * (1.0 / second_pivot), 0.0)
+        pivots = jnp.where(index == j, pivot, jnp.where(index == j + 1, second_pivot, pivots))
+        work = work - first_factor * first_row - second_factor * second_row
     return lax.rsqrt(pivots) * work[:, K:]
 
 
@@ -460,10 +487,7 @@
             y_ref[h * 8 + b] = value
 
     if not last:
-        for pair in range(4):
-            for part in range(2):
-                both = jnp.concatenate([y_ref[pair * 4 + part], y_ref[pair * 4 + 2 + part]], axis=0).T
-                xs_ref[part * 8:(part + 1) * 8, pair] = both.astype(BF).reshape(8, 16, TILE)
+        x_pieces(lambda b: y_ref[b], xs_ref)
         x_first(row, col, xs_ref, xc_ref, sems)
 
     gram = jnp.zeros((K, K), F32)
@@ -493,11 +517,8 @@
     total = collect(g3_ref, NR, 6) * (1.0 / NODES)
     if last:
         final = inverse_factor(gram_unpack(total))
-        for b in range(0, 16, 2):
-            both = [dot(final, y_ref[b + i], ((1,), (0,)), lax.Precision.HIGHEST) for i in range(2)]
-            both = jnp.concatenate(both, axis=0).T
-            z_ref[b * TILE:(b + 1) * TILE] = both[:, :K]
-            z_ref[(b + 1) * TILE:(b + 2) * TILE] = both[:, K:]
+        for b in range(16):
+            z_ref[:, b * TILE:(b + 1) * TILE] = dot(final, y_ref[b], ((1,), (0,)), lax.Precision.HIGHEST)
     else:
         gram_ref[...] = total
         x_finish(row, col, xs_ref, xc_ref, xt_ref, sems)
@@ -516,7 +537,7 @@
     half = (K // 2, TILE)
     out_shape, out_specs = [], []
     if last:
-        out_shape.append(jax.ShapeDtypeStruct((16 * TILE, K), F32))
+        out_shape.append(jax.ShapeDtypeStruct((K, 16 * TILE), F32))
         out_specs.append(VMEM)
     else:
         out_shape += [pltpu.VMEM((X_BLOCKS, K, TILE), BF), jax.ShapeDtypeStruct(half, F32)]
@@ -565,22 +586,18 @@
     slot_rows = jnp.where(code > 0, (code - 1) // 128, 0).reshape(DEV, CAP)
     slot_cols = jnp.where(code > 0, (code - 1) % 128, 128).reshape(DEV, CAP)
     meta = jnp.concatenate([slot_rows, slot_cols], axis=1).reshape(NR, NC, 2 * CAP).transpose(1, 0, 2)
-    meta = jnp.pad(meta.astype(F32), ((0, 0), (0, 0), (0, TILE - 2 * CAP)))
-    xs = embed.reshape(4, 2, NC, 16, K).transpose(2, 0, 3, 1, 4).reshape(NC, 4, 16, TILE)
-    slots, tiles, places, xc = exchange(pick, chg_tiles, tiles, meta, xs)
-    places = places.reshape(DEV, TILE)[:, :2 * CAP].astype(jnp.int32)
-    rows = places[:, :CAP].reshape(DEV * CAP)
-    cols = places[:, CAP:].reshape(DEV * CAP)
+    meta = jnp.pad(meta, ((0, 0), (0, 0), (0, TILE - 2 * CAP)))
+    slots, tiles, places, xc = exchange(pick, chg_tiles, tiles, meta, embed.T)
     own_rows = tile_rows % 256
     own_cols = block_index(tile_cols % 128)
-    part, degree = product(True, rows, cols, own_rows, own_cols, xc, tiles, slots)
+    part, degree = product(True, places, own_rows, own_cols, xc, tiles, slots)
     xc, gram, degree = normalize(True, False, part, degree, None)
     for iteration in range(1, ITERS):
-        (part,) = product(False, rows, cols, own_rows, own_cols, xc, tiles, slots)
+        (part,) = product(False, places, own_rows, own_cols, xc, tiles, slots)
         last = iteration == ITERS - 1
         outs = normalize(False, last, part, degree, gram)
         if last:
-            return outs[0]
+            return outs[0].T
         xc, gram = outs
 
 

time: 358 us -> 348 us (0.972)
  local copies, waits for them, and re-layouts: 8.57 us -> 2.7 us
  Pallas kernels: 348 us -> 343 us
    pallas_call x3, Pallas kernels: 161 us -> 156 us  [normalize(): pl.pallas_call(functools.partial(normalize_kernel, first, last), out_shap...]
    unnamed x11 -> x7, local copies, waits for them, and re-layouts: 5.74 us -> 1.64 us
where the time goes in v7:
time: 348 us
  Pallas kernels  343 us (99%)
    pallas_call x1, Pallas kernels, exchange(): pl.pallas_call(exchange_kernel, out_shape=(jax.ShapeDtypeStruct(slots, BF...  162 us
    pallas_call x3, Pallas kernels, normalize(): pl.pallas_call(functools.partial(normalize_kernel, first, last), out_shap...  156 us
    pallas_call x3, Pallas kernels, product(): pl.pallas_call(functools.partial(product_kernel, with_degree), out_shape=...  25.5 us

profile of v7, /device:TPU:1, one launch (start us, length us, event | category | flops | bytes accessed | tf_op | source)
XLA Modules:
  0.0 348.0 jit_solution(6353829137465737101)
XLA Ops:
  0.0 0.0 copy-start.2
  0.0 0.0 copy-start.1
  0.0 0.7 fusion.7
  0.8 0.2 convert_reduce_fusion
  0.9 0.7 select_reduce_fusion
  1.7 0.2 sub.45
  1.9 0.2 gt.12
  2.1 0.1 fusion.1
  2.2 0.1 add_bitcast_fusion
  2.3 0.6 pad.4.meta_ref
  3.0 161.6 %exchange.1 = (bf16[8,16,384,128]{3,2,1,0:T(8,128)(2,1)}, bf16[8,16,192,128]{3,2,1,0:T(8,128)(2,1)}, bf16[8,16,192,128]{3,2,1,0:T(8,128)(2,1)}, bf16[64,128,128]...) custom-call(s32[384]{0:T(512)} %get-tuple-element.28.pick_ref, ...), custom_call_target="tpu_custom_call" | custom-call | tf_op jit(solution)/shard_map/exchange/pallas_call | solution.py:256
  164.5 0.0 copy-done.2
  164.5 0.0 copy-done.1
  164.6 0.0 copy-start
  164.6 0.8 copy-done
  165.4 11.5 %product.3 = (f32[256,64,128]{2,1,0:T(8,128)S(1)}, f32[256,128]{1,0:T(8,128)S(1)}) custom-call(s32[8,16,128]{2,1,0:T(8,128)S(1)} %copy-done, s32[64]{0:T(128)S(1)} %get-tuple-element.33.own_rows_ref, s32[64]{0:T(128)S(1)} %get-tuple-element.34.own_cols_ref, bf16[130,64,128]{2,1,0:T(8,128)(2,1)S(1)} %get-tuple-element.17.xt_ref, ...), custom_call_target="tpu_custom_call" | custom-call | flops 939524096 | bytes 14680064 | tf_op jit(solution)/shard_map/product/pallas_call | solution.py:334
  176.9 52.5 %normalize.3 = (bf16[130,64,128]{2,1,0:T(8,128)(2,1)S(1)}, f32[32,128]{1,0:T(8,128)S(1)}, f32[16,128]{1,0:T(8,128)S(1)}) custom-call(f32[4,4,16,64,128]{4,3,2,1,0:T(8,128)S(1)} %bitcast.9, f32[256,128]{1,0:T(8,128)S(1)} %get-tuple-element.21.degree_in_ref), custom_call_target="tpu_custom_call" | custom-call | tf_op jit(solution)/shard_map/normalize/pallas_call | solution.py:559
  229.4 6.9 %product.4 = f32[256,64,128]{2,1,0:T(8,128)S(1)} custom-call(s32[8,16,128]{2,1,0:T(8,128)S(1)} %copy-done, s32[64]{0:T(128)S(1)} %get-tuple-element.33.own_rows_ref, s32[64]{0:T(128)S(1)} %get-tuple-element.34.own_cols_ref, bf16[130,64,128]{2,1,0:T(8,128)(2,1)S(1)} %get-tuple-element.22.xt_ref, bf16[64,128,128]{2,1,0:T(8,128)(2,1)S(1)} %get-tuple-element.18.own_ref, ...), custom_call_target="tpu_custom_call" | custom-call | flops 939524096 | bytes 14680064 | tf_op jit(solution)/shard_map/product/pallas_call | solution.py:334
  236.3 50.1 %normalize.4 = (bf16[130,64,128]{2,1,0:T(8,128)(2,1)S(1)}, f32[32,128]{1,0:T(8,128)S(1)}) custom-call(f32[4,4,16,64,128]{4,3,2,1,0:T(8,128)S(1)} %bitcast.8, f32[16,128]{1,0:T(8,128)S(1)} %get-tuple-element.23.degree_in_ref, f32[32,128]{1,0:T(8,128)S(1)} %get-tuple-element.24.rest_0_), custom_call_target="tpu_custom_call" | custom-call | tf_op jit(solution)/shard_map/normalize/pallas_call | solution.py:559
  286.4 7.1 %product.5 = f32[256,64,128]{2,1,0:T(8,128)S(1)} custom-call(s32[8,16,128]{2,1,0:T(8,128)S(1)} %copy-done, s32[64]{0:T(128)S(1)} %get-tuple-element.33.own_rows_ref, s32[64]{0:T(128)S(1)} %get-tuple-element.34.own_cols_ref, bf16[130,64,128]{2,1,0:T(8,128)(2,1)S(1)} %get-tuple-element.25.xt_ref, bf16[64,128,128]{2,1,0:T(8,128)(2,1)S(1)} %get-tuple-element.18.own_ref, ...), custom_call_target="tpu_custom_call" | custom-call | flops 939524096 | bytes 14680064 | tf_op jit(solution)/shard_map/product/pallas_call | solution.py:334
  293.6 53.6 %normalize.5 = f32[64,2048]{1,0:T(8,128)S(1)} custom-call(f32[4,4,16,64,128]{4,3,2,1,0:T(8,128)S(1)} %bitcast.7, f32[16,128]{1,0:T(8,128)S(1)} %get-tuple-element.23.degree_in_ref, f32[32,128]{1,0:T(8,128)S(1)} %get-tuple-element.26.rest_0_), custom_call_target="tpu_custom_call" | custom-call | tf_op jit(solution)/shard_map/normalize/pallas_call | solution.py:559
  347.2 0.8 copy.45
  (4 shorter events, 0.0 us)
Async XLA Ops:
  0.0 164.5 %copy-start.2 = (s32[64]{0:T(128)S(1)}, s32[64]{0:T(128)}, u32[]{:S(2)}) copy-start(s32[64]{0:T(128)} %param.10) | copy-start | bytes 772
  0.0 164.5 %copy-start.1 = (s32[64]{0:T(128)S(1)}, s32[64]{0:T(128)}, u32[]{:S(2)}) copy-start(s32[64]{0:T(128)} %param.9) | copy-start | bytes 772
  164.6 0.8 copy-start

commit v8 on v7

--- a/solution.py
+++ b/solution.py
@@ -68,56 +68,64 @@
     return lax.rem(row // 2 + dz, 4) * 2 + lax.rem(row + flip, 2)
 
 
-def x_pieces(block, xs):
-    for pair in range(4):
+def x_pieces(batch, block, xs):
+    for i in range(2):
         for part in range(2):
+            pair = batch * 2 + i
             both = jnp.concatenate([block(pair * 4 + part), block(pair * 4 + 2 + part)], axis=0).T
-            xs[part * 8:(part + 1) * 8, pair] = both.astype(BF).reshape(8, 16, TILE)
-
-
-def x_first(row, col, xs, xc, sems):
-    pltpu.make_async_copy(xs.at[col], xc.at[row, col], sems["x_own"]).start()
+            xs[batch, part * 8:(part + 1) * 8, i] = both.astype(BF).reshape(8, 16, TILE)
+
+
+def x_own_copy(batch, row, col, xs, xc, sems):
+    return pltpu.make_async_copy(xs.at[batch, col], xc.at[batch, row, col], sems["x_own"].at[batch])
+
+
+def x_first(batch, row, col, xs, xc, sems):
+    x_own_copy(batch, row, col, xs, xc, sems).start()
 
     def send(k, carry):
         peer = col_peer(col, k)
-        remote(xs.at[peer], xc.at[row, col], sems["xa_send"], sems["xa_recv"], col=peer).start()
+        remote(xs.at[batch, peer], xc.at[batch, row, col], sems["xa_send"].at[batch], sems["xa_recv"].at[batch], col=peer).start()
         return carry
 
     lax.fori_loop(1, NC, send, 0)
 
 
-def x_second(row, col, xs, xc, sems):
-    pltpu.make_async_copy(xs.at[col], xc.at[row, col], sems["x_own"]).wait()
-    wait_bytes(xc.at[row, pl.ds(0, NC - 1)], sems["xa_recv"])
+def x_second(batch, row, col, xs, xc, sems):
+    x_own_copy(batch, row, col, xs, xc, sems).wait()
+    wait_bytes(xc.at[batch, row, pl.ds(0, NC - 1)], sems["xa_recv"].at[batch])
     for i, (dz, flip) in enumerate(((1, 0), (3, 0), (2, 0), (0, 1))):
-        remote(xc.at[row], xc.at[row], sems["xb_send"].at[i], sems["xb_recv"].at[row], row=row_peer(row, dz, flip)).start()
-
-
-def x_third(row, col, xs, xc, sems):
+        remote(xc.at[batch, row], xc.at[batch, row], sems["xb_send"].at[batch, i], sems["xb_recv"].at[batch, row],
+               row=row_peer(row, dz, flip)).start()
+
+
+def x_third(batch, row, col, xs, xc, sems):
     for i, dz in enumerate((1, 3, 2)):
         source = row_peer(row, dz)
-        wait_bytes(xc.at[source], sems["xb_recv"].at[source])
-        remote(xc.at[source], xc.at[source], sems["xb_send"].at[4 + i], sems["xb_recv"].at[source], row=row_peer(row, 0, 1)).start()
-
-
-def x_finish(row, col, xs, xc, xt, sems):
-    xt[X_BLOCKS - 2:] = jnp.zeros((2, K, TILE), BF)
+        wait_bytes(xc.at[batch, source], sems["xb_recv"].at[batch, source])
+        remote(xc.at[batch, source], xc.at[batch, source], sems["xb_send"].at[batch, 4 + i], sems["xb_recv"].at[batch, source],
+               row=row_peer(row, 0, 1)).start()
+
+
+def x_finish(batch, row, col, xs, xc, xt, sems):
     for dz in range(4):
-        turn(row_peer(row, dz), xc, xt)
+        turn(batch, row_peer(row, dz), xc, xt)
     for dz in (0, 1, 3, 2):
         source = row_peer(row, dz, 1)
-        wait_bytes(xc.at[source], sems["xb_recv"].at[source])
-        turn(source, xc, xt)
-    wait_bytes(xs.at[pl.ds(0, NC - 1)], sems["xa_send"])
+        wait_bytes(xc.at[batch, source], sems["xb_recv"].at[batch, source])
+        turn(batch, source, xc, xt)
+    wait_bytes(xs.at[batch, pl.ds(0, NC - 1)], sems["xa_send"].at[batch])
     for i in range(7):
-        wait_bytes(xc.at[row], sems["xb_send"].at[i])
-
-
-def turn(source, xc, xt):
+        wait_bytes(xc.at[batch, row], sems["xb_send"].at[batch, i])
+    if batch:
+        xt[X_BLOCKS - 2:] = jnp.zeros((2, K, TILE), BF)
+
+
+def turn(batch, source, xc, xt):
     for part in range(2):
-        for pair in range(4):
-            block = xc[source, part * 8:(part + 1) * 8, pair].reshape(TILE, TILE)
-            xt[pl.ds((pair * 16 + source * 2 + part) * 2, 2)] = block.T.reshape(2, K, TILE)
+        for i in range(2):
+            block = xc[batch, source, part * 8:(part + 1) * 8, i].reshape(TILE, TILE)
+            xt[pl.ds(((batch * 2 + i) * 16 + source * 2 + part) * 2, 2)] = block.T.reshape(2, K, TILE)
 
 
 X_SEMS = ("x_own", "xa_send", "xa_recv", "xb_send", "xb_recv")
@@ -125,7 +133,11 @@
 
 def x_sems():
     dma = pltpu.SemaphoreType.DMA
-    return [dma, dma, dma, dma((7,)), dma((NR,))]
+    return [dma((2,)), dma((2,)), dma((2,)), dma((2, 7)), dma((2, NR))]
+
+
+XS_SHAPE = (2, NC, 2, 16, TILE)
+XC_SHAPE = (2, NR, NC, 2, 16, TILE)
 
 
 def exchange_kernel(pick_ref, tiles_in_ref, own_in_ref, meta_ref, embed_ref,
@@ -143,8 +155,9 @@
     row = lax.axis_index("row")
     col = lax.axis_index("col")
     greet(row, col)
-    x_pieces(lambda b: embed_ref[:, b * TILE:(b + 1) * TILE], xs_ref)
-    x_first(row, col, xs_ref, xc_ref, sems)
+    for batch in range(2):
+        x_pieces(batch, lambda b: embed_ref[:, b * TILE:(b + 1) * TILE], xs_ref)
+        x_first(batch, row, col, xs_ref, xc_ref, sems)
     targets = [row_peer(row, dz, flip) for dz, flip in ROW_ORDER] + [row]
     sources = [row_peer(row, (4 - dz) % 4, flip) for dz, flip in ROW_ORDER]
 
@@ -204,8 +217,8 @@
         if step < NR - 1:
             remote(send_ref.at[targets[step], :, tail], far_ref.at[row], c_send.at[step], c_recv.at[row], row=targets[step]).start()
             first(step)
-        if step == 0:
-            x_second(row, col, xs_ref, xc_ref, sems)
+        if step < 2:
+            x_second(step, row, col, xs_ref, xc_ref, sems)
     wait_bytes(meta_mid_ref.at[pl.ds(0, NC - 1)], m_recv)
     for c in range(NC):
         for r in range(NR):
@@ -213,7 +226,8 @@
     for step in range(NR - 1):
         remote(meta_next_ref.at[targets[step]], places_ref.at[row], n_send, n_recv, row=targets[step]).start()
     places_ref[row] = meta_next_ref[row]
-    x_third(row, col, xs_ref, xc_ref, sems)
+    for batch in range(2):
+        x_third(batch, row, col, xs_ref, xc_ref, sems)
 
     def flip_own(i, carry):
         for u in range(4):
@@ -231,7 +245,8 @@
         second(step)
     first(NR - 1)
     second(NR - 1)
-    x_finish(row, col, xs_ref, xc_ref, xt_ref, sems)
+    for batch in range(2):
+        x_finish(batch, row, col, xs_ref, xc_ref, xt_ref, sems)
     some = mid_ref.at[0, pl.ds(0, NC - 1)]
     wait_bytes(some, a_recv.at[NR - 1])
     first_own(NR - 1).wait()
@@ -260,9 +275,9 @@
         in_specs=[SMEM, ANY, ANY, VMEM, VMEM],
         out_specs=(ANY, ANY, ANY, VMEM, VMEM, VMEM),
         scratch_shapes=[
-            pltpu.VMEM(slots, BF), pltpu.VMEM((NR, NC, 4, 16, TILE), BF),
+            pltpu.VMEM(slots, BF), pltpu.VMEM(XC_SHAPE, BF),
             pltpu.VMEM((NC, NR, TILE), jnp.int32), pltpu.VMEM((NR, NC, TILE), jnp.int32),
-            pltpu.VMEM((NC, 4, 16, TILE), BF), pltpu.VMEM(chg_tiles.shape, BF), pltpu.VMEM(own.shape, BF), dma, dma,
+            pltpu.VMEM(XS_SHAPE, BF), pltpu.VMEM(chg_tiles.shape, BF), pltpu.VMEM(own.shape, BF), dma, dma,
         ] + x_sems() + [dma((NR,))] * 8 + [dma, dma, dma, dma, dma((NR,)), dma((NR,))],
         compiler_params=pltpu.CompilerParams(collective_id=0, has_side_effects=True, vmem_limit_bytes=58 * MIB),
         name="exchange",
@@ -485,10 +500,12 @@
             if not first:
                 value = dot(inverse, value, ((1,), (0,)), lax.Precision.HIGHEST)
             y_ref[h * 8 + b] = value
+        if not last:
+            x_pieces(h, lambda b: y_ref[b], xs_ref)
+            x_first(h, row, col, xs_ref, xc_ref, sems)
 
     if not last:
-        x_pieces(lambda b: y_ref[b], xs_ref)
-        x_first(row, col, xs_ref, xc_ref, sems)
+        x_second(0, row, col, xs_ref, xc_ref, sems)
 
     gram = jnp.zeros((K, K), F32)
     for b in range(16):
@@ -509,11 +526,12 @@
 
     share(g1_ref, x, gram_pack(gram), [dict(col=x_peer(k)) for k in (1, 3, 2)], 0)
     if not last:
-        x_second(row, col, xs_ref, xc_ref, sems)
+        x_second(1, row, col, xs_ref, xc_ref, sems)
     share(g2_ref, y, collect(g1_ref, 4, 0), [dict(col=y_peer(k)) for k in (1, 3, 2)], 3)
     share(g3_ref, row, collect(g2_ref, 4, 3), [dict(row=row_peer(row, dz, flip)) for dz, flip in ROW_ORDER], 6)
     if not last:
-        x_third(row, col, xs_ref, xc_ref, sems)
+        x_third(0, row, col, xs_ref, xc_ref, sems)
+        x_third(1, row, col, xs_ref, xc_ref, sems)
     total = collect(g3_ref, NR, 6) * (1.0 / NODES)
     if last:
         final = inverse_factor(gram_unpack(total))
@@ -521,7 +539,8 @@
             z_ref[:, b * TILE:(b + 1) * TILE] = dot(final, y_ref[b], ((1,), (0,)), lax.Precision.HIGHEST)
     else:
         gram_ref[...] = total
-        x_finish(row, col, xs_ref, xc_ref, xt_ref, sems)
+        x_finish(0, row, col, xs_ref, xc_ref, xt_ref, sems)
+        x_finish(1, row, col, xs_ref, xc_ref, xt_ref, sems)
     for h in range(2):
         for message in range(6):
             wait_bytes(a1_ref.at[h, message], s1_send.at[h, message])
@@ -554,7 +573,7 @@
     if first:
         scratch += [pltpu.VMEM((NC, 16, TILE), F32), dma, dma, dma]
     if not last:
-        scratch += [pltpu.VMEM((NC, 4, 16, TILE), BF), pltpu.VMEM((NR, NC, 4, 16, TILE), BF)] + x_sems()
+        scratch += [pltpu.VMEM(XS_SHAPE, BF), pltpu.VMEM(XC_SHAPE, BF)] + x_sems()
     args = [part.reshape(4, 4, 16, K, TILE), degree] + ([] if first else [gram])
     return pl.pallas_call(
         functools.partial(normalize_kernel, first, last),

time: 348 us -> 347 us (level)
  no operation moved by 1% of the time
where the time goes in v8:
time: 347 us
  Pallas kernels  343 us (99%)
    pallas_call x1, Pallas kernels, exchange(): pl.pallas_call(exchange_kernel, out_shape=(jax.ShapeDtypeStruct(slots, BF...  162 us
    pallas_call x3, Pallas kernels, normalize(): pl.pallas_call(functools.partial(normalize_kernel, first, last), out_shap...  155 us
    pallas_call x3, Pallas kernels, product(): pl.pallas_call(functools.partial(product_kernel, with_degree), out_shape=...  25.5 us

profile of v8, /device:TPU:1, one launch (start us, length us, event | category | flops | bytes accessed | tf_op | source)
XLA Modules:
  0.0 347.3 jit_solution(4690279872712695104)
XLA Ops:
  0.0 0.0 copy-start.2
  0.0 0.0 copy-start.1
  0.0 0.7 fusion.7
  0.8 0.2 convert_reduce_fusion
  0.9 0.7 select_reduce_fusion
  1.7 0.2 sub.45
  1.9 0.2 gt.12
  2.1 0.1 fusion.1
  2.2 0.1 add_bitcast_fusion
  2.3 0.6 pad.4.meta_ref
  3.0 162.1 %exchange.1 = (bf16[8,16,384,128]{3,2,1,0:T(8,128)(2,1)}, bf16[8,16,192,128]{3,2,1,0:T(8,128)(2,1)}, bf16[8,16,192,128]{3,2,1,0:T(8,128)(2,1)}, bf16[64,128,128]...) custom-call(s32[384]{0:T(512)} %get-tuple-element.28.pick_ref, ...), custom_call_target="tpu_custom_call" | custom-call | tf_op jit(solution)/shard_map/exchange/pallas_call | solution.py:271
  165.0 0.0 copy-done.2
  165.0 0.0 copy-done.1
  165.1 0.0 copy-start
  165.1 0.8 copy-done
  165.9 11.5 %product.3 = (f32[256,64,128]{2,1,0:T(8,128)S(1)}, f32[256,128]{1,0:T(8,128)S(1)}) custom-call(s32[8,16,128]{2,1,0:T(8,128)S(1)} %copy-done, s32[64]{0:T(128)S(1)} %get-tuple-element.33.own_rows_ref, s32[64]{0:T(128)S(1)} %get-tuple-element.34.own_cols_ref, bf16[130,64,128]{2,1,0:T(8,128)(2,1)S(1)} %get-tuple-element.17.xt_ref, ...), custom_call_target="tpu_custom_call" | custom-call | flops 939524096 | bytes 14680064 | tf_op jit(solution)/shard_map/product/pallas_call | solution.py:349
  177.4 51.3 %normalize.3 = (bf16[130,64,128]{2,1,0:T(8,128)(2,1)S(1)}, f32[32,128]{1,0:T(8,128)S(1)}, f32[16,128]{1,0:T(8,128)S(1)}) custom-call(f32[4,4,16,64,128]{4,3,2,1,0:T(8,128)S(1)} %bitcast.9, f32[256,128]{1,0:T(8,128)S(1)} %get-tuple-element.21.degree_in_ref), custom_call_target="tpu_custom_call" | custom-call | tf_op jit(solution)/shard_map/normalize/pallas_call | solution.py:578
  228.7 6.9 %product.4 = f32[256,64,128]{2,1,0:T(8,128)S(1)} custom-call(s32[8,16,128]{2,1,0:T(8,128)S(1)} %copy-done, s32[64]{0:T(128)S(1)} %get-tuple-element.33.own_rows_ref, s32[64]{0:T(128)S(1)} %get-tuple-element.34.own_cols_ref, bf16[130,64,128]{2,1,0:T(8,128)(2,1)S(1)} %get-tuple-element.22.xt_ref, bf16[64,128,128]{2,1,0:T(8,128)(2,1)S(1)} %get-tuple-element.18.own_ref, ...), custom_call_target="tpu_custom_call" | custom-call | flops 939524096 | bytes 14680064 | tf_op jit(solution)/shard_map/product/pallas_call | solution.py:349
  235.6 50.6 %normalize.4 = (bf16[130,64,128]{2,1,0:T(8,128)(2,1)S(1)}, f32[32,128]{1,0:T(8,128)S(1)}) custom-call(f32[4,4,16,64,128]{4,3,2,1,0:T(8,128)S(1)} %bitcast.8, f32[16,128]{1,0:T(8,128)S(1)} %get-tuple-element.23.degree_in_ref, f32[32,128]{1,0:T(8,128)S(1)} %get-tuple-element.24.rest_0_), custom_call_target="tpu_custom_call" | custom-call | tf_op jit(solution)/shard_map/normalize/pallas_call | solution.py:578
  286.2 7.1 %product.5 = f32[256,64,128]{2,1,0:T(8,128)S(1)} custom-call(s32[8,16,128]{2,1,0:T(8,128)S(1)} %copy-done, s32[64]{0:T(128)S(1)} %get-tuple-element.33.own_rows_ref, s32[64]{0:T(128)S(1)} %get-tuple-element.34.own_cols_ref, bf16[130,64,128]{2,1,0:T(8,128)(2,1)S(1)} %get-tuple-element.25.xt_ref, bf16[64,128,128]{2,1,0:T(8,128)(2,1)S(1)} %get-tuple-element.18.own_ref, ...), custom_call_target="tpu_custom_call" | custom-call | flops 939524096 | bytes 14680064 | tf_op jit(solution)/shard_map/product/pallas_call | solution.py:349
  293.3 53.2 %normalize.5 = f32[64,2048]{1,0:T(8,128)S(1)} custom-call(f32[4,4,16,64,128]{4,3,2,1,0:T(8,128)S(1)} %bitcast.7, f32[16,128]{1,0:T(8,128)S(1)} %get-tuple-element.23.degree_in_ref, f32[32,128]{1,0:T(8,128)S(1)} %get-tuple-element.26.rest_0_), custom_call_target="tpu_custom_call" | custom-call | tf_op jit(solution)/shard_map/normalize/pallas_call | solution.py:578
  346.5 0.8 copy.45
  (4 shorter events, 0.0 us)
Async XLA Ops:
  0.0 165.0 %copy-start.2 = (s32[64]{0:T(128)S(1)}, s32[64]{0:T(128)}, u32[]{:S(2)}) copy-start(s32[64]{0:T(128)} %param.10) | copy-start | bytes 772
  0.0 165.0 %copy-start.1 = (s32[64]{0:T(128)S(1)}, s32[64]{0:T(128)}, u32[]{:S(2)}) copy-start(s32[64]{0:T(128)} %param.9) | copy-start | bytes 772
  165.1 0.8 copy-start

commit v9 on v8

--- a/solution.py
+++ b/solution.py
@@ -271,7 +271,7 @@
     recv, _, _, own, places, xt = pl.pallas_call(
         exchange_kernel,
         out_shape=(jax.ShapeDtypeStruct(slots, BF), halves, halves, pltpu.VMEM((OWN, TILE, TILE), BF),
-                   jax.ShapeDtypeStruct((NR, NC, TILE), jnp.int32), pltpu.VMEM((X_BLOCKS, K, TILE), BF)),
+                   pltpu.VMEM((NR, NC, TILE), jnp.int32), pltpu.VMEM((X_BLOCKS, K, TILE), BF)),
         in_specs=[SMEM, ANY, ANY, VMEM, VMEM],
         out_specs=(ANY, ANY, ANY, VMEM, VMEM, VMEM),
         scratch_shapes=[
@@ -279,7 +279,7 @@
             pltpu.VMEM((NC, NR, TILE), jnp.int32), pltpu.VMEM((NR, NC, TILE), jnp.int32),
             pltpu.VMEM(XS_SHAPE, BF), pltpu.VMEM(chg_tiles.shape, BF), pltpu.VMEM(own.shape, BF), dma, dma,
         ] + x_sems() + [dma((NR,))] * 8 + [dma, dma, dma, dma, dma((NR,)), dma((NR,))],
-        compiler_params=pltpu.CompilerParams(collective_id=0, has_side_effects=True, vmem_limit_bytes=58 * MIB),
+        compiler_params=pltpu.CompilerParams(collective_id=0, has_side_effects=True, vmem_limit_bytes=56 * MIB),
         name="exchange",
     )(pick, chg_tiles, own, meta, xs)
     return recv, own, places, xt

time: 347 us -> 345 us (level)
  no operation moved by 1% of the time
where the time goes in v9:
time: 345 us
  Pallas kernels  341 us (99%)
    pallas_call x1, Pallas kernels, exchange(): pl.pallas_call(exchange_kernel, out_shape=(jax.ShapeDtypeStruct(slots, BF...  161 us
    pallas_call x3, Pallas kernels, normalize(): pl.pallas_call(functools.partial(normalize_kernel, first, last), out_shap...  154 us
    pallas_call x3, Pallas kernels, product(): pl.pallas_call(functools.partial(product_kernel, with_degree), out_shape=...  25.5 us

profile of v9, /device:TPU:1, one launch (start us, length us, event | category | flops | bytes accessed | tf_op | source)
XLA Modules:
  0.0 344.8 jit_solution(1356909890253150449)
XLA Ops:
  0.0 0.0 copy-start.1
  0.0 0.0 copy-start
  0.0 0.7 fusion.7
  0.8 0.2 convert_reduce_fusion
  0.9 0.7 select_reduce_fusion
  1.7 0.2 sub.45
  1.9 0.2 gt.12
  2.1 0.1 fusion.1
  2.2 0.1 add_bitcast_fusion
  2.3 0.6 pad.4.meta_ref
  2.9 161.4 %exchange.1 = (bf16[8,16,384,128]{3,2,1,0:T(8,128)(2,1)}, bf16[8,16,192,128]{3,2,1,0:T(8,128)(2,1)}, bf16[8,16,192,128]{3,2,1,0:T(8,128)(2,1)}, bf16[64,128,128]...) custom-call(s32[384]{0:T(512)} %get-tuple-element.28.pick_ref, ...), custom_call_target="tpu_custom_call" | custom-call | tf_op jit(solution)/shard_map/exchange/pallas_call | solution.py:271
  164.4 0.0 copy-done.1
  164.4 0.0 copy-done
  164.4 11.4 %product.3 = (f32[256,64,128]{2,1,0:T(8,128)S(1)}, f32[256,128]{1,0:T(8,128)S(1)}) custom-call(s32[8,16,128]{2,1,0:T(8,128)S(1)} %get-tuple-element.16.places_ref, s32[64]{0:T(128)S(1)} %get-tuple-element.33.own_rows_ref, s32[64]{0:T(128)S(1)} %get-tuple-element.34.own_cols_ref, bf16[130,64,128]{2,1,0:T(8,128)(2,1)S(1)} %get-tuple-element.17.xt_ref, ...), custom_call_target="tpu_custom_call" | custom-call | flops 939524096 | bytes 14680064 | tf_op jit(solution)/shard_map/product/pallas_call | solution.py:349
  175.9 51.3 %normalize.3 = (bf16[130,64,128]{2,1,0:T(8,128)(2,1)S(1)}, f32[32,128]{1,0:T(8,128)S(1)}, f32[16,128]{1,0:T(8,128)S(1)}) custom-call(f32[4,4,16,64,128]{4,3,2,1,0:T(8,128)S(1)} %bitcast.9, f32[256,128]{1,0:T(8,128)S(1)} %get-tuple-element.21.degree_in_ref), custom_call_target="tpu_custom_call" | custom-call | tf_op jit(solution)/shard_map/normalize/pallas_call | solution.py:578
  227.2 6.9 %product.4 = f32[256,64,128]{2,1,0:T(8,128)S(1)} custom-call(s32[8,16,128]{2,1,0:T(8,128)S(1)} %get-tuple-element.16.places_ref, s32[64]{0:T(128)S(1)} %get-tuple-element.33.own_rows_ref, s32[64]{0:T(128)S(1)} %get-tuple-element.34.own_cols_ref, bf16[130,64,128]{2,1,0:T(8,128)(2,1)S(1)} %get-tuple-element.22.xt_ref, ...), custom_call_target="tpu_custom_call" | custom-call | flops 939524096 | bytes 14680064 | tf_op jit(solution)/shard_map/product/pallas_call | solution.py:349
  234.1 50.5 %normalize.4 = (bf16[130,64,128]{2,1,0:T(8,128)(2,1)S(1)}, f32[32,128]{1,0:T(8,128)S(1)}) custom-call(f32[4,4,16,64,128]{4,3,2,1,0:T(8,128)S(1)} %bitcast.8, f32[16,128]{1,0:T(8,128)S(1)} %get-tuple-element.23.degree_in_ref, f32[32,128]{1,0:T(8,128)S(1)} %get-tuple-element.24.rest_0_), custom_call_target="tpu_custom_call" | custom-call | tf_op jit(solution)/shard_map/normalize/pallas_call | solution.py:578
  284.5 7.1 %product.5 = f32[256,64,128]{2,1,0:T(8,128)S(1)} custom-call(s32[8,16,128]{2,1,0:T(8,128)S(1)} %get-tuple-element.16.places_ref, s32[64]{0:T(128)S(1)} %get-tuple-element.33.own_rows_ref, s32[64]{0:T(128)S(1)} %get-tuple-element.34.own_cols_ref, bf16[130,64,128]{2,1,0:T(8,128)(2,1)S(1)} %get-tuple-element.25.xt_ref, ...), custom_call_target="tpu_custom_call" | custom-call | flops 939524096 | bytes 14680064 | tf_op jit(solution)/shard_map/product/pallas_call | solution.py:349
  291.7 52.4 %normalize.5 = f32[64,2048]{1,0:T(8,128)S(1)} custom-call(f32[4,4,16,64,128]{4,3,2,1,0:T(8,128)S(1)} %bitcast.7, f32[16,128]{1,0:T(8,128)S(1)} %get-tuple-element.23.degree_in_ref, f32[32,128]{1,0:T(8,128)S(1)} %get-tuple-element.26.rest_0_), custom_call_target="tpu_custom_call" | custom-call | tf_op jit(solution)/shard_map/normalize/pallas_call | solution.py:578
  344.0 0.8 copy.45
  (4 shorter events, 0.0 us)
Async XLA Ops:
  0.0 164.4 %copy-start.1 = (s32[64]{0:T(128)S(1)}, s32[64]{0:T(128)}, u32[]{:S(2)}) copy-start(s32[64]{0:T(128)} %param.10) | copy-start | bytes 772
  0.0 164.4 %copy-start = (s32[64]{0:T(128)S(1)}, s32[64]{0:T(128)}, u32[]{:S(2)}) copy-start(s32[64]{0:T(128)} %param.9) | copy-start | bytes 772
